TPU v7x, 768 devices: a whole 4x8x12 slice. The times are simulated.
768 devices in a mesh: img: 48 (over y_lo, z, core), txt: 16 (over x, y_hi).
Axes of the slice: x: 4, y: 8 (y_hi: 4, y_lo: 2; y = y_hi * 2 + y_lo), z: 12, core: 2. Of those that a mesh axis runs over, the one named last changes fastest.
Arguments:
- image_emb: float32 [6144, 1536], P('img', 'txt'), may hold values from -0.15625 to 0.15625
- text_emb: float32 [6144, 1536], P('txt', 'img'), may hold values from -0.15625 to 0.15625
- vision_feat: bfloat16 [6144, 5120], P('img', 'txt'), may hold values from -0.125 to 0.125
- positive: int32 [6144], P('img'), may hold values from 0 to 6143, each once
- logit_scale: float32 [1], replicated, may hold values from 5 to 15
- logit_bias: float32 [1], replicated, may hold values from -3 to -1
Outputs:
- grad_image: float32 [6144, 1536], P('img', 'txt')
- grad_text: float32 [6144, 1536], P('txt', 'img')
- grad_proj: float32 [5120, 1536], P('txt', 'img')
Inputs may be any that keep to these rules, and one draw needn't show every extreme that they name: `positive`: each text index is the match of exactly one image.
All inputs are finite; a program needn't handle non-finite values.
Results may differ from a plain program's by a relative error of at most 0.0029.
Values may be sent and summed in bfloat16 or wider, within the bound.
No kernel may reach another device: no remote copies, remote signals or barrier semaphores. Data moves between devices by JAX's collectives and lax.ppermute only.
A program may use at most 32 MiB of HBM per device.

v0:
```python
import jax
import jax.numpy as jnp
from jax import lax
from jax.sharding import Mesh
from jax.sharding import PartitionSpec as P

IMG = ("img_0", "img_1", "img_2")


def in_order(tiles, dim):
    lengths = list(tiles.shape[1:])
    lengths[dim] *= tiles.shape[0]
    return jnp.moveaxis(tiles, 0, dim).reshape(lengths)


def sent_to_all(array, axis):
    length = lax.axis_size(axis)
    return lax.all_to_all(
        jnp.broadcast_to(array[None], (length, *array.shape)), axis, 0, 0, tiled=True
    )


def collect(array, axis, dim):
    return in_order(sent_to_all(array, axis), dim)


def all_blocks(array, axes, turns):
    tiles = array[None]
    for k in turns:
        tiles = lax.all_gather(tiles, axes[k], axis=0, tiled=True)
    block = [lax.axis_size(axes[k]) for k in reversed(turns)]
    tiles = tiles.reshape(*block, *array.shape)
    turned = sorted(range(len(turns)), key=lambda place: turns[len(turns) - 1 - place])
    return tiles.transpose(*turned, *range(len(turns), tiles.ndim)).reshape(-1, *array.shape)


def gathered_by_axis(array, axes, turns, dim):
    return in_order(all_blocks(array, axes, turns), dim)


def cut_along(array, dim, length):
    lengths = array.shape
    tiles = array.reshape(*lengths[:dim], length, lengths[dim] // length, *lengths[dim + 1 :])
    return jnp.moveaxis(tiles, dim, 0)


def sum_at_owner(array, axis, dim):
    tiles = cut_along(array, dim, lax.axis_size(axis))
    arrived = lax.all_to_all(tiles, axis, split_axis=0, concat_axis=0, tiled=True)
    return arrived.sum(axis=0)


def per_device(image_emb, text_emb, vision_feat, positive, logit_scale, logit_bias):
    scale = logit_scale[0]
    bias = logit_bias[0]
    image_full = collect(image_emb, "txt", 1)
    text_full = gathered_by_axis(text_emb, IMG, (0, 1, 2), 1)
    text_rows = text_full.shape[0]
    first_col = lax.axis_index("txt") * text_rows
    columns = first_col + lax.iota(jnp.int32, text_rows)
    logits = (
        scale
        * jnp.dot(
            image_full,
            text_full.T,
            precision=lax.Precision.HIGHEST,
            preferred_element_type=jnp.float32,
        )
        + bias
    )
    sign = jnp.where(positive[:, None] == columns[None, :], 1.0, -1.0).astype(jnp.float32)
    slope = -sign * jax.nn.sigmoid(-sign * logits)
    image_terms = scale * jnp.dot(
        slope, text_full, precision=lax.Precision.HIGHEST, preferred_element_type=jnp.float32
    )
    text_terms = scale * jnp.dot(
        slope.T, image_full, precision=lax.Precision.HIGHEST, preferred_element_type=jnp.float32
    )
    grad_text = sum_at_owner(text_terms, IMG, 1)
    grad_image = sum_at_owner(image_terms, "txt", 1)
    image_low = collect(grad_image.astype(jnp.bfloat16), "txt", 1)
    weight_terms = jnp.dot(vision_feat.T, image_low, preferred_element_type=jnp.float32)
    grad_proj = sum_at_owner(weight_terms, IMG, 1)
    return (grad_image, grad_text, grad_proj)


def solution(mesh):
    torus = Mesh(
        mesh.devices.reshape(2, 12, 2, mesh.shape["txt"]), ("img_0", "img_1", "img_2", "txt")
    )
    in_specs = (P(IMG, "txt"), P("txt", IMG), P(IMG, "txt"), P(IMG), P(), P())
    out_specs = (P(IMG, "txt"), P("txt", IMG), P("txt", IMG))
    return jax.shard_map(
        per_device, mesh=torus, in_specs=in_specs, out_specs=out_specs, check_vma=False
    )
```

profile of v0, /device:TPU:1, one launch (start us, length us, event | category | flops | bytes accessed | tf_op | source)
XLA Modules:
  0.0 352.9 jit_solution(6374234505501531076)
XLA Ops:
  7.2 0.0 copy-start
  7.2 0.0 all-gather.4.cloned.1.call-start
  7.2 4.5 %all-gather = f32[768,32]{0,1:T(8,128)S(1)} all-gather(f32[384,32]{0,1:T(8,128)} %param.7), channel_id=2, replica_groups=mesh['img_0'=2,'img_1'=12,'img_2'=2,'txt'=16] {'img_0'}, dimensions={0}, use_global_device_ids=true | all-gather | bytes 147456 | tf_op jit(solution)/shard_map/all_gather | solution.py:30
  11.8 0.6 copy.35
  12.4 0.0 all-gather.4.cloned.1.call-update
  12.4 0.0 all-gather.6.cloned.1.call-start
  12.5 59.6 %all-gather.4.cloned.1.call-done = f32[24,384,32]{1,2,0:T(8,128)} async-done(((f32[2,384,32]{1,2,0:T(8,128)}), f32[24,384,32]{1,2,0:T(8,128)}) %all-gather.4.cloned.1.call-update) | async-done | bytes 1179664 | tf_op jit(solution)/shard_map/all_gather | solution.py:30
  72.1 0.0 all-gather.6.cloned.1.call-update
  72.1 1.8 broadcast_in_dim.27
  73.9 9.0 %all-to-all-start = ((f32[16,128,96]{1,2,0:T(8,128)}), f32[16,128,96]{1,2,0:T(8,128)S(1)}, u32[]{:S(2)}, u32[]{:S(2)}) async-start(f32[16,128,96]{1,2,0:T(8,128)} %broadcast_in_dim.27), calls=%async_computation | async-start | bytes 1572864 | tf_op jit(solution)/shard_map/all_to_all | solution.py:18
  84.2 19.6 %all-gather.6.cloned.1.call-done = f32[48,384,32]{1,2,0:T(8,128)} async-done(((f32[24,384,32]{1,2,0:T(8,128)}), f32[48,384,32]{1,2,0:T(8,128)}) %all-gather.6.cloned.1.call-update) | async-done | bytes 2359312 | tf_op jit(solution)/shard_map/all_gather | solution.py:30
  103.8 1.9 copy.29
  105.7 0.0 all-to-all-done
  105.7 0.0 copy-done.2
  105.7 1.8 fusion.6
  107.5 3.4 convolution_multiply_fusion.1
  111.0 1.4 copy.30
  112.4 30.5 %all_to_all.25 = f32[16,128,96]{1,2,0:T(8,128)S(1)} all-to-all(f32[16,128,96]{1,2,0:T(8,128)S(1)} %bitcast.49), channel_id=1, replica_groups=mesh['img_0'=2,'img_1'=12,'img_2'=2,'txt'=16] {'txt'}, dimensions={0} | all-to-all | bytes 1572864 | tf_op jit(solution)/shard_map/all_to_all | solution.py:49
  142.9 0.0 copy-start.1
  142.9 0.8 broadcast_in_dim.29
  143.7 4.4 %all-to-all-start.3 = ((bf16[16,128,96]{1,2,0:T(8,128)(2,1)}), bf16[16,128,96]{1,2,0:T(8,128)(2,1)}, u32[]{:S(2)}, u32[]{:S(2)}) async-start(bf16[16,128,96]{1,2,0:T(8,128)(2,1)} %broadcast_in_dim.29), calls=%async_computation.3 | async-start | bytes 786432 | tf_op jit(solution)/shard_map/all_to_all | solution.py:18
  148.2 2.1 convolution_multiply_fusion
  150.2 2.0 copy.31
  152.2 9.6 %all-to-all-done.3 = bf16[16,128,96]{1,2,0:T(8,128)(2,1)} async-done(((bf16[16,128,96]{1,2,0:T(8,128)(2,1)}), bf16[16,128,96]{1,2,0:T(8,128)(2,1)}, u32[]{:S(2)}, u32[]{:S(2)}) %all-to-all-start.3) | async-done | bytes 393248 | tf_op jit(solution)/shard_map/all_to_all | solution.py:18
  161.8 13.2 %all-to-all-start.2 = ((f32[48,384,32]{1,2,0:T(8,128)}), f32[48,384,32]{1,2,0:T(8,128)S(1)}, u32[]{:S(2)}, u32[]{:S(2)}) async-start(f32[48,384,32]{1,2,0:T(8,128)} %bitcast.45), calls=%async_computation.2 | async-start | bytes 4718592 | tf_op jit(solution)/shard_map/all_to_all | solution.py:49
  175.0 2.7 convolution_bitcast_fusion
  177.7 3.0 copy.32
  180.7 74.5 %all-to-all-done.2 = f32[48,384,32]{1,2,0:T(8,128)S(1)} async-done(((f32[48,384,32]{1,2,0:T(8,128)}), f32[48,384,32]{1,2,0:T(8,128)S(1)}, u32[]{:S(2)}, u32[]{:S(2)}) %all-to-all-start.2) | async-done | bytes 2359328 | tf_op jit(solution)/shard_map/all_to_all | solution.py:49
  255.2 8.1 %all-to-all-start.4 = ((f32[48,320,32]{1,2,0:T(8,128)}), f32[48,320,32]{1,2,0:T(8,128)}, u32[]{:S(2)}, u32[]{:S(2)}) async-start(f32[48,320,32]{1,2,0:T(8,128)} %bitcast.46), calls=%async_computation.4 | async-start | bytes 4718592 | tf_op jit(solution)/shard_map/all_to_all | solution.py:49
  263.3 0.8 reduce_sum.28
  264.1 79.5 %all-to-all-done.4 = f32[48,320,32]{1,2,0:T(8,128)} async-done(((f32[48,320,32]{1,2,0:T(8,128)}), f32[48,320,32]{1,2,0:T(8,128)}, u32[]{:S(2)}, u32[]{:S(2)}) %all-to-all-start.4) | async-done | bytes 1966112 | tf_op jit(solution)/shard_map/all_to_all | solution.py:49
  343.6 2.4 reduce_sum.29
  (6 shorter events, 0.1 us)
Async XLA Ops:
  7.2 167.8 %copy-start = (bf16[128,320]{0,1:T(8,128)(2,1)S(1)}, bf16[128,320]{0,1:T(8,128)(2,1)}, u32[]{:S(2)}) copy-start(bf16[128,320]{0,1:T(8,128)(2,1)} %param.8) | copy-start | bytes 245764
  7.2 64.9 %all-gather.4.cloned.1.call-start = ((), (), s32[]{:S(2)}) async-start(), calls=%async_computation.5 | async-start | bytes 1277952 | tf_op jit(solution)/shard_map/all_gather | solution.py:30
  12.4 91.4 %all-gather.6.cloned.1.call-start = ((), (), s32[]{:S(2)}) async-start(), calls=%async_computation.6 | async-start | bytes 3538944 | tf_op jit(solution)/shard_map/all_gather | solution.py:30
  73.9 31.8 %all-to-all-start = ((f32[16,128,96]{1,2,0:T(8,128)}), f32[16,128,96]{1,2,0:T(8,128)S(1)}, u32[]{:S(2)}, u32[]{:S(2)}) async-start(f32[16,128,96]{1,2,0:T(8,128)} %broadcast_in_dim.27), calls=%async_computation | async-start | bytes 1572864 | tf_op jit(solution)/shard_map/all_to_all | solution.py:18
  103.8 1.9 copy-start.2
  142.9 9.3 %copy-start.1 = (f32[128,96]{0,1:T(8,128)}, f32[128,96]{0,1:T(8,128)S(1)}, u32[]{:S(2)}) copy-start(f32[128,96]{0,1:T(8,128)S(1)} %reduce_sum.27) | copy-start | bytes 147460
  143.7 18.0 %all-to-all-start.3 = ((bf16[16,128,96]{1,2,0:T(8,128)(2,1)}), bf16[16,128,96]{1,2,0:T(8,128)(2,1)}, u32[]{:S(2)}, u32[]{:S(2)}) async-start(bf16[16,128,96]{1,2,0:T(8,128)(2,1)} %broadcast_in_dim.29), calls=%async_computation.3 | async-start | bytes 786432 | tf_op jit(solution)/shard_map/all_to_all | solution.py:18
  161.8 93.5 %all-to-all-start.2 = ((f32[48,384,32]{1,2,0:T(8,128)}), f32[48,384,32]{1,2,0:T(8,128)S(1)}, u32[]{:S(2)}, u32[]{:S(2)}) async-start(f32[48,384,32]{1,2,0:T(8,128)} %bitcast.45), calls=%async_computation.2 | async-start | bytes 4718592 | tf_op jit(solution)/shard_map/all_to_all | solution.py:49
  255.2 88.4 %all-to-all-start.4 = ((f32[48,320,32]{1,2,0:T(8,128)}), f32[48,320,32]{1,2,0:T(8,128)}, u32[]{:S(2)}, u32[]{:S(2)}) async-start(f32[48,320,32]{1,2,0:T(8,128)} %bitcast.46), calls=%async_computation.4 | async-start | bytes 4718592 | tf_op jit(solution)/shard_map/all_to_all | solution.py:49
Sparse Core Ops, SparseCore 0:
  12.5 59.4 all-gather.3
  74.4 29.3 all-gather.5
where the time goes:
time: 354 us; the launch traced here: 353 us
  waiting for transfers between devices  243 us (69%)
  blocking collectives  35 us (10%)
  starting transfers between devices  34.8 us (10%)
  between operations  15.5 us (4%)
  local copies, waits for them, and re-layouts  11.5 us (3%)
  matrix products  10.1 us (3%)
    all_to_all x2, waiting for transfers between devices, sum_at_owner(): lax.all_to_all(tiles, axis, split_axis=0, concat_axis=0, tiled=True)  154 us
    all_gather x2, waiting for transfers between devices, all_blocks(): tiles = lax.all_gather(tiles, axes[k], axis=0, tiled=True)  79.2 us
    all_to_all x1, blocking collectives, sum_at_owner(): lax.all_to_all(tiles, axis, split_axis=0, concat_axis=0, tiled=True)  30.5 us
    all_to_all x2, starting transfers between devices, sum_at_owner(): lax.all_to_all(tiles, axis, split_axis=0, concat_axis=0, tiled=True)  21.3 us
    all_to_all x2, starting transfers between devices, sent_to_all(): lax.all_to_all(jnp.broadcast_to(array[None], (length, *array.shape)), axi...  13.4 us
    all_to_all x2, waiting for transfers between devices, sent_to_all(): lax.all_to_all(jnp.broadcast_to(array[None], (length, *array.shape)), axi...  9.57 us
  transfers between devices with their start and end apart: 6, of which 5 were waited for; matrix products, arithmetic and copies ran while one was open for 4% of the time, Pallas kernels for 0%

commit v1 on v0

v1 whole, which is shorter than its diff:
```python
import jax
import jax.numpy as jnp
from jax import lax
from jax.sharding import Mesh
from jax.sharding import PartitionSpec as P


IMG = ("yl", "z", "core")
TXT = ("x", "yh")
CHIPS = ("yl", "z")
HALF = jnp.float16
F32 = jnp.float32
HIGH = lax.Precision.HIGH

EMB_UP = 2.0**18
IMAGE_UP = 2.0**10
TEXT_UP = (2.0**11, 2.0**10, 2.0**9, 2.0**8, 2.0**7)
PROJ_UP = (2.0**-2, 2.0**-3)


def exchange(tiles, axis):
    return lax.all_to_all(tiles, axis, split_axis=0, concat_axis=0, tiled=True)


def to_all(array, axis):
    return exchange(jnp.broadcast_to(array[None], (lax.axis_size(axis), *array.shape)), axis)


def swap(array):
    return lax.ppermute(array, "core", ((0, 1), (1, 0)))


def shifted(array, axis, step):
    length = lax.axis_size(axis)
    return lax.ppermute(array, axis, tuple((i, (i + step) % length) for i in range(length)))


def in_order(came, place):
    length = len(came)
    return jnp.stack(
        [
            lax.select_n(place, *(came[(here - member) % length] for here in range(length)))
            for member in range(length)
        ]
    )


def per_device(image_emb, text_emb, vision_feat, positive, logit_scale, logit_bias):
    scale = logit_scale[0]
    bias = logit_bias[0]
    core = lax.axis_index("core")
    yl, z = lax.axis_index("yl"), lax.axis_index("z")

    def dot(a, b, ca, cb):
        return lax.dot_general(
            a, b, (((ca,), (cb,)), ((), ())), precision=HIGH, preferred_element_type=F32
        )

    def of_core(blocks, which):
        blocks = blocks.reshape(24, 2, 32, blocks.shape[-1])
        return lax.dynamic_index_in_dim(blocks, which, 1, keepdims=False).reshape(768, -1)

    text_tile = (text_emb.T * EMB_UP).astype(HALF)
    image_tile = (image_emb.T * EMB_UP).astype(HALF)
    own = to_all(text_tile, CHIPS)
    other = swap(own).reshape(768, -1).astype(F32)
    own = own.reshape(768, -1).astype(F32)
    near = jnp.stack([image_tile] + [shifted(image_tile, "yh", k) for k in (1, 2, 3)])
    far = [near] + [shifted(near, "x", k) for k in (1, 2, 3)]
    by_x = in_order(far, lax.axis_index("x"))
    image_full = in_order([by_x[:, k] for k in range(4)], lax.axis_index("yh"))
    image_full = jnp.moveaxis(image_full, 0, 1).astype(F32)
    image_own = of_core(image_full, core)
    image_other = of_core(image_full, 1 - core)

    text_rows = own.shape[1]
    first_col = lax.axis_index(TXT) * text_rows
    columns = first_col + lax.iota(jnp.int32, text_rows)
    products = dot(image_own, own, 0, 0) + dot(image_other, other, 0, 0)
    logits = (scale * (1.0 / EMB_UP**2)) * products + bias
    sign = jnp.where(positive[:, None] == columns[None, :], 1.0, -1.0).astype(F32)
    slope = -sign * jax.nn.sigmoid(-sign * logits)
    up = IMAGE_UP / EMB_UP
    first = (dot(own, slope, 1, 1) * up).astype(HALF).reshape(24, 32, -1)
    second = (dot(other, slope, 1, 1) * up).astype(HALF).reshape(24, 32, -1)
    sent = jnp.stack(
        (jnp.where(core == 0, first, second), jnp.where(core == 0, second, first)), axis=1
    )
    got = exchange(sent.reshape(16, 96, -1), TXT)
    grad_image = got.astype(F32).sum(axis=0) * (scale * (1.0 / IMAGE_UP))
    image_low = to_all(grad_image.astype(jnp.bfloat16), TXT)

    theirs = dot(image_other, slope, 1, 0)
    got = swap((theirs * (TEXT_UP[0] / EMB_UP)).astype(HALF))
    mine = dot(image_own, slope, 1, 0)
    tiles = mine * (1.0 / EMB_UP) + got.astype(F32) * (1.0 / TEXT_UP[0])
    tiles = tiles.reshape(2, 3, 2, 2, 32, text_rows)
    stages = (
        ("yl", yl, 0, ((0, 1), (1, 0))),
        ("z", z % 2, 2, tuple((i, i ^ 1) for i in range(12))),
        ("z", (z // 2) % 2, 1, tuple((i, i ^ 2) for i in range(12))),
    )
    for k, (axis, place, dim, pairs) in enumerate(stages, 1):
        theirs = lax.dynamic_index_in_dim(tiles, 1 - place, dim, keepdims=False)
        got = lax.ppermute((theirs * TEXT_UP[k]).astype(HALF), axis, pairs)
        mine = lax.dynamic_index_in_dim(tiles, place, dim, keepdims=False)
        tiles = mine + got.astype(F32) * (1.0 / TEXT_UP[k])
    block = z // 4
    total = lax.dynamic_index_in_dim(tiles, block, 0, keepdims=False)
    for step in (1, 2):
        theirs = lax.dynamic_index_in_dim(tiles, (block + step) % 3, 0, keepdims=False)
        got = shifted((theirs * TEXT_UP[4]).astype(HALF), "z", 4 * step)
        total = total + got.astype(F32) * (1.0 / TEXT_UP[4])
    grad_text = total * scale

    def weights(which):
        low = of_core(image_low, which)
        return lax.dot_general(low, vision_feat, (((1,), (0,)), ((), ())), preferred_element_type=F32)

    got = swap((weights(1 - core) * PROJ_UP[0]).astype(HALF))
    mine = weights(core)
    sent = ((mine + got.astype(F32) * (1.0 / PROJ_UP[0])) * PROJ_UP[1]).astype(HALF)
    got = exchange(sent.reshape(24, 32, -1), CHIPS)
    grad_proj = got.astype(F32).sum(axis=0) * (1.0 / PROJ_UP[1])
    return (grad_image.T, grad_text.T, grad_proj.T)


def solution(mesh):
    torus = Mesh(mesh.devices.reshape(2, 12, 2, 4, 4), (*IMG, *TXT))
    in_specs = (P(IMG, TXT), P(TXT, IMG), P(IMG, TXT), P(IMG), P(), P())
    out_specs = (P(IMG, TXT), P(TXT, IMG), P(TXT, IMG))
    return jax.shard_map(
        per_device, mesh=torus, in_specs=in_specs, out_specs=out_specs, check_vma=False
    )
```

time: 354 us -> 170 us (0.48)
  waiting for transfers between devices: 243 us -> 60 us
  starting transfers between devices: 34.8 us -> 92.9 us
  blocking collectives: 35 us -> 0 us
  between operations: 15.5 us -> 2.52 us
  local copies, waits for them, and re-layouts: 11.5 us -> 3.17 us
  matrix products: 10.1 us -> 4.45 us
    all_to_all x4, waiting for transfers between devices: 164 us -> 23.7 us  [exchange(): return lax.all_to_all(tiles, axis, split_axis=0, concat_axis=0, tiled=True)]
    all_gather x2 -> x0, waiting for transfers between devices: 79.2 us -> none  [all_blocks(): tiles = lax.all_gather(tiles, axes[k], axis=0, tiled=True)]
    ppermute x0 -> x14, starting transfers between devices: none -> 57 us  [the longest x8 33.2 us: shifted(): lax.ppermute(array, axis, tuple(((i, (i + step) % length) for i in range(...]
    ppermute x0 -> x14, waiting for transfers between devices: none -> 36.3 us  [the longest x3 23.5 us: per_device(): got = lax.ppermute((theirs * TEXT_UP[k]).astype(HALF), axis, pairs)]
    all_to_all x1 -> x0, blocking collectives: 30.5 us -> none  [sum_at_owner(): lax.all_to_all(tiles, axis, split_axis=0, concat_axis=0, tiled=True)]
    dot_general x4 -> x8, matrix products: 10.1 us -> 4.45 us  [the longest x6 3.87 us: dot(): lax.dot_general(a, b, (((ca,), (cb,)), ((), ())), precision=HIGH, preferr...]
    all_gather x1 -> x0, blocking collectives: 4.52 us -> none  [all_blocks(): tiles = lax.all_gather(tiles, axes[k], axis=0, tiled=True)]
  transfers between devices with their start and end apart: 6 -> 18, of which waited for: 5 -> 10; matrix products, arithmetic and copies ran while one was open for 4% -> 3% of each run, Pallas kernels for 0% -> 0%
where the time goes in v1:
time: 170 us; the launch traced here: 168 us
  starting transfers between devices  92.9 us (55%)
  waiting for transfers between devices  60 us (35%)
  other arithmetic  4.77 us (3%)
  matrix products  4.45 us (3%)
  local copies, waits for them, and re-layouts  3.17 us (2%)
  between operations  2.52 us (1%)
    all_to_all x4, starting transfers between devices, exchange(): return lax.all_to_all(tiles, axis, split_axis=0, concat_axis=0, tiled=True)  35.8 us
    ppermute x8, starting transfers between devices, shifted(): lax.ppermute(array, axis, tuple(((i, (i + step) % length) for i in range(...  33.2 us
    all_to_all x4, waiting for transfers between devices, exchange(): return lax.all_to_all(tiles, axis, split_axis=0, concat_axis=0, tiled=True)  23.7 us
    ppermute x3, waiting for transfers between devices, per_device(): got = lax.ppermute((theirs * TEXT_UP[k]).astype(HALF), axis, pairs)  23.5 us
    ppermute x3, starting transfers between devices, swap(): return lax.ppermute(array, 'core', ((0, 1), (1, 0)))  13.3 us
    ppermute x8, waiting for transfers between devices, shifted(): lax.ppermute(array, axis, tuple(((i, (i + step) % length) for i in range(...  12.2 us
    ppermute x3, starting transfers between devices, per_device(): got = lax.ppermute((theirs * TEXT_UP[k]).astype(HALF), axis, pairs)  10.5 us
    dot_general x6, matrix products, dot(): lax.dot_general(a, b, (((ca,), (cb,)), ((), ())), precision=HIGH, preferr...  3.87 us
  transfers between devices with their start and end apart: 18, of which 10 were waited for; matrix products, arithmetic and copies ran while one was open for 3% of the time, Pallas kernels for 0%

profile of v1, /device:TPU:1, one launch (start us, length us, event | category | flops | bytes accessed | tf_op | source)
XLA Modules:
  0.0 167.8 jit_solution(15831080724259046427)
XLA Ops:
  0.7 0.9 fusion.19
  1.5 0.9 broadcast_in_dim.12
  2.4 16.9 %all-to-all-start = ((f16[24,32,384]{2,1,0:T(8,128)(2,1)}), f16[24,32,384]{2,1,0:T(8,128)(2,1)S(1)}, u32[]{:S(2)}, u32[]{:S(2)}) async-start(f16[24,32,384]{2,1,0:T(8,128)(2,1)} %broadcast_in_dim.12), calls=%async_computation | async-start | bytes 1179648 | tf_op jit(solution)/shard_map/all_to_all | solution.py:22
  19.4 5.0 %collective-permute-start.2 = (f16[96,128]{1,0:T(8,128)(2,1)S(1)}, f16[96,128]{1,0:T(8,128)(2,1)S(1)}, u32[]{:S(2)}, u32[]{:S(2)}) collective-permute-start(f16[96,128]{1,0:T(8,128)(2,1)S(1)} %get-tuple-element.23), channel_id=1, source_target_pairs={{0,3},{1,0},{2,1},{3,2},{4,7},{5,4},{6,5},{7,6},{8,11},{9,8},{10,9... | collective-permute-start | bytes 73736 | tf_op jit(solution)/shard_map/ppermute | solution.py:35
  24.4 4.4 %collective-permute-start.1 = (f16[96,128]{1,0:T(8,128)(2,1)S(1)}, f16[96,128]{1,0:T(8,128)(2,1)S(1)}, u32[]{:S(2)}, u32[]{:S(2)}) collective-permute-start(f16[96,128]{1,0:T(8,128)(2,1)S(1)} %get-tuple-element.23), channel_id=1, source_target_pairs={{0,2},{1,3},{2,0},{3,1},{4,6},{5,7},{6,4},{7,5},{8,10},{9,11},{10,... | collective-permute-start | bytes 73736 | tf_op jit(solution)/shard_map/ppermute | solution.py:35
  28.8 3.3 %collective-permute-start = (f16[96,128]{1,0:T(8,128)(2,1)S(1)}, f16[96,128]{1,0:T(8,128)(2,1)S(1)}, u32[]{:S(2)}, u32[]{:S(2)}) collective-permute-start(f16[96,128]{1,0:T(8,128)(2,1)S(1)} %get-tuple-element.23), channel_id=1, source_target_pairs={{0,1},{1,2},{2,3},{3,0},{4,5},{5,6},{6,7},{7,4},{8,9},{9,10},{10,1... | collective-permute-start | bytes 73736 | tf_op jit(solution)/shard_map/ppermute | solution.py:35
  33.9 2.1 %collective-permute-done = f16[96,128]{1,0:T(8,128)(2,1)S(1)} collective-permute-done((f16[96,128]{1,0:T(8,128)(2,1)S(1)}, f16[96,128]{1,0:T(8,128)(2,1)S(1)}, u32[]{:S(2)}, u32[]{:S(2)}) %collective-permute-start) | collective-permute-done | bytes 24608 | tf_op jit(solution)/shard_map/ppermute | solution.py:35
  36.0 4.7 %collective-permute-start.4 = (f16[4,96,128]{2,1,0:T(8,128)(2,1)S(1)}, f16[4,96,128]{2,1,0:T(8,128)(2,1)S(1)}, u32[]{:S(2)}, u32[]{:S(2)}) collective-permute-start(f16[4,96,128]{2,1,0:T(8,128)(2,1)S(1)} %pad_maximum_fusion.3), channel_id=1, source_target_pairs={{0,8},{4,12},{8,0},{12,4},{1,9},{5,13},{9,1},{13,5},{2,10},{6,14},... | collective-permute-start | bytes 294920 | tf_op jit(solution)/shard_map/ppermute | solution.py:35
  40.6 2.8 %collective-permute-start.5 = (f16[4,96,128]{2,1,0:T(8,128)(2,1)S(1)}, f16[4,96,128]{2,1,0:T(8,128)(2,1)S(1)}, u32[]{:S(2)}, u32[]{:S(2)}) collective-permute-start(f16[4,96,128]{2,1,0:T(8,128)(2,1)S(1)} %pad_maximum_fusion.3), channel_id=1, source_target_pairs={{0,12},{4,0},{8,4},{12,8},{1,13},{5,1},{9,5},{13,9},{2,14},{6,2},{... | collective-permute-start | bytes 294920 | tf_op jit(solution)/shard_map/ppermute | solution.py:35
  43.4 2.5 %collective-permute-start.3 = (f16[4,96,128]{2,1,0:T(8,128)(2,1)S(1)}, f16[4,96,128]{2,1,0:T(8,128)(2,1)S(1)}, u32[]{:S(2)}, u32[]{:S(2)}) collective-permute-start(f16[4,96,128]{2,1,0:T(8,128)(2,1)S(1)} %pad_maximum_fusion.3), channel_id=1, source_target_pairs={{0,4},{4,8},{8,12},{12,0},{1,5},{5,9},{9,13},{13,1},{2,6},{6,10},{... | collective-permute-start | bytes 294920 | tf_op jit(solution)/shard_map/ppermute | solution.py:35
  45.9 0.7 collective-permute-done.5
  46.7 3.3 %collective-permute-done.3 = f16[4,96,128]{2,1,0:T(8,128)(2,1)S(1)} collective-permute-done((f16[4,96,128]{2,1,0:T(8,128)(2,1)S(1)}, f16[4,96,128]{2,1,0:T(8,128)(2,1)S(1)}, u32[]{:S(2)}, u32[]{:S(2)}) %collective-permute-start.3) | collective-permute-done | bytes 98336 | tf_op jit(solution)/shard_map/ppermute | solution.py:35
  50.4 5.9 %collective-permute-start.6 = (f16[24,32,384]{2,1,0:T(8,128)(2,1)S(1)}, f16[24,32,384]{2,1,0:T(8,128)(2,1)S(1)}, u32[]{:S(2)}, u32[]{:S(2)}) collective-permute-start(f16[24,32,384]{2,1,0:T(8,128)(2,1)S(1)} %all-to-all-done), channel_id=1, source_target_pairs={{0,16},{16,0},{1,17},{17,1},{2,18},{18,2},{3,19},{19,3},{4,20},{20... | collective-permute-start | bytes 1769480 | tf_op jit(solution)/shard_map/ppermute | solution.py:30
  59.8 0.9 pad_maximum_fusion.2
  60.7 4.3 %all-to-all-start.1 = ((f16[16,96,128]{2,1,0:T(8,128)(2,1)}), f16[16,96,128]{2,1,0:T(8,128)(2,1)S(1)}, u32[]{:S(2)}, u32[]{:S(2)}) async-start(f16[16,96,128]{2,1,0:T(8,128)(2,1)} %bitcast.33), calls=%async_computation.1 | async-start | bytes 786432 | tf_op jit(solution)/shard_map/all_to_all | solution.py:22
  65.0 13.7 %all-to-all-done.1 = f16[16,96,128]{2,1,0:T(8,128)(2,1)S(1)} async-done(((f16[16,96,128]{2,1,0:T(8,128)(2,1)}), f16[16,96,128]{2,1,0:T(8,128)(2,1)S(1)}, u32[]{:S(2)}, u32[]{:S(2)}) %all-to-all-start.1) | async-done | bytes 393248 | tf_op jit(solution)/shard_map/all_to_all | solution.py:22
  79.3 0.8 broadcast_in_dim.25
  80.2 5.3 %all-to-all-start.2 = ((bf16[16,96,128]{2,1,0:T(8,128)(2,1)}), bf16[16,96,128]{2,1,0:T(8,128)(2,1)S(1)}, u32[]{:S(2)}, u32[]{:S(2)}) async-start(bf16[16,96,128]{2,1,0:T(8,128)(2,1)} %broadcast_in_dim.25), calls=%async_computation.2 | async-start | bytes 786432 | tf_op jit(solution)/shard_map/all_to_all | solution.py:22
  86.1 3.1 %collective-permute-start.7 = (f16[768,384]{1,0:T(8,128)(2,1)S(1)}, f16[768,384]{1,0:T(8,128)(2,1)S(1)}, u32[]{:S(2)}, u32[]{:S(2)}) collective-permute-start(f16[768,384]{1,0:T(8,128)(2,1)S(1)} %fusion), channel_id=1, source_target_pairs={{0,16},{16,0},{1,17},{17,1},{2,18},{18,2},{3,19},{19,3},{4,20},{20... | collective-permute-start | bytes 1769480 | tf_op jit(solution)/shard_map/ppermute | solution.py:30
  89.2 10.0 %all-to-all-done.2 = bf16[16,96,128]{2,1,0:T(8,128)(2,1)S(1)} async-done(((bf16[16,96,128]{2,1,0:T(8,128)(2,1)}), bf16[16,96,128]{2,1,0:T(8,128)(2,1)S(1)}, u32[]{:S(2)}, u32[]{:S(2)}) %all-to-all-start.2) | async-done | bytes 393248 | tf_op jit(solution)/shard_map/all_to_all | solution.py:22
  99.5 4.4 %collective-permute-start.13 = (f16[768,320]{0,1:T(8,128)(2,1)S(1)}, f16[768,320]{0,1:T(8,128)(2,1)S(1)}, u32[]{:S(2)}, u32[]{:S(2)}) collective-permute-start(f16[768,320]{0,1:T(8,128)(2,1)S(1)} %fusion.1), channel_id=1, source_target_pairs={{0,16},{16,0},{1,17},{17,1},{2,18},{18,2},{3,19},{19,3},{4,20},{20... | collective-permute-start | bytes 1474568 | tf_op jit(solution)/shard_map/ppermute | solution.py:30
  103.9 0.7 multiply_add_fusion
  104.8 3.9 %collective-permute-start.8 = (f16[3,2,2,32,384]{4,3,0,1,2:T(8,128)(2,1)S(1)}, f16[3,2,2,32,384]{4,3,0,1,2:T(8,128)(2,1)S(1)}, u32[]{:S(2)}, u32[]{:S(2)}) collective-permute-start(f16[3,2,2,32,384]{4,3,0,1,2:T(8,128)(2,1)S(1)} %fusion.13), channel_id=1, source_target_pairs={{0,384},{384,0},{1,385},{385,1},{2,386},{386,2},{3,387},{387,3},{4... | collective-permute-start | bytes 884744 | tf_op jit(solution)/shard_map/ppermute | solution.py:105
  109.1 1.2 copy.31
  110.3 9.4 %all-to-all-start.3 = ((f16[24,32,320]{2,1,0:T(8,128)(2,1)}), f16[24,32,320]{2,1,0:T(8,128)(2,1)S(1)}, u32[]{:S(2)}, u32[]{:S(2)}) async-start(f16[24,32,320]{2,1,0:T(8,128)(2,1)} %bitcast.49), calls=%async_computation.3 | async-start | bytes 1179648 | tf_op jit(solution)/shard_map/all_to_all | solution.py:22
  119.9 3.2 %collective-permute-start.9 = (f16[3,2,32,384]{3,2,0,1:T(8,128)(2,1)S(1)}, f16[3,2,32,384]{3,2,0,1:T(8,128)(2,1)S(1)}, u32[]{:S(2)}, u32[]{:S(2)}) collective-permute-start(f16[3,2,32,384]{3,2,0,1:T(8,128)(2,1)S(1)} %fusion.14), channel_id=1, source_target_pairs={{0,32},{32,0},{64,96},{96,64},{128,160},{160,128},{192,224},{224,1... | collective-permute-start | bytes 442376 | tf_op jit(solution)/shard_map/ppermute | solution.py:105
  123.1 20.2 %collective-permute-done.9 = f16[3,2,32,384]{3,2,0,1:T(8,128)(2,1)S(1)} collective-permute-done((f16[3,2,32,384]{3,2,0,1:T(8,128)(2,1)S(1)}, f16[3,2,32,384]{3,2,0,1:T(8,128)(2,1)S(1)}, u32[]{:S(2)}, u32[]{:S(2)}) %collective-permute-start.9) | collective-permute-done | bytes 147488 | tf_op jit(solution)/shard_map/ppermute | solution.py:105
  143.3 3.3 %collective-permute-start.10 = (f16[3,32,384]{2,1,0:T(8,128)(2,1)S(1)}, f16[3,32,384]{2,1,0:T(8,128)(2,1)S(1)}, u32[]{:S(2)}, u32[]{:S(2)}) collective-permute-start(f16[3,32,384]{2,1,0:T(8,128)(2,1)S(1)} %fusion.15), channel_id=1, source_target_pairs={{0,64},{32,96},{64,0},{96,32},{128,192},{160,224},{192,128},{224,1... | collective-permute-start | bytes 221192 | tf_op jit(solution)/shard_map/ppermute | solution.py:105
  146.8 3.4 %collective-permute-done.10 = f16[3,32,384]{2,1,0:T(8,128)(2,1)S(1)} collective-permute-done((f16[3,32,384]{2,1,0:T(8,128)(2,1)S(1)}, f16[3,32,384]{2,1,0:T(8,128)(2,1)S(1)}, u32[]{:S(2)}, u32[]{:S(2)}) %collective-permute-start.10) | collective-permute-done | bytes 73760 | tf_op jit(solution)/shard_map/ppermute | solution.py:105
  150.2 7.8 %collective-permute-start.12 = (f16[32,384]{1,0:T(8,128)(2,1)S(1)}, f16[32,384]{1,0:T(8,128)(2,1)S(1)}, u32[]{:S(2)}, u32[]{:S(2)}) collective-permute-start(f16[32,384]{1,0:T(8,128)(2,1)S(1)} %get-tuple-element.19), channel_id=1, source_target_pairs={{0,256},{32,288},{64,320},{96,352},{128,0},{160,32},{192,64},{224,... | collective-permute-start | bytes 73736 | tf_op jit(solution)/shard_map/ppermute | solution.py:35
  158.0 2.8 %collective-permute-start.11 = (f16[32,384]{1,0:T(8,128)(2,1)S(1)}, f16[32,384]{1,0:T(8,128)(2,1)S(1)}, u32[]{:S(2)}, u32[]{:S(2)}) collective-permute-start(f16[32,384]{1,0:T(8,128)(2,1)S(1)} %get-tuple-element.18), channel_id=1, source_target_pairs={{0,128},{32,160},{64,192},{96,224},{128,256},{160,288},{192,320},{... | collective-permute-start | bytes 73736 | tf_op jit(solution)/shard_map/ppermute | solution.py:35
  160.8 5.7 %collective-permute-done.11 = f16[32,384]{1,0:T(8,128)(2,1)S(1)} collective-permute-done((f16[32,384]{1,0:T(8,128)(2,1)S(1)}, f16[32,384]{1,0:T(8,128)(2,1)S(1)}, u32[]{:S(2)}, u32[]{:S(2)}) %collective-permute-start.11) | collective-permute-done | bytes 24608 | tf_op jit(solution)/shard_map/ppermute | solution.py:35
  (46 shorter events, 8.0 us)
Async XLA Ops:
  0.6 98.6 %copy-start = (bf16[128,320]{0,1:T(8,128)(2,1)S(1)}, bf16[128,320]{0,1:T(8,128)(2,1)}, u32[]{:S(2)}) copy-start(bf16[128,320]{0,1:T(8,128)(2,1)} %param.8) | copy-start | bytes 245764
  0.6 18.7 %copy-start.1 = (f32[128,96]{0,1:T(8,128)S(1)}, f32[128,96]{0,1:T(8,128)}, u32[]{:S(2)}) copy-start(f32[128,96]{0,1:T(8,128)} %param.6) | copy-start | bytes 147460
  2.4 47.9 %all-to-all-start = ((f16[24,32,384]{2,1,0:T(8,128)(2,1)}), f16[24,32,384]{2,1,0:T(8,128)(2,1)S(1)}, u32[]{:S(2)}, u32[]{:S(2)}) async-start(f16[24,32,384]{2,1,0:T(8,128)(2,1)} %broadcast_in_dim.12), calls=%async_computation | async-start | bytes 1179648 | tf_op jit(solution)/shard_map/all_to_all | solution.py:22
  19.4 14.1 %collective-permute-start.2 = (f16[96,128]{1,0:T(8,128)(2,1)S(1)}, f16[96,128]{1,0:T(8,128)(2,1)S(1)}, u32[]{:S(2)}, u32[]{:S(2)}) collective-permute-start(f16[96,128]{1,0:T(8,128)(2,1)S(1)} %get-tuple-element.23), channel_id=1, source_target_pairs={{0,3},{1,0},{2,1},{3,2},{4,7},{5,4},{6,5},{7,6},{8,11},{9,8},{10,9... | collective-permute-start | bytes 73736 | tf_op jit(solution)/shard_map/ppermute | solution.py:35
  24.4 9.5 %collective-permute-start.1 = (f16[96,128]{1,0:T(8,128)(2,1)S(1)}, f16[96,128]{1,0:T(8,128)(2,1)S(1)}, u32[]{:S(2)}, u32[]{:S(2)}) collective-permute-start(f16[96,128]{1,0:T(8,128)(2,1)S(1)} %get-tuple-element.23), channel_id=1, source_target_pairs={{0,2},{1,3},{2,0},{3,1},{4,6},{5,7},{6,4},{7,5},{8,10},{9,11},{10,... | collective-permute-start | bytes 73736 | tf_op jit(solution)/shard_map/ppermute | solution.py:35
  28.8 7.1 %collective-permute-start = (f16[96,128]{1,0:T(8,128)(2,1)S(1)}, f16[96,128]{1,0:T(8,128)(2,1)S(1)}, u32[]{:S(2)}, u32[]{:S(2)}) collective-permute-start(f16[96,128]{1,0:T(8,128)(2,1)S(1)} %get-tuple-element.23), channel_id=1, source_target_pairs={{0,1},{1,2},{2,3},{3,0},{4,5},{5,6},{6,7},{7,4},{8,9},{9,10},{10,1... | collective-permute-start | bytes 73736 | tf_op jit(solution)/shard_map/ppermute | solution.py:35
  36.0 10.0 %collective-permute-start.4 = (f16[4,96,128]{2,1,0:T(8,128)(2,1)S(1)}, f16[4,96,128]{2,1,0:T(8,128)(2,1)S(1)}, u32[]{:S(2)}, u32[]{:S(2)}) collective-permute-start(f16[4,96,128]{2,1,0:T(8,128)(2,1)S(1)} %pad_maximum_fusion.3), channel_id=1, source_target_pairs={{0,8},{4,12},{8,0},{12,4},{1,9},{5,13},{9,1},{13,5},{2,10},{6,14},... | collective-permute-start | bytes 294920 | tf_op jit(solution)/shard_map/ppermute | solution.py:35
  40.6 6.0 %collective-permute-start.5 = (f16[4,96,128]{2,1,0:T(8,128)(2,1)S(1)}, f16[4,96,128]{2,1,0:T(8,128)(2,1)S(1)}, u32[]{:S(2)}, u32[]{:S(2)}) collective-permute-start(f16[4,96,128]{2,1,0:T(8,128)(2,1)S(1)} %pad_maximum_fusion.3), channel_id=1, source_target_pairs={{0,12},{4,0},{8,4},{12,8},{1,13},{5,1},{9,5},{13,9},{2,14},{6,2},{... | collective-permute-start | bytes 294920 | tf_op jit(solution)/shard_map/ppermute | solution.py:35
  43.4 6.6 %collective-permute-start.3 = (f16[4,96,128]{2,1,0:T(8,128)(2,1)S(1)}, f16[4,96,128]{2,1,0:T(8,128)(2,1)S(1)}, u32[]{:S(2)}, u32[]{:S(2)}) collective-permute-start(f16[4,96,128]{2,1,0:T(8,128)(2,1)S(1)} %pad_maximum_fusion.3), channel_id=1, source_target_pairs={{0,4},{4,8},{8,12},{12,0},{1,5},{5,9},{9,13},{13,1},{2,6},{6,10},{... | collective-permute-start | bytes 294920 | tf_op jit(solution)/shard_map/ppermute | solution.py:35
  50.4 7.5 %collective-permute-start.6 = (f16[24,32,384]{2,1,0:T(8,128)(2,1)S(1)}, f16[24,32,384]{2,1,0:T(8,128)(2,1)S(1)}, u32[]{:S(2)}, u32[]{:S(2)}) collective-permute-start(f16[24,32,384]{2,1,0:T(8,128)(2,1)S(1)} %all-to-all-done), channel_id=1, source_target_pairs={{0,16},{16,0},{1,17},{17,1},{2,18},{18,2},{3,19},{19,3},{4,20},{20... | collective-permute-start | bytes 1769480 | tf_op jit(solution)/shard_map/ppermute | solution.py:30
  56.4 1.4 copy-start.2
  60.7 18.0 %all-to-all-start.1 = ((f16[16,96,128]{2,1,0:T(8,128)(2,1)}), f16[16,96,128]{2,1,0:T(8,128)(2,1)S(1)}, u32[]{:S(2)}, u32[]{:S(2)}) async-start(f16[16,96,128]{2,1,0:T(8,128)(2,1)} %bitcast.33), calls=%async_computation.1 | async-start | bytes 786432 | tf_op jit(solution)/shard_map/all_to_all | solution.py:22
  80.2 19.0 %all-to-all-start.2 = ((bf16[16,96,128]{2,1,0:T(8,128)(2,1)}), bf16[16,96,128]{2,1,0:T(8,128)(2,1)S(1)}, u32[]{:S(2)}, u32[]{:S(2)}) async-start(bf16[16,96,128]{2,1,0:T(8,128)(2,1)} %broadcast_in_dim.25), calls=%async_computation.2 | async-start | bytes 786432 | tf_op jit(solution)/shard_map/all_to_all | solution.py:22
  86.1 17.9 %collective-permute-start.7 = (f16[768,384]{1,0:T(8,128)(2,1)S(1)}, f16[768,384]{1,0:T(8,128)(2,1)S(1)}, u32[]{:S(2)}, u32[]{:S(2)}) collective-permute-start(f16[768,384]{1,0:T(8,128)(2,1)S(1)} %fusion), channel_id=1, source_target_pairs={{0,16},{16,0},{1,17},{17,1},{2,18},{18,2},{3,19},{19,3},{4,20},{20... | collective-permute-start | bytes 1769480 | tf_op jit(solution)/shard_map/ppermute | solution.py:30
  99.5 9.3 %collective-permute-start.13 = (f16[768,320]{0,1:T(8,128)(2,1)S(1)}, f16[768,320]{0,1:T(8,128)(2,1)S(1)}, u32[]{:S(2)}, u32[]{:S(2)}) collective-permute-start(f16[768,320]{0,1:T(8,128)(2,1)S(1)} %fusion.1), channel_id=1, source_target_pairs={{0,16},{16,0},{1,17},{17,1},{2,18},{18,2},{3,19},{19,3},{4,20},{20... | collective-permute-start | bytes 1474568 | tf_op jit(solution)/shard_map/ppermute | solution.py:30
  104.8 14.9 %collective-permute-start.8 = (f16[3,2,2,32,384]{4,3,0,1,2:T(8,128)(2,1)S(1)}, f16[3,2,2,32,384]{4,3,0,1,2:T(8,128)(2,1)S(1)}, u32[]{:S(2)}, u32[]{:S(2)}) collective-permute-start(f16[3,2,2,32,384]{4,3,0,1,2:T(8,128)(2,1)S(1)} %fusion.13), channel_id=1, source_target_pairs={{0,384},{384,0},{1,385},{385,1},{2,386},{386,2},{3,387},{387,3},{4... | collective-permute-start | bytes 884744 | tf_op jit(solution)/shard_map/ppermute | solution.py:105
  110.3 56.7 %all-to-all-start.3 = ((f16[24,32,320]{2,1,0:T(8,128)(2,1)}), f16[24,32,320]{2,1,0:T(8,128)(2,1)S(1)}, u32[]{:S(2)}, u32[]{:S(2)}) async-start(f16[24,32,320]{2,1,0:T(8,128)(2,1)} %bitcast.49), calls=%async_computation.3 | async-start | bytes 1179648 | tf_op jit(solution)/shard_map/all_to_all | solution.py:22
  119.9 23.4 %collective-permute-start.9 = (f16[3,2,32,384]{3,2,0,1:T(8,128)(2,1)S(1)}, f16[3,2,32,384]{3,2,0,1:T(8,128)(2,1)S(1)}, u32[]{:S(2)}, u32[]{:S(2)}) collective-permute-start(f16[3,2,32,384]{3,2,0,1:T(8,128)(2,1)S(1)} %fusion.14), channel_id=1, source_target_pairs={{0,32},{32,0},{64,96},{96,64},{128,160},{160,128},{192,224},{224,1... | collective-permute-start | bytes 442376 | tf_op jit(solution)/shard_map/ppermute | solution.py:105
  143.3 6.8 %collective-permute-start.10 = (f16[3,32,384]{2,1,0:T(8,128)(2,1)S(1)}, f16[3,32,384]{2,1,0:T(8,128)(2,1)S(1)}, u32[]{:S(2)}, u32[]{:S(2)}) collective-permute-start(f16[3,32,384]{2,1,0:T(8,128)(2,1)S(1)} %fusion.15), channel_id=1, source_target_pairs={{0,64},{32,96},{64,0},{96,32},{128,192},{160,224},{192,128},{224,1... | collective-permute-start | bytes 221192 | tf_op jit(solution)/shard_map/ppermute | solution.py:105
  150.2 10.6 %collective-permute-start.12 = (f16[32,384]{1,0:T(8,128)(2,1)S(1)}, f16[32,384]{1,0:T(8,128)(2,1)S(1)}, u32[]{:S(2)}, u32[]{:S(2)}) collective-permute-start(f16[32,384]{1,0:T(8,128)(2,1)S(1)} %get-tuple-element.19), channel_id=1, source_target_pairs={{0,256},{32,288},{64,320},{96,352},{128,0},{160,32},{192,64},{224,... | collective-permute-start | bytes 73736 | tf_op jit(solution)/shard_map/ppermute | solution.py:35
  158.0 8.5 %collective-permute-start.11 = (f16[32,384]{1,0:T(8,128)(2,1)S(1)}, f16[32,384]{1,0:T(8,128)(2,1)S(1)}, u32[]{:S(2)}, u32[]{:S(2)}) collective-permute-start(f16[32,384]{1,0:T(8,128)(2,1)S(1)} %get-tuple-element.18), channel_id=1, source_target_pairs={{0,128},{32,160},{64,192},{96,224},{128,256},{160,288},{192,320},{... | collective-permute-start | bytes 73736 | tf_op jit(solution)/shard_map/ppermute | solution.py:35

commit v2 on v1

--- a/solution.py
+++ b/solution.py
@@ -14,7 +14,7 @@
 
 EMB_UP = 2.0**18
 IMAGE_UP = 2.0**10
-TEXT_UP = (2.0**11, 2.0**10, 2.0**9, 2.0**8, 2.0**7)
+TEXT_UP = (2.0**11, 2.0**10, 2.0**9, 2.0**7, 2.0**6)
 PROJ_UP = (2.0**-2, 2.0**-3)
 
 
@@ -66,7 +66,8 @@
     other = swap(own).reshape(768, -1).astype(F32)
     own = own.reshape(768, -1).astype(F32)
     near = jnp.stack([image_tile] + [shifted(image_tile, "yh", k) for k in (1, 2, 3)])
-    far = [near] + [shifted(near, "x", k) for k in (1, 2, 3)]
+    far = [near] + [shifted(near, "x", k) for k in (1, 3)]
+    far.insert(2, shifted(near, "x", 2))
     by_x = in_order(far, lax.axis_index("x"))
     image_full = in_order([by_x[:, k] for k in range(4)], lax.axis_index("yh"))
     image_full = jnp.moveaxis(image_full, 0, 1).astype(F32)
@@ -95,32 +96,33 @@
     mine = dot(image_own, slope, 1, 0)
     tiles = mine * (1.0 / EMB_UP) + got.astype(F32) * (1.0 / TEXT_UP[0])
     tiles = tiles.reshape(2, 3, 2, 2, 32, text_rows)
-    stages = (
-        ("yl", yl, 0, ((0, 1), (1, 0))),
-        ("z", z % 2, 2, tuple((i, i ^ 1) for i in range(12))),
-        ("z", (z // 2) % 2, 1, tuple((i, i ^ 2) for i in range(12))),
-    )
-    for k, (axis, place, dim, pairs) in enumerate(stages, 1):
+
+    def halve(tiles, k, axis, place, dim, pairs):
         theirs = lax.dynamic_index_in_dim(tiles, 1 - place, dim, keepdims=False)
         got = lax.ppermute((theirs * TEXT_UP[k]).astype(HALF), axis, pairs)
         mine = lax.dynamic_index_in_dim(tiles, place, dim, keepdims=False)
-        tiles = mine + got.astype(F32) * (1.0 / TEXT_UP[k])
+        return mine + got.astype(F32) * (1.0 / TEXT_UP[k])
+
+    tiles = halve(tiles, 1, "yl", yl, 0, ((0, 1), (1, 0)))
     block = z // 4
-    total = lax.dynamic_index_in_dim(tiles, block, 0, keepdims=False)
+    came = []
     for step in (1, 2):
         theirs = lax.dynamic_index_in_dim(tiles, (block + step) % 3, 0, keepdims=False)
-        got = shifted((theirs * TEXT_UP[4]).astype(HALF), "z", 4 * step)
-        total = total + got.astype(F32) * (1.0 / TEXT_UP[4])
+        came.append(shifted((theirs * TEXT_UP[2]).astype(HALF), "z", 4 * step))
+    tiles = lax.dynamic_index_in_dim(tiles, block, 0, keepdims=False)
+    tiles = tiles + (came[0].astype(F32) + came[1].astype(F32)) * (1.0 / TEXT_UP[2])
+    tiles = halve(tiles, 3, "z", z % 2, 1, tuple((i, i ^ 1) for i in range(12)))
+    total = halve(tiles, 4, "z", (z // 2) % 2, 0, tuple((i, i ^ 2) for i in range(12)))
     grad_text = total * scale
 
     def weights(which):
-        low = of_core(image_low, which)
-        return lax.dot_general(low, vision_feat, (((1,), (0,)), ((), ())), preferred_element_type=F32)
+        low = of_core(image_low, which).reshape(24, 32, -1)
+        return lax.dot_general(low, vision_feat, (((2,), (0,)), ((), ())), preferred_element_type=F32)
 
     got = swap((weights(1 - core) * PROJ_UP[0]).astype(HALF))
     mine = weights(core)
     sent = ((mine + got.astype(F32) * (1.0 / PROJ_UP[0])) * PROJ_UP[1]).astype(HALF)
-    got = exchange(sent.reshape(24, 32, -1), CHIPS)
+    got = exchange(sent, CHIPS)
     grad_proj = got.astype(F32).sum(axis=0) * (1.0 / PROJ_UP[1])
     return (grad_image.T, grad_text.T, grad_proj.T)
 

time: 170 us -> 167 us (0.982)
  the two profiles are of different devices: /device:TPU:1 before, /device:TPU:8 now
where the time goes in v2:
time: 167 us; the launch traced here: 166 us
  starting transfers between devices  85.1 us (51%)
  waiting for transfers between devices  65.6 us (39%)
  matrix products  6.44 us (4%)
  other arithmetic  4.75 us (3%)
  between operations  2.49 us (1%)
  local copies, waits for them, and re-layouts  1.9 us (1%)
    all_to_all x4, starting transfers between devices, exchange(): return lax.all_to_all(tiles, axis, split_axis=0, concat_axis=0, tiled=True)  36.2 us
    ppermute x8, starting transfers between devices, shifted(): lax.ppermute(array, axis, tuple(((i, (i + step) % length) for i in range(...  34.1 us
    ppermute x8, waiting for transfers between devices, shifted(): lax.ppermute(array, axis, tuple(((i, (i + step) % length) for i in range(...  30.3 us
    all_to_all x4, waiting for transfers between devices, exchange(): return lax.all_to_all(tiles, axis, split_axis=0, concat_axis=0, tiled=True)  28.9 us
    ppermute x3, starting transfers between devices, halve(): got = lax.ppermute((theirs * TEXT_UP[k]).astype(HALF), axis, pairs)  8.98 us
    ppermute x3, starting transfers between devices, swap(): return lax.ppermute(array, 'core', ((0, 1), (1, 0)))  5.76 us
    ppermute x3, waiting for transfers between devices, halve(): got = lax.ppermute((theirs * TEXT_UP[k]).astype(HALF), axis, pairs)  5.49 us
    dot_general x6, matrix products, dot(): lax.dot_general(a, b, (((ca,), (cb,)), ((), ())), precision=HIGH, preferr...  4.94 us
  transfers between devices with their start and end apart: 18, of which 10 were waited for; matrix products, arithmetic and copies ran while one was open for 4% of the time, Pallas kernels for 0%

profile of v2, /device:TPU:8, one launch (start us, length us, event | category | flops | bytes accessed | tf_op | source)
XLA Modules:
  0.0 166.2 jit_solution(18085318048325977049)
XLA Ops:
  0.7 0.9 fusion.28
  1.5 0.9 broadcast_in_dim.12
  2.4 16.7 %all-to-all-start = ((f16[24,32,384]{2,1,0:T(8,128)(2,1)}), f16[24,32,384]{2,1,0:T(8,128)(2,1)S(1)}, u32[]{:S(2)}, u32[]{:S(2)}) async-start(f16[24,32,384]{2,1,0:T(8,128)(2,1)} %broadcast_in_dim.12), calls=%async_computation | async-start | bytes 1179648 | tf_op jit(solution)/shard_map/all_to_all | solution.py:22
  19.1 5.3 %collective-permute-start.2 = (f16[96,128]{1,0:T(8,128)(2,1)S(1)}, f16[96,128]{1,0:T(8,128)(2,1)S(1)}, u32[]{:S(2)}, u32[]{:S(2)}) collective-permute-start(f16[96,128]{1,0:T(8,128)(2,1)S(1)} %get-tuple-element.21), channel_id=1, source_target_pairs={{0,3},{1,0},{2,1},{3,2},{4,7},{5,4},{6,5},{7,6},{8,11},{9,8},{10,9... | collective-permute-start | bytes 73736 | tf_op jit(solution)/shard_map/ppermute | solution.py:35
  24.4 4.7 %collective-permute-start.1 = (f16[96,128]{1,0:T(8,128)(2,1)S(1)}, f16[96,128]{1,0:T(8,128)(2,1)S(1)}, u32[]{:S(2)}, u32[]{:S(2)}) collective-permute-start(f16[96,128]{1,0:T(8,128)(2,1)S(1)} %get-tuple-element.21), channel_id=1, source_target_pairs={{0,2},{1,3},{2,0},{3,1},{4,6},{5,7},{6,4},{7,5},{8,10},{9,11},{10,... | collective-permute-start | bytes 73736 | tf_op jit(solution)/shard_map/ppermute | solution.py:35
  29.1 3.6 %collective-permute-start = (f16[96,128]{1,0:T(8,128)(2,1)S(1)}, f16[96,128]{1,0:T(8,128)(2,1)S(1)}, u32[]{:S(2)}, u32[]{:S(2)}) collective-permute-start(f16[96,128]{1,0:T(8,128)(2,1)S(1)} %get-tuple-element.21), channel_id=1, source_target_pairs={{0,1},{1,2},{2,3},{3,0},{4,5},{5,6},{6,7},{7,4},{8,9},{9,10},{10,1... | collective-permute-start | bytes 73736 | tf_op jit(solution)/shard_map/ppermute | solution.py:35
  34.2 2.9 %collective-permute-done = f16[96,128]{1,0:T(8,128)(2,1)S(1)} collective-permute-done((f16[96,128]{1,0:T(8,128)(2,1)S(1)}, f16[96,128]{1,0:T(8,128)(2,1)S(1)}, u32[]{:S(2)}, u32[]{:S(2)}) %collective-permute-start) | collective-permute-done | bytes 24608 | tf_op jit(solution)/shard_map/ppermute | solution.py:35
  37.1 4.9 %collective-permute-start.4 = (f16[4,96,128]{2,1,0:T(8,128)(2,1)S(1)}, f16[4,96,128]{2,1,0:T(8,128)(2,1)S(1)}, u32[]{:S(2)}, u32[]{:S(2)}) collective-permute-start(f16[4,96,128]{2,1,0:T(8,128)(2,1)S(1)} %pad_maximum_fusion.3), channel_id=1, source_target_pairs={{0,8},{4,12},{8,0},{12,4},{1,9},{5,13},{9,1},{13,5},{2,10},{6,14},... | collective-permute-start | bytes 294920 | tf_op jit(solution)/shard_map/ppermute | solution.py:35
  42.0 3.0 %collective-permute-start.5 = (f16[4,96,128]{2,1,0:T(8,128)(2,1)S(1)}, f16[4,96,128]{2,1,0:T(8,128)(2,1)S(1)}, u32[]{:S(2)}, u32[]{:S(2)}) collective-permute-start(f16[4,96,128]{2,1,0:T(8,128)(2,1)S(1)} %pad_maximum_fusion.3), channel_id=1, source_target_pairs={{0,12},{4,0},{8,4},{12,8},{1,13},{5,1},{9,5},{13,9},{2,14},{6,2},{... | collective-permute-start | bytes 294920 | tf_op jit(solution)/shard_map/ppermute | solution.py:35
  45.1 2.8 %collective-permute-start.3 = (f16[4,96,128]{2,1,0:T(8,128)(2,1)S(1)}, f16[4,96,128]{2,1,0:T(8,128)(2,1)S(1)}, u32[]{:S(2)}, u32[]{:S(2)}) collective-permute-start(f16[4,96,128]{2,1,0:T(8,128)(2,1)S(1)} %pad_maximum_fusion.3), channel_id=1, source_target_pairs={{0,4},{4,8},{8,12},{12,0},{1,5},{5,9},{9,13},{13,1},{2,6},{6,10},{... | collective-permute-start | bytes 294920 | tf_op jit(solution)/shard_map/ppermute | solution.py:35
  48.5 4.3 %collective-permute-done.3 = f16[4,96,128]{2,1,0:T(8,128)(2,1)S(1)} collective-permute-done((f16[4,96,128]{2,1,0:T(8,128)(2,1)S(1)}, f16[4,96,128]{2,1,0:T(8,128)(2,1)S(1)}, u32[]{:S(2)}, u32[]{:S(2)}) %collective-permute-start.3) | collective-permute-done | bytes 98336 | tf_op jit(solution)/shard_map/ppermute | solution.py:35
  53.2 1.9 %collective-permute-start.6 = (f16[24,32,384]{2,1,0:T(8,128)(2,1)S(1)}, f16[24,32,384]{2,1,0:T(8,128)(2,1)S(1)}, u32[]{:S(2)}, u32[]{:S(2)}) collective-permute-start(f16[24,32,384]{2,1,0:T(8,128)(2,1)S(1)} %all-to-all-done), channel_id=1, source_target_pairs={{0,16},{16,0},{1,17},{17,1},{2,18},{18,2},{3,19},{19,3},{4,20},{20... | collective-permute-start | bytes 1769480 | tf_op jit(solution)/shard_map/ppermute | solution.py:30
  56.1 0.9 collective-permute-done.6
  59.1 0.9 pad_maximum_fusion.2
  59.9 4.5 %all-to-all-start.1 = ((f16[16,96,128]{2,1,0:T(8,128)(2,1)}), f16[16,96,128]{2,1,0:T(8,128)(2,1)S(1)}, u32[]{:S(2)}, u32[]{:S(2)}) async-start(f16[16,96,128]{2,1,0:T(8,128)(2,1)} %bitcast.33), calls=%async_computation.1 | async-start | bytes 786432 | tf_op jit(solution)/shard_map/all_to_all | solution.py:22
  64.4 15.7 %all-to-all-done.1 = f16[16,96,128]{2,1,0:T(8,128)(2,1)S(1)} async-done(((f16[16,96,128]{2,1,0:T(8,128)(2,1)}), f16[16,96,128]{2,1,0:T(8,128)(2,1)S(1)}, u32[]{:S(2)}, u32[]{:S(2)}) %all-to-all-start.1) | async-done | bytes 393248 | tf_op jit(solution)/shard_map/all_to_all | solution.py:22
  80.9 0.8 broadcast_in_dim.25
  81.7 3.6 %all-to-all-start.2 = ((bf16[16,96,128]{2,1,0:T(8,128)(2,1)}), bf16[16,96,128]{2,1,0:T(8,128)(2,1)S(1)}, u32[]{:S(2)}, u32[]{:S(2)}) async-start(bf16[16,96,128]{2,1,0:T(8,128)(2,1)} %broadcast_in_dim.25), calls=%async_computation.2 | async-start | bytes 786432 | tf_op jit(solution)/shard_map/all_to_all | solution.py:22
  85.9 1.9 %collective-permute-start.7 = (f16[768,384]{1,0:T(8,128)(2,1)S(1)}, f16[768,384]{1,0:T(8,128)(2,1)}, u32[]{:S(2)}, u32[]{:S(2)}) collective-permute-start(f16[768,384]{1,0:T(8,128)(2,1)S(1)} %fusion), channel_id=1, source_target_pairs={{0,16},{16,0},{1,17},{17,1},{2,18},{18,2},{3,19},{19,3},{4,20},{20... | collective-permute-start | bytes 1769480 | tf_op jit(solution)/shard_map/ppermute | solution.py:30
  87.8 13.1 %all-to-all-done.2 = bf16[16,96,128]{2,1,0:T(8,128)(2,1)S(1)} async-done(((bf16[16,96,128]{2,1,0:T(8,128)(2,1)}), bf16[16,96,128]{2,1,0:T(8,128)(2,1)S(1)}, u32[]{:S(2)}, u32[]{:S(2)}) %all-to-all-start.2) | async-done | bytes 393248 | tf_op jit(solution)/shard_map/all_to_all | solution.py:22
  101.2 1.9 %collective-permute-start.13 = (f16[24,32,320]{2,1,0:T(8,128)(2,1)S(1)}, f16[24,32,320]{2,1,0:T(8,128)(2,1)S(1)}, u32[]{:S(2)}, u32[]{:S(2)}) collective-permute-start(f16[24,32,320]{2,1,0:T(8,128)(2,1)S(1)} %fusion.1), channel_id=1, source_target_pairs={{0,16},{16,0},{1,17},{17,1},{2,18},{18,2},{3,19},{19,3},{4,20},{20... | collective-permute-start | bytes 1474568 | tf_op jit(solution)/shard_map/ppermute | solution.py:30
  103.2 1.8 %multiply_add_fusion = f32[768,384]{1,0:T(8,128)S(1)} fusion(f16[768,384]{1,0:T(8,128)(2,1)} %collective-permute-done.7, f16[768,128]{1,0:T(8,128)(2,1)S(1)} %bitcast.117, f32[128,384]{1,0:T(8,128)S(1)} %fusion.11), kind=kOutput, calls=%fused_computation.9 | convolution fusion | flops 227672064 | bytes 2162688 | tf_op jit(solution)/shard_map/dot_general | solution.py:55
  105.1 1.9 %collective-permute-start.8 = (f16[3,2,2,32,384]{4,3,1,2,0:T(8,128)(2,1)S(1)}, f16[3,2,2,32,384]{4,3,1,2,0:T(8,128)(2,1)S(1)}, u32[]{:S(2)}, u32[]{:S(2)}) collective-permute-start(f16[3,2,2,32,384]{4,3,1,2,0:T(8,128)(2,1)S(1)} %fusion.13), channel_id=1, source_target_pairs={{0,384},{384,0},{1,385},{385,1},{2,386},{386,2},{3,387},{387,3},{4... | collective-permute-start | bytes 884744 | tf_op jit(solution)/shard_map/ppermute | solution.py:102
  107.1 1.2 multiply_convert_fusion
  108.3 11.5 %all-to-all-start.3 = ((f16[24,32,320]{2,1,0:T(8,128)(2,1)}), f16[24,32,320]{2,1,0:T(8,128)(2,1)S(1)}, u32[]{:S(2)}, u32[]{:S(2)}) async-start(f16[24,32,320]{2,1,0:T(8,128)(2,1)} %multiply_convert_fusion), calls=%async_computation.3 | async-start | bytes 1179648 | tf_op jit(solution)/shard_map/all_to_all | solution.py:22
  120.0 7.3 %collective-permute-start.10 = (f16[2,2,32,384]{3,2,0,1:T(8,128)(2,1)S(1)}, f16[2,2,32,384]{3,2,0,1:T(8,128)(2,1)S(1)}, u32[]{:S(2)}, u32[]{:S(2)}) collective-permute-start(f16[2,2,32,384]{3,2,0,1:T(8,128)(2,1)S(1)} %get-tuple-element.6), channel_id=1, source_target_pairs={{0,256},{32,288},{64,320},{96,352},{128,0},{160,32},{192,64},{224,... | collective-permute-start | bytes 294920 | tf_op jit(solution)/shard_map/ppermute | solution.py:35
  127.3 2.5 %collective-permute-start.9 = (f16[2,2,32,384]{3,2,0,1:T(8,128)(2,1)S(1)}, f16[2,2,32,384]{3,2,0,1:T(8,128)(2,1)S(1)}, u32[]{:S(2)}, u32[]{:S(2)}) collective-permute-start(f16[2,2,32,384]{3,2,0,1:T(8,128)(2,1)S(1)} %get-tuple-element.5), channel_id=1, source_target_pairs={{0,128},{32,160},{64,192},{96,224},{128,256},{160,288},{192,320},{... | collective-permute-start | bytes 294920 | tf_op jit(solution)/shard_map/ppermute | solution.py:35
  129.8 22.4 %collective-permute-done.10 = f16[2,2,32,384]{3,2,0,1:T(8,128)(2,1)S(1)} collective-permute-done((f16[2,2,32,384]{3,2,0,1:T(8,128)(2,1)S(1)}, f16[2,2,32,384]{3,2,0,1:T(8,128)(2,1)S(1)}, u32[]{:S(2)}, u32[]{:S(2)}) %collective-permute-start.10) | collective-permute-done | bytes 98336 | tf_op jit(solution)/shard_map/ppermute | solution.py:35
  152.2 2.4 %collective-permute-start.11 = (f16[2,32,384]{2,1,0:T(8,128)(2,1)S(1)}, f16[2,32,384]{2,1,0:T(8,128)(2,1)S(1)}, u32[]{:S(2)}, u32[]{:S(2)}) collective-permute-start(f16[2,32,384]{2,1,0:T(8,128)(2,1)S(1)} %fusion.25), channel_id=1, source_target_pairs={{0,32},{32,0},{64,96},{96,64},{128,160},{160,128},{192,224},{224,1... | collective-permute-start | bytes 147464 | tf_op jit(solution)/shard_map/ppermute | solution.py:102
  154.7 3.5 %collective-permute-done.11 = f16[2,32,384]{2,1,0:T(8,128)(2,1)S(1)} collective-permute-done((f16[2,32,384]{2,1,0:T(8,128)(2,1)S(1)}, f16[2,32,384]{2,1,0:T(8,128)(2,1)S(1)}, u32[]{:S(2)}, u32[]{:S(2)}) %collective-permute-start.11) | collective-permute-done | bytes 49184 | tf_op jit(solution)/shard_map/ppermute | solution.py:102
  158.3 4.7 %collective-permute-start.12 = (f16[32,384]{1,0:T(8,128)(2,1)S(1)}, f16[32,384]{1,0:T(8,128)(2,1)S(1)}, u32[]{:S(2)}, u32[]{:S(2)}) collective-permute-start(f16[32,384]{1,0:T(8,128)(2,1)S(1)} %fusion.29), channel_id=1, source_target_pairs={{0,64},{32,96},{64,0},{96,32},{128,192},{160,224},{192,128},{224,1... | collective-permute-start | bytes 73736 | tf_op jit(solution)/shard_map/ppermute | solution.py:102
  162.9 1.9 %collective-permute-done.12 = f16[32,384]{1,0:T(8,128)(2,1)S(1)} collective-permute-done((f16[32,384]{1,0:T(8,128)(2,1)S(1)}, f16[32,384]{1,0:T(8,128)(2,1)S(1)}, u32[]{:S(2)}, u32[]{:S(2)}) %collective-permute-start.12) | collective-permute-done | bytes 24608 | tf_op jit(solution)/shard_map/ppermute | solution.py:102
  (44 shorter events, 7.5 us)
Async XLA Ops:
  0.6 100.3 %copy-start = (bf16[128,320]{0,1:T(8,128)(2,1)S(1)}, bf16[128,320]{0,1:T(8,128)(2,1)}, u32[]{:S(2)}) copy-start(bf16[128,320]{0,1:T(8,128)(2,1)} %param.8) | copy-start | bytes 245764
  0.6 18.4 %copy-start.1 = (f32[128,96]{0,1:T(8,128)S(1)}, f32[128,96]{0,1:T(8,128)}, u32[]{:S(2)}) copy-start(f32[128,96]{0,1:T(8,128)} %param.6) | copy-start | bytes 147460
  2.4 50.8 %all-to-all-start = ((f16[24,32,384]{2,1,0:T(8,128)(2,1)}), f16[24,32,384]{2,1,0:T(8,128)(2,1)S(1)}, u32[]{:S(2)}, u32[]{:S(2)}) async-start(f16[24,32,384]{2,1,0:T(8,128)(2,1)} %broadcast_in_dim.12), calls=%async_computation | async-start | bytes 1179648 | tf_op jit(solution)/shard_map/all_to_all | solution.py:22
  19.1 14.9 %collective-permute-start.2 = (f16[96,128]{1,0:T(8,128)(2,1)S(1)}, f16[96,128]{1,0:T(8,128)(2,1)S(1)}, u32[]{:S(2)}, u32[]{:S(2)}) collective-permute-start(f16[96,128]{1,0:T(8,128)(2,1)S(1)} %get-tuple-element.21), channel_id=1, source_target_pairs={{0,3},{1,0},{2,1},{3,2},{4,7},{5,4},{6,5},{7,6},{8,11},{9,8},{10,9... | collective-permute-start | bytes 73736 | tf_op jit(solution)/shard_map/ppermute | solution.py:35
  24.4 9.8 %collective-permute-start.1 = (f16[96,128]{1,0:T(8,128)(2,1)S(1)}, f16[96,128]{1,0:T(8,128)(2,1)S(1)}, u32[]{:S(2)}, u32[]{:S(2)}) collective-permute-start(f16[96,128]{1,0:T(8,128)(2,1)S(1)} %get-tuple-element.21), channel_id=1, source_target_pairs={{0,2},{1,3},{2,0},{3,1},{4,6},{5,7},{6,4},{7,5},{8,10},{9,11},{10,... | collective-permute-start | bytes 73736 | tf_op jit(solution)/shard_map/ppermute | solution.py:35
  29.1 7.9 %collective-permute-start = (f16[96,128]{1,0:T(8,128)(2,1)S(1)}, f16[96,128]{1,0:T(8,128)(2,1)S(1)}, u32[]{:S(2)}, u32[]{:S(2)}) collective-permute-start(f16[96,128]{1,0:T(8,128)(2,1)S(1)} %get-tuple-element.21), channel_id=1, source_target_pairs={{0,1},{1,2},{2,3},{3,0},{4,5},{5,6},{6,7},{7,4},{8,9},{9,10},{10,1... | collective-permute-start | bytes 73736 | tf_op jit(solution)/shard_map/ppermute | solution.py:35
  37.1 10.8 %collective-permute-start.4 = (f16[4,96,128]{2,1,0:T(8,128)(2,1)S(1)}, f16[4,96,128]{2,1,0:T(8,128)(2,1)S(1)}, u32[]{:S(2)}, u32[]{:S(2)}) collective-permute-start(f16[4,96,128]{2,1,0:T(8,128)(2,1)S(1)} %pad_maximum_fusion.3), channel_id=1, source_target_pairs={{0,8},{4,12},{8,0},{12,4},{1,9},{5,13},{9,1},{13,5},{2,10},{6,14},... | collective-permute-start | bytes 294920 | tf_op jit(solution)/shard_map/ppermute | solution.py:35
  42.0 6.5 %collective-permute-start.5 = (f16[4,96,128]{2,1,0:T(8,128)(2,1)S(1)}, f16[4,96,128]{2,1,0:T(8,128)(2,1)S(1)}, u32[]{:S(2)}, u32[]{:S(2)}) collective-permute-start(f16[4,96,128]{2,1,0:T(8,128)(2,1)S(1)} %pad_maximum_fusion.3), channel_id=1, source_target_pairs={{0,12},{4,0},{8,4},{12,8},{1,13},{5,1},{9,5},{13,9},{2,14},{6,2},{... | collective-permute-start | bytes 294920 | tf_op jit(solution)/shard_map/ppermute | solution.py:35
  45.1 7.7 %collective-permute-start.3 = (f16[4,96,128]{2,1,0:T(8,128)(2,1)S(1)}, f16[4,96,128]{2,1,0:T(8,128)(2,1)S(1)}, u32[]{:S(2)}, u32[]{:S(2)}) collective-permute-start(f16[4,96,128]{2,1,0:T(8,128)(2,1)S(1)} %pad_maximum_fusion.3), channel_id=1, source_target_pairs={{0,4},{4,8},{8,12},{12,0},{1,5},{5,9},{9,13},{13,1},{2,6},{6,10},{... | collective-permute-start | bytes 294920 | tf_op jit(solution)/shard_map/ppermute | solution.py:35
  53.2 3.9 %collective-permute-start.6 = (f16[24,32,384]{2,1,0:T(8,128)(2,1)S(1)}, f16[24,32,384]{2,1,0:T(8,128)(2,1)S(1)}, u32[]{:S(2)}, u32[]{:S(2)}) collective-permute-start(f16[24,32,384]{2,1,0:T(8,128)(2,1)S(1)} %all-to-all-done), channel_id=1, source_target_pairs={{0,16},{16,0},{1,17},{17,1},{2,18},{18,2},{3,19},{19,3},{4,20},{20... | collective-permute-start | bytes 1769480 | tf_op jit(solution)/shard_map/ppermute | solution.py:30
  55.3 1.8 %copy-start.2 = (s32[128]{0:T(128)S(1)}, s32[128]{0:T(128)}, u32[]{:S(2)}) copy-start(s32[128]{0:T(128)} %param.9) | copy-start | bytes 1540
  59.9 20.2 %all-to-all-start.1 = ((f16[16,96,128]{2,1,0:T(8,128)(2,1)}), f16[16,96,128]{2,1,0:T(8,128)(2,1)S(1)}, u32[]{:S(2)}, u32[]{:S(2)}) async-start(f16[16,96,128]{2,1,0:T(8,128)(2,1)} %bitcast.33), calls=%async_computation.1 | async-start | bytes 786432 | tf_op jit(solution)/shard_map/all_to_all | solution.py:22
  81.7 19.2 %all-to-all-start.2 = ((bf16[16,96,128]{2,1,0:T(8,128)(2,1)}), bf16[16,96,128]{2,1,0:T(8,128)(2,1)S(1)}, u32[]{:S(2)}, u32[]{:S(2)}) async-start(bf16[16,96,128]{2,1,0:T(8,128)(2,1)} %broadcast_in_dim.25), calls=%async_computation.2 | async-start | bytes 786432 | tf_op jit(solution)/shard_map/all_to_all | solution.py:22
  85.9 17.3 %collective-permute-start.7 = (f16[768,384]{1,0:T(8,128)(2,1)S(1)}, f16[768,384]{1,0:T(8,128)(2,1)}, u32[]{:S(2)}, u32[]{:S(2)}) collective-permute-start(f16[768,384]{1,0:T(8,128)(2,1)S(1)} %fusion), channel_id=1, source_target_pairs={{0,16},{16,0},{1,17},{17,1},{2,18},{18,2},{3,19},{19,3},{4,20},{20... | collective-permute-start | bytes 1769480 | tf_op jit(solution)/shard_map/ppermute | solution.py:30
  101.2 5.9 %collective-permute-start.13 = (f16[24,32,320]{2,1,0:T(8,128)(2,1)S(1)}, f16[24,32,320]{2,1,0:T(8,128)(2,1)S(1)}, u32[]{:S(2)}, u32[]{:S(2)}) collective-permute-start(f16[24,32,320]{2,1,0:T(8,128)(2,1)S(1)} %fusion.1), channel_id=1, source_target_pairs={{0,16},{16,0},{1,17},{17,1},{2,18},{18,2},{3,19},{19,3},{4,20},{20... | collective-permute-start | bytes 1474568 | tf_op jit(solution)/shard_map/ppermute | solution.py:30
  105.1 14.7 %collective-permute-start.8 = (f16[3,2,2,32,384]{4,3,1,2,0:T(8,128)(2,1)S(1)}, f16[3,2,2,32,384]{4,3,1,2,0:T(8,128)(2,1)S(1)}, u32[]{:S(2)}, u32[]{:S(2)}) collective-permute-start(f16[3,2,2,32,384]{4,3,1,2,0:T(8,128)(2,1)S(1)} %fusion.13), channel_id=1, source_target_pairs={{0,384},{384,0},{1,385},{385,1},{2,386},{386,2},{3,387},{387,3},{4... | collective-permute-start | bytes 884744 | tf_op jit(solution)/shard_map/ppermute | solution.py:102
  108.3 57.2 %all-to-all-start.3 = ((f16[24,32,320]{2,1,0:T(8,128)(2,1)}), f16[24,32,320]{2,1,0:T(8,128)(2,1)S(1)}, u32[]{:S(2)}, u32[]{:S(2)}) async-start(f16[24,32,320]{2,1,0:T(8,128)(2,1)} %multiply_convert_fusion), calls=%async_computation.3 | async-start | bytes 1179648 | tf_op jit(solution)/shard_map/all_to_all | solution.py:22
  120.0 32.2 %collective-permute-start.10 = (f16[2,2,32,384]{3,2,0,1:T(8,128)(2,1)S(1)}, f16[2,2,32,384]{3,2,0,1:T(8,128)(2,1)S(1)}, u32[]{:S(2)}, u32[]{:S(2)}) collective-permute-start(f16[2,2,32,384]{3,2,0,1:T(8,128)(2,1)S(1)} %get-tuple-element.6), channel_id=1, source_target_pairs={{0,256},{32,288},{64,320},{96,352},{128,0},{160,32},{192,64},{224,... | collective-permute-start | bytes 294920 | tf_op jit(solution)/shard_map/ppermute | solution.py:35
  127.3 24.9 %collective-permute-start.9 = (f16[2,2,32,384]{3,2,0,1:T(8,128)(2,1)S(1)}, f16[2,2,32,384]{3,2,0,1:T(8,128)(2,1)S(1)}, u32[]{:S(2)}, u32[]{:S(2)}) collective-permute-start(f16[2,2,32,384]{3,2,0,1:T(8,128)(2,1)S(1)} %get-tuple-element.5), channel_id=1, source_target_pairs={{0,128},{32,160},{64,192},{96,224},{128,256},{160,288},{192,320},{... | collective-permute-start | bytes 294920 | tf_op jit(solution)/shard_map/ppermute | solution.py:35
  152.2 6.0 %collective-permute-start.11 = (f16[2,32,384]{2,1,0:T(8,128)(2,1)S(1)}, f16[2,32,384]{2,1,0:T(8,128)(2,1)S(1)}, u32[]{:S(2)}, u32[]{:S(2)}) collective-permute-start(f16[2,32,384]{2,1,0:T(8,128)(2,1)S(1)} %fusion.25), channel_id=1, source_target_pairs={{0,32},{32,0},{64,96},{96,64},{128,160},{160,128},{192,224},{224,1... | collective-permute-start | bytes 147464 | tf_op jit(solution)/shard_map/ppermute | solution.py:102
  158.3 6.6 %collective-permute-start.12 = (f16[32,384]{1,0:T(8,128)(2,1)S(1)}, f16[32,384]{1,0:T(8,128)(2,1)S(1)}, u32[]{:S(2)}, u32[]{:S(2)}) collective-permute-start(f16[32,384]{1,0:T(8,128)(2,1)S(1)} %fusion.29), channel_id=1, source_target_pairs={{0,64},{32,96},{64,0},{96,32},{128,192},{160,224},{192,128},{224,1... | collective-permute-start | bytes 73736 | tf_op jit(solution)/shard_map/ppermute | solution.py:102

commit v3 on v2

--- a/solution.py
+++ b/solution.py
@@ -62,12 +62,12 @@
 
     text_tile = (text_emb.T * EMB_UP).astype(HALF)
     image_tile = (image_emb.T * EMB_UP).astype(HALF)
+    across = shifted(image_tile, "yh", 2)
     own = to_all(text_tile, CHIPS)
     other = swap(own).reshape(768, -1).astype(F32)
     own = own.reshape(768, -1).astype(F32)
-    near = jnp.stack([image_tile] + [shifted(image_tile, "yh", k) for k in (1, 2, 3)])
-    far = [near] + [shifted(near, "x", k) for k in (1, 3)]
-    far.insert(2, shifted(near, "x", 2))
+    near = jnp.stack((image_tile, shifted(image_tile, "yh", 1), across, shifted(image_tile, "yh", 3)))
+    far = [near] + [shifted(near, "x", k) for k in (1, 2, 3)]
     by_x = in_order(far, lax.axis_index("x"))
     image_full = in_order([by_x[:, k] for k in range(4)], lax.axis_index("yh"))
     image_full = jnp.moveaxis(image_full, 0, 1).astype(F32)
@@ -122,8 +122,12 @@
     got = swap((weights(1 - core) * PROJ_UP[0]).astype(HALF))
     mine = weights(core)
     sent = ((mine + got.astype(F32) * (1.0 / PROJ_UP[0])) * PROJ_UP[1]).astype(HALF)
+    end = jnp.concatenate((sent[:, :16, 256:], sent[:, 16:, 256:]), axis=2)
+    sent = jnp.concatenate((sent[:, :, :128], sent[:, :, 128:256], end), axis=1)
     got = exchange(sent, CHIPS)
-    grad_proj = got.astype(F32).sum(axis=0) * (1.0 / PROJ_UP[1])
+    total = got.astype(F32).sum(axis=0) * (1.0 / PROJ_UP[1])
+    end = jnp.concatenate((total[64:, :64], total[64:, 64:]), axis=0)
+    grad_proj = jnp.concatenate((total[:32], total[32:64], end), axis=1)
     return (grad_image.T, grad_text.T, grad_proj.T)
 
 

time: 167 us -> 163 us (0.976)
  waiting for transfers between devices: 65.6 us -> 62.1 us
  matrix products: 6.44 us -> 4.52 us
    ppermute x8, waiting for transfers between devices: 30.3 us -> 27 us  [shifted(): lax.ppermute(array, axis, tuple(((i, (i + step) % length) for i in range(...]
  transfers between devices with their start and end apart: 18 -> 18, of which waited for: 10 -> 10; matrix products, arithmetic and copies ran while one was open for 4% -> 3% of each run, Pallas kernels for 0% -> 0%
where the time goes in v3:
time: 163 us; the launch traced here: 162 us
  starting transfers between devices  85.3 us (52%)
  waiting for transfers between devices  62.1 us (38%)
  other arithmetic  5.75 us (4%)
  matrix products  4.52 us (3%)
  between operations  2.52 us (2%)
  local copies, waits for them, and re-layouts  2.08 us (1%)
    all_to_all x4, starting transfers between devices, exchange(): return lax.all_to_all(tiles, axis, split_axis=0, concat_axis=0, tiled=True)  36.2 us
    ppermute x8, starting transfers between devices, shifted(): lax.ppermute(array, axis, tuple(((i, (i + step) % length) for i in range(...  34.1 us
    all_to_all x4, waiting for transfers between devices, exchange(): return lax.all_to_all(tiles, axis, split_axis=0, concat_axis=0, tiled=True)  28.8 us
    ppermute x8, waiting for transfers between devices, shifted(): lax.ppermute(array, axis, tuple(((i, (i + step) % length) for i in range(...  27 us
    ppermute x3, starting transfers between devices, halve(): got = lax.ppermute((theirs * TEXT_UP[k]).astype(HALF), axis, pairs)  9.19 us
    ppermute x3, starting transfers between devices, swap(): return lax.ppermute(array, 'core', ((0, 1), (1, 0)))  5.76 us
    ppermute x3, waiting for transfers between devices, halve(): got = lax.ppermute((theirs * TEXT_UP[k]).astype(HALF), axis, pairs)  5.33 us
    dot_general x6, matrix products, dot(): lax.dot_general(a, b, (((ca,), (cb,)), ((), ())), precision=HIGH, preferr...  3.87 us
  transfers between devices with their start and end apart: 18, of which 10 were waited for; matrix products, arithmetic and copies ran while one was open for 3% of the time, Pallas kernels for 0%

profile of v3, /device:TPU:8, one launch (start us, length us, event | category | flops | bytes accessed | tf_op | source)
XLA Modules:
  0.0 162.3 jit_solution(14737668590475359638)
XLA Ops:
  0.7 0.9 fusion.28
  1.5 0.9 broadcast_in_dim.12
  2.4 16.7 %all-to-all-start = ((f16[24,32,384]{2,1,0:T(8,128)(2,1)}), f16[24,32,384]{2,1,0:T(8,128)(2,1)S(1)}, u32[]{:S(2)}, u32[]{:S(2)}) async-start(f16[24,32,384]{2,1,0:T(8,128)(2,1)} %broadcast_in_dim.12), calls=%async_computation | async-start | bytes 1179648 | tf_op jit(solution)/shard_map/all_to_all | solution.py:22
  19.1 5.3 %collective-permute-start.2 = (f16[96,128]{1,0:T(8,128)(2,1)S(1)}, f16[96,128]{1,0:T(8,128)(2,1)S(1)}, u32[]{:S(2)}, u32[]{:S(2)}) collective-permute-start(f16[96,128]{1,0:T(8,128)(2,1)S(1)} %get-tuple-element.25), channel_id=1, source_target_pairs={{0,3},{1,0},{2,1},{3,2},{4,7},{5,4},{6,5},{7,6},{8,11},{9,8},{10,9... | collective-permute-start | bytes 73736 | tf_op jit(solution)/shard_map/ppermute | solution.py:35
  24.3 4.7 %collective-permute-start.1 = (f16[96,128]{1,0:T(8,128)(2,1)S(1)}, f16[96,128]{1,0:T(8,128)(2,1)S(1)}, u32[]{:S(2)}, u32[]{:S(2)}) collective-permute-start(f16[96,128]{1,0:T(8,128)(2,1)S(1)} %get-tuple-element.25), channel_id=1, source_target_pairs={{0,2},{1,3},{2,0},{3,1},{4,6},{5,7},{6,4},{7,5},{8,10},{9,11},{10,... | collective-permute-start | bytes 73736 | tf_op jit(solution)/shard_map/ppermute | solution.py:35
  29.1 3.6 %collective-permute-start = (f16[96,128]{1,0:T(8,128)(2,1)S(1)}, f16[96,128]{1,0:T(8,128)(2,1)S(1)}, u32[]{:S(2)}, u32[]{:S(2)}) collective-permute-start(f16[96,128]{1,0:T(8,128)(2,1)S(1)} %get-tuple-element.25), channel_id=1, source_target_pairs={{0,1},{1,2},{2,3},{3,0},{4,5},{5,6},{6,7},{7,4},{8,9},{9,10},{10,1... | collective-permute-start | bytes 73736 | tf_op jit(solution)/shard_map/ppermute | solution.py:35
  34.1 2.9 %collective-permute-done = f16[96,128]{1,0:T(8,128)(2,1)S(1)} collective-permute-done((f16[96,128]{1,0:T(8,128)(2,1)S(1)}, f16[96,128]{1,0:T(8,128)(2,1)S(1)}, u32[]{:S(2)}, u32[]{:S(2)}) %collective-permute-start) | collective-permute-done | bytes 24608 | tf_op jit(solution)/shard_map/ppermute | solution.py:35
  37.0 4.9 %collective-permute-start.4 = (f16[4,96,128]{2,1,0:T(8,128)(2,1)S(1)}, f16[4,96,128]{2,1,0:T(8,128)(2,1)S(1)}, u32[]{:S(2)}, u32[]{:S(2)}) collective-permute-start(f16[4,96,128]{2,1,0:T(8,128)(2,1)S(1)} %pad_maximum_fusion.3), channel_id=1, source_target_pairs={{0,8},{4,12},{8,0},{12,4},{1,9},{5,13},{9,1},{13,5},{2,10},{6,14},... | collective-permute-start | bytes 294920 | tf_op jit(solution)/shard_map/ppermute | solution.py:35
  42.0 3.0 %collective-permute-start.5 = (f16[4,96,128]{2,1,0:T(8,128)(2,1)S(1)}, f16[4,96,128]{2,1,0:T(8,128)(2,1)S(1)}, u32[]{:S(2)}, u32[]{:S(2)}) collective-permute-start(f16[4,96,128]{2,1,0:T(8,128)(2,1)S(1)} %pad_maximum_fusion.3), channel_id=1, source_target_pairs={{0,12},{4,0},{8,4},{12,8},{1,13},{5,1},{9,5},{13,9},{2,14},{6,2},{... | collective-permute-start | bytes 294920 | tf_op jit(solution)/shard_map/ppermute | solution.py:35
  45.0 2.8 %collective-permute-start.3 = (f16[4,96,128]{2,1,0:T(8,128)(2,1)S(1)}, f16[4,96,128]{2,1,0:T(8,128)(2,1)S(1)}, u32[]{:S(2)}, u32[]{:S(2)}) collective-permute-start(f16[4,96,128]{2,1,0:T(8,128)(2,1)S(1)} %pad_maximum_fusion.3), channel_id=1, source_target_pairs={{0,4},{4,8},{8,12},{12,0},{1,5},{5,9},{9,13},{13,1},{2,6},{6,10},{... | collective-permute-start | bytes 294920 | tf_op jit(solution)/shard_map/ppermute | solution.py:35
  48.5 4.3 %collective-permute-done.3 = f16[4,96,128]{2,1,0:T(8,128)(2,1)S(1)} collective-permute-done((f16[4,96,128]{2,1,0:T(8,128)(2,1)S(1)}, f16[4,96,128]{2,1,0:T(8,128)(2,1)S(1)}, u32[]{:S(2)}, u32[]{:S(2)}) %collective-permute-start.3) | collective-permute-done | bytes 98336 | tf_op jit(solution)/shard_map/ppermute | solution.py:35
  53.1 1.9 %collective-permute-start.6 = (f16[24,32,384]{2,1,0:T(8,128)(2,1)S(1)}, f16[24,32,384]{2,1,0:T(8,128)(2,1)S(1)}, u32[]{:S(2)}, u32[]{:S(2)}) collective-permute-start(f16[24,32,384]{2,1,0:T(8,128)(2,1)S(1)} %all-to-all-done), channel_id=1, source_target_pairs={{0,16},{16,0},{1,17},{17,1},{2,18},{18,2},{3,19},{19,3},{4,20},{20... | collective-permute-start | bytes 1769480 | tf_op jit(solution)/shard_map/ppermute | solution.py:30
  56.1 0.9 collective-permute-done.6
  59.0 0.9 pad_maximum_fusion.2
  59.9 4.5 %all-to-all-start.1 = ((f16[16,96,128]{2,1,0:T(8,128)(2,1)}), f16[16,96,128]{2,1,0:T(8,128)(2,1)S(1)}, u32[]{:S(2)}, u32[]{:S(2)}) async-start(f16[16,96,128]{2,1,0:T(8,128)(2,1)} %bitcast.33), calls=%async_computation.1 | async-start | bytes 786432 | tf_op jit(solution)/shard_map/all_to_all | solution.py:22
  64.4 15.7 %all-to-all-done.1 = f16[16,96,128]{2,1,0:T(8,128)(2,1)S(1)} async-done(((f16[16,96,128]{2,1,0:T(8,128)(2,1)}), f16[16,96,128]{2,1,0:T(8,128)(2,1)S(1)}, u32[]{:S(2)}, u32[]{:S(2)}) %all-to-all-start.1) | async-done | bytes 393248 | tf_op jit(solution)/shard_map/all_to_all | solution.py:22
  80.8 0.8 broadcast_in_dim.25
  81.6 3.6 %all-to-all-start.2 = ((bf16[16,96,128]{2,1,0:T(8,128)(2,1)}), bf16[16,96,128]{2,1,0:T(8,128)(2,1)S(1)}, u32[]{:S(2)}, u32[]{:S(2)}) async-start(bf16[16,96,128]{2,1,0:T(8,128)(2,1)} %broadcast_in_dim.25), calls=%async_computation.2 | async-start | bytes 786432 | tf_op jit(solution)/shard_map/all_to_all | solution.py:22
  85.8 1.9 %collective-permute-start.7 = (f16[768,384]{1,0:T(8,128)(2,1)S(1)}, f16[768,384]{1,0:T(8,128)(2,1)S(1)}, u32[]{:S(2)}, u32[]{:S(2)}) collective-permute-start(f16[768,384]{1,0:T(8,128)(2,1)S(1)} %fusion), channel_id=1, source_target_pairs={{0,16},{16,0},{1,17},{17,1},{2,18},{18,2},{3,19},{19,3},{4,20},{20... | collective-permute-start | bytes 1769480 | tf_op jit(solution)/shard_map/ppermute | solution.py:30
  87.8 13.1 %all-to-all-done.2 = bf16[16,96,128]{2,1,0:T(8,128)(2,1)S(1)} async-done(((bf16[16,96,128]{2,1,0:T(8,128)(2,1)}), bf16[16,96,128]{2,1,0:T(8,128)(2,1)S(1)}, u32[]{:S(2)}, u32[]{:S(2)}) %all-to-all-start.2) | async-done | bytes 393248 | tf_op jit(solution)/shard_map/all_to_all | solution.py:22
  101.2 1.9 %collective-permute-start.13 = (f16[24,32,320]{2,1,0:T(8,128)(2,1)S(1)}, f16[24,32,320]{2,1,0:T(8,128)(2,1)S(1)}, u32[]{:S(2)}, u32[]{:S(2)}) collective-permute-start(f16[24,32,320]{2,1,0:T(8,128)(2,1)S(1)} %fusion.1), channel_id=1, source_target_pairs={{0,16},{16,0},{1,17},{17,1},{2,18},{18,2},{3,19},{19,3},{4,20},{20... | collective-permute-start | bytes 1474568 | tf_op jit(solution)/shard_map/ppermute | solution.py:30
  103.1 0.7 multiply_add_fusion
  104.0 1.9 %collective-permute-start.8 = (f16[3,2,2,32,384]{4,3,1,2,0:T(8,128)(2,1)S(1)}, f16[3,2,2,32,384]{4,3,1,2,0:T(8,128)(2,1)S(1)}, u32[]{:S(2)}, u32[]{:S(2)}) collective-permute-start(f16[3,2,2,32,384]{4,3,1,2,0:T(8,128)(2,1)S(1)} %fusion.13), channel_id=1, source_target_pairs={{0,384},{384,0},{1,385},{385,1},{2,386},{386,2},{3,387},{387,3},{4... | collective-permute-start | bytes 884744 | tf_op jit(solution)/shard_map/ppermute | solution.py:102
  106.4 1.0 maximum_maximum_fusion
  107.4 11.5 %all-to-all-start.3 = ((f16[24,80,128]{2,1,0:T(8,128)(2,1)}), f16[24,80,128]{2,1,0:T(8,128)(2,1)S(1)}, u32[]{:S(2)}, u32[]{:S(2)}) async-start(f16[24,80,128]{2,1,0:T(8,128)(2,1)} %maximum_maximum_fusion), calls=%async_computation.3 | async-start | bytes 983040 | tf_op jit(solution)/shard_map/all_to_all | solution.py:22
  119.1 7.3 %collective-permute-start.10 = (f16[2,2,32,384]{3,2,0,1:T(8,128)(2,1)S(1)}, f16[2,2,32,384]{3,2,0,1:T(8,128)(2,1)S(1)}, u32[]{:S(2)}, u32[]{:S(2)}) collective-permute-start(f16[2,2,32,384]{3,2,0,1:T(8,128)(2,1)S(1)} %get-tuple-element.10), channel_id=1, source_target_pairs={{0,256},{32,288},{64,320},{96,352},{128,0},{160,32},{192,64},{224,... | collective-permute-start | bytes 294920 | tf_op jit(solution)/shard_map/ppermute | solution.py:35
  126.4 2.5 %collective-permute-start.9 = (f16[2,2,32,384]{3,2,0,1:T(8,128)(2,1)S(1)}, f16[2,2,32,384]{3,2,0,1:T(8,128)(2,1)S(1)}, u32[]{:S(2)}, u32[]{:S(2)}) collective-permute-start(f16[2,2,32,384]{3,2,0,1:T(8,128)(2,1)S(1)} %get-tuple-element.9), channel_id=1, source_target_pairs={{0,128},{32,160},{64,192},{96,224},{128,256},{160,288},{192,320},{... | collective-permute-start | bytes 294920 | tf_op jit(solution)/shard_map/ppermute | solution.py:35
  128.9 19.2 %collective-permute-done.10 = f16[2,2,32,384]{3,2,0,1:T(8,128)(2,1)S(1)} collective-permute-done((f16[2,2,32,384]{3,2,0,1:T(8,128)(2,1)S(1)}, f16[2,2,32,384]{3,2,0,1:T(8,128)(2,1)S(1)}, u32[]{:S(2)}, u32[]{:S(2)}) %collective-permute-start.10) | collective-permute-done | bytes 98336 | tf_op jit(solution)/shard_map/ppermute | solution.py:35
  148.1 2.4 %collective-permute-start.11 = (f16[2,32,384]{2,1,0:T(8,128)(2,1)S(1)}, f16[2,32,384]{2,1,0:T(8,128)(2,1)S(1)}, u32[]{:S(2)}, u32[]{:S(2)}) collective-permute-start(f16[2,32,384]{2,1,0:T(8,128)(2,1)S(1)} %fusion.25), channel_id=1, source_target_pairs={{0,32},{32,0},{64,96},{96,64},{128,160},{160,128},{192,224},{224,1... | collective-permute-start | bytes 147464 | tf_op jit(solution)/shard_map/ppermute | solution.py:102
  150.6 3.5 %collective-permute-done.11 = f16[2,32,384]{2,1,0:T(8,128)(2,1)S(1)} collective-permute-done((f16[2,32,384]{2,1,0:T(8,128)(2,1)S(1)}, f16[2,32,384]{2,1,0:T(8,128)(2,1)S(1)}, u32[]{:S(2)}, u32[]{:S(2)}) %collective-permute-start.11) | collective-permute-done | bytes 49184 | tf_op jit(solution)/shard_map/ppermute | solution.py:102
  154.2 4.9 %collective-permute-start.12 = (f16[32,384]{1,0:T(8,128)(2,1)S(1)}, f16[32,384]{1,0:T(8,128)(2,1)S(1)}, u32[]{:S(2)}, u32[]{:S(2)}) collective-permute-start(f16[32,384]{1,0:T(8,128)(2,1)S(1)} %fusion.29), channel_id=1, source_target_pairs={{0,64},{32,96},{64,0},{96,32},{128,192},{160,224},{192,128},{224,1... | collective-permute-start | bytes 73736 | tf_op jit(solution)/shard_map/ppermute | solution.py:102
  159.1 1.8 %collective-permute-done.12 = f16[32,384]{1,0:T(8,128)(2,1)S(1)} collective-permute-done((f16[32,384]{1,0:T(8,128)(2,1)S(1)}, f16[32,384]{1,0:T(8,128)(2,1)S(1)}, u32[]{:S(2)}, u32[]{:S(2)}) %collective-permute-start.12) | collective-permute-done | bytes 24608 | tf_op jit(solution)/shard_map/ppermute | solution.py:102
  (50 shorter events, 8.0 us)
Async XLA Ops:
  0.6 100.3 %copy-start = (bf16[128,320]{0,1:T(8,128)(2,1)S(1)}, bf16[128,320]{0,1:T(8,128)(2,1)}, u32[]{:S(2)}) copy-start(bf16[128,320]{0,1:T(8,128)(2,1)} %param.8) | copy-start | bytes 245764
  0.6 18.4 %copy-start.1 = (f32[128,96]{0,1:T(8,128)S(1)}, f32[128,96]{0,1:T(8,128)}, u32[]{:S(2)}) copy-start(f32[128,96]{0,1:T(8,128)} %param.6) | copy-start | bytes 147460
  2.4 50.8 %all-to-all-start = ((f16[24,32,384]{2,1,0:T(8,128)(2,1)}), f16[24,32,384]{2,1,0:T(8,128)(2,1)S(1)}, u32[]{:S(2)}, u32[]{:S(2)}) async-start(f16[24,32,384]{2,1,0:T(8,128)(2,1)} %broadcast_in_dim.12), calls=%async_computation | async-start | bytes 1179648 | tf_op jit(solution)/shard_map/all_to_all | solution.py:22
  19.1 14.9 %collective-permute-start.2 = (f16[96,128]{1,0:T(8,128)(2,1)S(1)}, f16[96,128]{1,0:T(8,128)(2,1)S(1)}, u32[]{:S(2)}, u32[]{:S(2)}) collective-permute-start(f16[96,128]{1,0:T(8,128)(2,1)S(1)} %get-tuple-element.25), channel_id=1, source_target_pairs={{0,3},{1,0},{2,1},{3,2},{4,7},{5,4},{6,5},{7,6},{8,11},{9,8},{10,9... | collective-permute-start | bytes 73736 | tf_op jit(solution)/shard_map/ppermute | solution.py:35
  24.3 9.8 %collective-permute-start.1 = (f16[96,128]{1,0:T(8,128)(2,1)S(1)}, f16[96,128]{1,0:T(8,128)(2,1)S(1)}, u32[]{:S(2)}, u32[]{:S(2)}) collective-permute-start(f16[96,128]{1,0:T(8,128)(2,1)S(1)} %get-tuple-element.25), channel_id=1, source_target_pairs={{0,2},{1,3},{2,0},{3,1},{4,6},{5,7},{6,4},{7,5},{8,10},{9,11},{10,... | collective-permute-start | bytes 73736 | tf_op jit(solution)/shard_map/ppermute | solution.py:35
  29.1 7.9 %collective-permute-start = (f16[96,128]{1,0:T(8,128)(2,1)S(1)}, f16[96,128]{1,0:T(8,128)(2,1)S(1)}, u32[]{:S(2)}, u32[]{:S(2)}) collective-permute-start(f16[96,128]{1,0:T(8,128)(2,1)S(1)} %get-tuple-element.25), channel_id=1, source_target_pairs={{0,1},{1,2},{2,3},{3,0},{4,5},{5,6},{6,7},{7,4},{8,9},{9,10},{10,1... | collective-permute-start | bytes 73736 | tf_op jit(solution)/shard_map/ppermute | solution.py:35
  37.0 10.8 %collective-permute-start.4 = (f16[4,96,128]{2,1,0:T(8,128)(2,1)S(1)}, f16[4,96,128]{2,1,0:T(8,128)(2,1)S(1)}, u32[]{:S(2)}, u32[]{:S(2)}) collective-permute-start(f16[4,96,128]{2,1,0:T(8,128)(2,1)S(1)} %pad_maximum_fusion.3), channel_id=1, source_target_pairs={{0,8},{4,12},{8,0},{12,4},{1,9},{5,13},{9,1},{13,5},{2,10},{6,14},... | collective-permute-start | bytes 294920 | tf_op jit(solution)/shard_map/ppermute | solution.py:35
  42.0 6.5 %collective-permute-start.5 = (f16[4,96,128]{2,1,0:T(8,128)(2,1)S(1)}, f16[4,96,128]{2,1,0:T(8,128)(2,1)S(1)}, u32[]{:S(2)}, u32[]{:S(2)}) collective-permute-start(f16[4,96,128]{2,1,0:T(8,128)(2,1)S(1)} %pad_maximum_fusion.3), channel_id=1, source_target_pairs={{0,12},{4,0},{8,4},{12,8},{1,13},{5,1},{9,5},{13,9},{2,14},{6,2},{... | collective-permute-start | bytes 294920 | tf_op jit(solution)/shard_map/ppermute | solution.py:35
  45.0 7.7 %collective-permute-start.3 = (f16[4,96,128]{2,1,0:T(8,128)(2,1)S(1)}, f16[4,96,128]{2,1,0:T(8,128)(2,1)S(1)}, u32[]{:S(2)}, u32[]{:S(2)}) collective-permute-start(f16[4,96,128]{2,1,0:T(8,128)(2,1)S(1)} %pad_maximum_fusion.3), channel_id=1, source_target_pairs={{0,4},{4,8},{8,12},{12,0},{1,5},{5,9},{9,13},{13,1},{2,6},{6,10},{... | collective-permute-start | bytes 294920 | tf_op jit(solution)/shard_map/ppermute | solution.py:35
  53.1 3.9 %collective-permute-start.6 = (f16[24,32,384]{2,1,0:T(8,128)(2,1)S(1)}, f16[24,32,384]{2,1,0:T(8,128)(2,1)S(1)}, u32[]{:S(2)}, u32[]{:S(2)}) collective-permute-start(f16[24,32,384]{2,1,0:T(8,128)(2,1)S(1)} %all-to-all-done), channel_id=1, source_target_pairs={{0,16},{16,0},{1,17},{17,1},{2,18},{18,2},{3,19},{19,3},{4,20},{20... | collective-permute-start | bytes 1769480 | tf_op jit(solution)/shard_map/ppermute | solution.py:30
  55.2 1.8 %copy-start.2 = (s32[128]{0:T(128)S(1)}, s32[128]{0:T(128)}, u32[]{:S(2)}) copy-start(s32[128]{0:T(128)} %param.9) | copy-start | bytes 1540
  59.9 20.2 %all-to-all-start.1 = ((f16[16,96,128]{2,1,0:T(8,128)(2,1)}), f16[16,96,128]{2,1,0:T(8,128)(2,1)S(1)}, u32[]{:S(2)}, u32[]{:S(2)}) async-start(f16[16,96,128]{2,1,0:T(8,128)(2,1)} %bitcast.33), calls=%async_computation.1 | async-start | bytes 786432 | tf_op jit(solution)/shard_map/all_to_all | solution.py:22
  81.6 19.2 %all-to-all-start.2 = ((bf16[16,96,128]{2,1,0:T(8,128)(2,1)}), bf16[16,96,128]{2,1,0:T(8,128)(2,1)S(1)}, u32[]{:S(2)}, u32[]{:S(2)}) async-start(bf16[16,96,128]{2,1,0:T(8,128)(2,1)} %broadcast_in_dim.25), calls=%async_computation.2 | async-start | bytes 786432 | tf_op jit(solution)/shard_map/all_to_all | solution.py:22
  85.8 17.3 %collective-permute-start.7 = (f16[768,384]{1,0:T(8,128)(2,1)S(1)}, f16[768,384]{1,0:T(8,128)(2,1)S(1)}, u32[]{:S(2)}, u32[]{:S(2)}) collective-permute-start(f16[768,384]{1,0:T(8,128)(2,1)S(1)} %fusion), channel_id=1, source_target_pairs={{0,16},{16,0},{1,17},{17,1},{2,18},{18,2},{3,19},{19,3},{4,20},{20... | collective-permute-start | bytes 1769480 | tf_op jit(solution)/shard_map/ppermute | solution.py:30
  101.2 4.7 %collective-permute-start.13 = (f16[24,32,320]{2,1,0:T(8,128)(2,1)S(1)}, f16[24,32,320]{2,1,0:T(8,128)(2,1)S(1)}, u32[]{:S(2)}, u32[]{:S(2)}) collective-permute-start(f16[24,32,320]{2,1,0:T(8,128)(2,1)S(1)} %fusion.1), channel_id=1, source_target_pairs={{0,16},{16,0},{1,17},{17,1},{2,18},{18,2},{3,19},{19,3},{4,20},{20... | collective-permute-start | bytes 1474568 | tf_op jit(solution)/shard_map/ppermute | solution.py:30
  104.0 15.0 %collective-permute-start.8 = (f16[3,2,2,32,384]{4,3,1,2,0:T(8,128)(2,1)S(1)}, f16[3,2,2,32,384]{4,3,1,2,0:T(8,128)(2,1)S(1)}, u32[]{:S(2)}, u32[]{:S(2)}) collective-permute-start(f16[3,2,2,32,384]{4,3,1,2,0:T(8,128)(2,1)S(1)} %fusion.13), channel_id=1, source_target_pairs={{0,384},{384,0},{1,385},{385,1},{2,386},{386,2},{3,387},{387,3},{4... | collective-permute-start | bytes 884744 | tf_op jit(solution)/shard_map/ppermute | solution.py:102
  107.4 54.0 %all-to-all-start.3 = ((f16[24,80,128]{2,1,0:T(8,128)(2,1)}), f16[24,80,128]{2,1,0:T(8,128)(2,1)S(1)}, u32[]{:S(2)}, u32[]{:S(2)}) async-start(f16[24,80,128]{2,1,0:T(8,128)(2,1)} %maximum_maximum_fusion), calls=%async_computation.3 | async-start | bytes 983040 | tf_op jit(solution)/shard_map/all_to_all | solution.py:22
  119.1 28.9 %collective-permute-start.10 = (f16[2,2,32,384]{3,2,0,1:T(8,128)(2,1)S(1)}, f16[2,2,32,384]{3,2,0,1:T(8,128)(2,1)S(1)}, u32[]{:S(2)}, u32[]{:S(2)}) collective-permute-start(f16[2,2,32,384]{3,2,0,1:T(8,128)(2,1)S(1)} %get-tuple-element.10), channel_id=1, source_target_pairs={{0,256},{32,288},{64,320},{96,352},{128,0},{160,32},{192,64},{224,... | collective-permute-start | bytes 294920 | tf_op jit(solution)/shard_map/ppermute | solution.py:35
  126.4 21.6 %collective-permute-start.9 = (f16[2,2,32,384]{3,2,0,1:T(8,128)(2,1)S(1)}, f16[2,2,32,384]{3,2,0,1:T(8,128)(2,1)S(1)}, u32[]{:S(2)}, u32[]{:S(2)}) collective-permute-start(f16[2,2,32,384]{3,2,0,1:T(8,128)(2,1)S(1)} %get-tuple-element.9), channel_id=1, source_target_pairs={{0,128},{32,160},{64,192},{96,224},{128,256},{160,288},{192,320},{... | collective-permute-start | bytes 294920 | tf_op jit(solution)/shard_map/ppermute | solution.py:35
  148.1 6.0 %collective-permute-start.11 = (f16[2,32,384]{2,1,0:T(8,128)(2,1)S(1)}, f16[2,32,384]{2,1,0:T(8,128)(2,1)S(1)}, u32[]{:S(2)}, u32[]{:S(2)}) collective-permute-start(f16[2,32,384]{2,1,0:T(8,128)(2,1)S(1)} %fusion.25), channel_id=1, source_target_pairs={{0,32},{32,0},{64,96},{96,64},{128,160},{160,128},{192,224},{224,1... | collective-permute-start | bytes 147464 | tf_op jit(solution)/shard_map/ppermute | solution.py:102
  154.2 6.7 %collective-permute-start.12 = (f16[32,384]{1,0:T(8,128)(2,1)S(1)}, f16[32,384]{1,0:T(8,128)(2,1)S(1)}, u32[]{:S(2)}, u32[]{:S(2)}) collective-permute-start(f16[32,384]{1,0:T(8,128)(2,1)S(1)} %fusion.29), channel_id=1, source_target_pairs={{0,64},{32,96},{64,0},{96,32},{128,192},{160,224},{192,128},{224,1... | collective-permute-start | bytes 73736 | tf_op jit(solution)/shard_map/ppermute | solution.py:102

commit v4 on v3

--- a/solution.py
+++ b/solution.py
@@ -14,7 +14,7 @@
 
 EMB_UP = 2.0**18
 IMAGE_UP = 2.0**10
-TEXT_UP = (2.0**11, 2.0**10, 2.0**9, 2.0**7, 2.0**6)
+TEXT_UP = (2.0**11, 2.0**10, 2.0**9, 2.0**8, 2.0**7)
 PROJ_UP = (2.0**-2, 2.0**-3)
 
 
@@ -62,11 +62,10 @@
 
     text_tile = (text_emb.T * EMB_UP).astype(HALF)
     image_tile = (image_emb.T * EMB_UP).astype(HALF)
-    across = shifted(image_tile, "yh", 2)
     own = to_all(text_tile, CHIPS)
     other = swap(own).reshape(768, -1).astype(F32)
     own = own.reshape(768, -1).astype(F32)
-    near = jnp.stack((image_tile, shifted(image_tile, "yh", 1), across, shifted(image_tile, "yh", 3)))
+    near = jnp.stack([image_tile] + [shifted(image_tile, "yh", k) for k in (1, 2, 3)])
     far = [near] + [shifted(near, "x", k) for k in (1, 2, 3)]
     by_x = in_order(far, lax.axis_index("x"))
     image_full = in_order([by_x[:, k] for k in range(4)], lax.axis_index("yh"))
@@ -104,15 +103,15 @@
         return mine + got.astype(F32) * (1.0 / TEXT_UP[k])
 
     tiles = halve(tiles, 1, "yl", yl, 0, ((0, 1), (1, 0)))
+    tiles = halve(tiles, 2, "z", z % 2, 2, tuple((i, i ^ 1) for i in range(12)))
+    tiles = halve(tiles, 3, "z", (z // 2) % 2, 1, tuple((i, i ^ 2) for i in range(12)))
     block = z // 4
     came = []
     for step in (1, 2):
         theirs = lax.dynamic_index_in_dim(tiles, (block + step) % 3, 0, keepdims=False)
-        came.append(shifted((theirs * TEXT_UP[2]).astype(HALF), "z", 4 * step))
-    tiles = lax.dynamic_index_in_dim(tiles, block, 0, keepdims=False)
-    tiles = tiles + (came[0].astype(F32) + came[1].astype(F32)) * (1.0 / TEXT_UP[2])
-    tiles = halve(tiles, 3, "z", z % 2, 1, tuple((i, i ^ 1) for i in range(12)))
-    total = halve(tiles, 4, "z", (z // 2) % 2, 0, tuple((i, i ^ 2) for i in range(12)))
+        came.append(shifted((theirs * TEXT_UP[4]).astype(HALF), "z", 4 * step))
+    total = lax.dynamic_index_in_dim(tiles, block, 0, keepdims=False)
+    total = total + (came[0].astype(F32) + came[1].astype(F32)) * (1.0 / TEXT_UP[4])
     grad_text = total * scale
 
     def weights(which):

time: 163 us -> 167 us (1.025)
  the two profiles are of different devices: /device:TPU:8 before, /device:TPU:1 now
where the time goes in v4:
time: 167 us; the launch traced here: 165 us
  starting transfers between devices  94.2 us (56%)
  waiting for transfers between devices  55.6 us (33%)
  other arithmetic  5.76 us (3%)
  matrix products  4.54 us (3%)
  between operations  2.53 us (2%)
  local copies, waits for them, and re-layouts  2.08 us (1%)
    all_to_all x4, starting transfers between devices, exchange(): return lax.all_to_all(tiles, axis, split_axis=0, concat_axis=0, tiled=True)  34.8 us
    ppermute x8, starting transfers between devices, shifted(): lax.ppermute(array, axis, tuple(((i, (i + step) % length) for i in range(...  33.1 us
    all_to_all x4, waiting for transfers between devices, exchange(): return lax.all_to_all(tiles, axis, split_axis=0, concat_axis=0, tiled=True)  22.2 us
    ppermute x3, waiting for transfers between devices, halve(): got = lax.ppermute((theirs * TEXT_UP[k]).astype(HALF), axis, pairs)  20.4 us
    ppermute x3, starting transfers between devices, swap(): return lax.ppermute(array, 'core', ((0, 1), (1, 0)))  14.6 us
    ppermute x8, waiting for transfers between devices, shifted(): lax.ppermute(array, axis, tuple(((i, (i + step) % length) for i in range(...  12.3 us
    ppermute x3, starting transfers between devices, halve(): got = lax.ppermute((theirs * TEXT_UP[k]).astype(HALF), axis, pairs)  11.8 us
    dot_general x6, matrix products, dot(): lax.dot_general(a, b, (((ca,), (cb,)), ((), ())), precision=HIGH, preferr...  3.87 us
  transfers between devices with their start and end apart: 18, of which 10 were waited for; matrix products, arithmetic and copies ran while one was open for 3% of the time, Pallas kernels for 0%

profile of v4, /device:TPU:1, one launch (start us, length us, event | category | flops | bytes accessed | tf_op | source)
XLA Modules:
  0.0 164.7 jit_solution(13291104881416272014)
XLA Ops:
  0.7 0.9 fusion.27
  1.5 0.9 broadcast_in_dim.12
  2.4 16.9 %all-to-all-start = ((f16[24,32,384]{2,1,0:T(8,128)(2,1)}), f16[24,32,384]{2,1,0:T(8,128)(2,1)S(1)}, u32[]{:S(2)}, u32[]{:S(2)}) async-start(f16[24,32,384]{2,1,0:T(8,128)(2,1)} %broadcast_in_dim.12), calls=%async_computation | async-start | bytes 1179648 | tf_op jit(solution)/shard_map/all_to_all | solution.py:22
  19.3 5.0 %collective-permute-start.2 = (f16[96,128]{1,0:T(8,128)(2,1)S(1)}, f16[96,128]{1,0:T(8,128)(2,1)S(1)}, u32[]{:S(2)}, u32[]{:S(2)}) collective-permute-start(f16[96,128]{1,0:T(8,128)(2,1)S(1)} %get-tuple-element.25), channel_id=1, source_target_pairs={{0,3},{1,0},{2,1},{3,2},{4,7},{5,4},{6,5},{7,6},{8,11},{9,8},{10,9... | collective-permute-start | bytes 73736 | tf_op jit(solution)/shard_map/ppermute | solution.py:35
  24.3 4.4 %collective-permute-start.1 = (f16[96,128]{1,0:T(8,128)(2,1)S(1)}, f16[96,128]{1,0:T(8,128)(2,1)S(1)}, u32[]{:S(2)}, u32[]{:S(2)}) collective-permute-start(f16[96,128]{1,0:T(8,128)(2,1)S(1)} %get-tuple-element.25), channel_id=1, source_target_pairs={{0,2},{1,3},{2,0},{3,1},{4,6},{5,7},{6,4},{7,5},{8,10},{9,11},{10,... | collective-permute-start | bytes 73736 | tf_op jit(solution)/shard_map/ppermute | solution.py:35
  28.8 3.3 %collective-permute-start = (f16[96,128]{1,0:T(8,128)(2,1)S(1)}, f16[96,128]{1,0:T(8,128)(2,1)S(1)}, u32[]{:S(2)}, u32[]{:S(2)}) collective-permute-start(f16[96,128]{1,0:T(8,128)(2,1)S(1)} %get-tuple-element.25), channel_id=1, source_target_pairs={{0,1},{1,2},{2,3},{3,0},{4,5},{5,6},{6,7},{7,4},{8,9},{9,10},{10,1... | collective-permute-start | bytes 73736 | tf_op jit(solution)/shard_map/ppermute | solution.py:35
  33.8 2.1 %collective-permute-done = f16[96,128]{1,0:T(8,128)(2,1)S(1)} collective-permute-done((f16[96,128]{1,0:T(8,128)(2,1)S(1)}, f16[96,128]{1,0:T(8,128)(2,1)S(1)}, u32[]{:S(2)}, u32[]{:S(2)}) %collective-permute-start) | collective-permute-done | bytes 24608 | tf_op jit(solution)/shard_map/ppermute | solution.py:35
  35.9 4.7 %collective-permute-start.4 = (f16[4,96,128]{2,1,0:T(8,128)(2,1)S(1)}, f16[4,96,128]{2,1,0:T(8,128)(2,1)S(1)}, u32[]{:S(2)}, u32[]{:S(2)}) collective-permute-start(f16[4,96,128]{2,1,0:T(8,128)(2,1)S(1)} %pad_maximum_fusion.3), channel_id=1, source_target_pairs={{0,8},{4,12},{8,0},{12,4},{1,9},{5,13},{9,1},{13,5},{2,10},{6,14},... | collective-permute-start | bytes 294920 | tf_op jit(solution)/shard_map/ppermute | solution.py:35
  40.6 2.8 %collective-permute-start.5 = (f16[4,96,128]{2,1,0:T(8,128)(2,1)S(1)}, f16[4,96,128]{2,1,0:T(8,128)(2,1)S(1)}, u32[]{:S(2)}, u32[]{:S(2)}) collective-permute-start(f16[4,96,128]{2,1,0:T(8,128)(2,1)S(1)} %pad_maximum_fusion.3), channel_id=1, source_target_pairs={{0,12},{4,0},{8,4},{12,8},{1,13},{5,1},{9,5},{13,9},{2,14},{6,2},{... | collective-permute-start | bytes 294920 | tf_op jit(solution)/shard_map/ppermute | solution.py:35
  43.4 2.5 %collective-permute-start.3 = (f16[4,96,128]{2,1,0:T(8,128)(2,1)S(1)}, f16[4,96,128]{2,1,0:T(8,128)(2,1)S(1)}, u32[]{:S(2)}, u32[]{:S(2)}) collective-permute-start(f16[4,96,128]{2,1,0:T(8,128)(2,1)S(1)} %pad_maximum_fusion.3), channel_id=1, source_target_pairs={{0,4},{4,8},{8,12},{12,0},{1,5},{5,9},{9,13},{13,1},{2,6},{6,10},{... | collective-permute-start | bytes 294920 | tf_op jit(solution)/shard_map/ppermute | solution.py:35
  45.9 0.7 collective-permute-done.5
  46.6 3.3 %collective-permute-done.3 = f16[4,96,128]{2,1,0:T(8,128)(2,1)S(1)} collective-permute-done((f16[4,96,128]{2,1,0:T(8,128)(2,1)S(1)}, f16[4,96,128]{2,1,0:T(8,128)(2,1)S(1)}, u32[]{:S(2)}, u32[]{:S(2)}) %collective-permute-start.3) | collective-permute-done | bytes 98336 | tf_op jit(solution)/shard_map/ppermute | solution.py:35
  50.3 5.9 %collective-permute-start.6 = (f16[24,32,384]{2,1,0:T(8,128)(2,1)S(1)}, f16[24,32,384]{2,1,0:T(8,128)(2,1)S(1)}, u32[]{:S(2)}, u32[]{:S(2)}) collective-permute-start(f16[24,32,384]{2,1,0:T(8,128)(2,1)S(1)} %all-to-all-done), channel_id=1, source_target_pairs={{0,16},{16,0},{1,17},{17,1},{2,18},{18,2},{3,19},{19,3},{4,20},{20... | collective-permute-start | bytes 1769480 | tf_op jit(solution)/shard_map/ppermute | solution.py:30
  59.8 0.9 pad_maximum_fusion.2
  60.7 4.3 %all-to-all-start.1 = ((f16[16,96,128]{2,1,0:T(8,128)(2,1)}), f16[16,96,128]{2,1,0:T(8,128)(2,1)S(1)}, u32[]{:S(2)}, u32[]{:S(2)}) async-start(f16[16,96,128]{2,1,0:T(8,128)(2,1)} %bitcast.33), calls=%async_computation.1 | async-start | bytes 786432 | tf_op jit(solution)/shard_map/all_to_all | solution.py:22
  64.9 13.7 %all-to-all-done.1 = f16[16,96,128]{2,1,0:T(8,128)(2,1)S(1)} async-done(((f16[16,96,128]{2,1,0:T(8,128)(2,1)}), f16[16,96,128]{2,1,0:T(8,128)(2,1)S(1)}, u32[]{:S(2)}, u32[]{:S(2)}) %all-to-all-start.1) | async-done | bytes 393248 | tf_op jit(solution)/shard_map/all_to_all | solution.py:22
  79.3 0.8 broadcast_in_dim.25
  80.1 4.2 %all-to-all-start.2 = ((bf16[16,96,128]{2,1,0:T(8,128)(2,1)}), bf16[16,96,128]{2,1,0:T(8,128)(2,1)S(1)}, u32[]{:S(2)}, u32[]{:S(2)}) async-start(bf16[16,96,128]{2,1,0:T(8,128)(2,1)} %broadcast_in_dim.25), calls=%async_computation.2 | async-start | bytes 786432 | tf_op jit(solution)/shard_map/all_to_all | solution.py:22
  84.9 4.2 %collective-permute-start.7 = (f16[768,384]{1,0:T(8,128)(2,1)S(1)}, f16[768,384]{1,0:T(8,128)(2,1)S(1)}, u32[]{:S(2)}, u32[]{:S(2)}) collective-permute-start(f16[768,384]{1,0:T(8,128)(2,1)S(1)} %fusion), channel_id=1, source_target_pairs={{0,16},{16,0},{1,17},{17,1},{2,18},{18,2},{3,19},{19,3},{4,20},{20... | collective-permute-start | bytes 1769480 | tf_op jit(solution)/shard_map/ppermute | solution.py:30
  89.2 8.6 %all-to-all-done.2 = bf16[16,96,128]{2,1,0:T(8,128)(2,1)S(1)} async-done(((bf16[16,96,128]{2,1,0:T(8,128)(2,1)}), bf16[16,96,128]{2,1,0:T(8,128)(2,1)S(1)}, u32[]{:S(2)}, u32[]{:S(2)}) %all-to-all-start.2) | async-done | bytes 393248 | tf_op jit(solution)/shard_map/all_to_all | solution.py:22
  98.0 4.5 %collective-permute-start.13 = (f16[24,32,320]{2,1,0:T(8,128)(2,1)S(1)}, f16[24,32,320]{2,1,0:T(8,128)(2,1)S(1)}, u32[]{:S(2)}, u32[]{:S(2)}) collective-permute-start(f16[24,32,320]{2,1,0:T(8,128)(2,1)S(1)} %fusion.1), channel_id=1, source_target_pairs={{0,16},{16,0},{1,17},{17,1},{2,18},{18,2},{3,19},{19,3},{4,20},{20... | collective-permute-start | bytes 1474568 | tf_op jit(solution)/shard_map/ppermute | solution.py:30
  102.6 0.7 multiply_add_fusion
  103.4 5.3 %collective-permute-start.8 = (f16[3,2,2,32,384]{4,3,0,1,2:T(8,128)(2,1)S(1)}, f16[3,2,2,32,384]{4,3,0,1,2:T(8,128)(2,1)S(1)}, u32[]{:S(2)}, u32[]{:S(2)}) collective-permute-start(f16[3,2,2,32,384]{4,3,0,1,2:T(8,128)(2,1)S(1)} %fusion.13), channel_id=1, source_target_pairs={{0,384},{384,0},{1,385},{385,1},{2,386},{386,2},{3,387},{387,3},{4... | collective-permute-start | bytes 884744 | tf_op jit(solution)/shard_map/ppermute | solution.py:101
  109.2 1.0 maximum_maximum_fusion
  110.2 9.4 %all-to-all-start.3 = ((f16[24,80,128]{2,1,0:T(8,128)(2,1)}), f16[24,80,128]{2,1,0:T(8,128)(2,1)S(1)}, u32[]{:S(2)}, u32[]{:S(2)}) async-start(f16[24,80,128]{2,1,0:T(8,128)(2,1)} %maximum_maximum_fusion), calls=%async_computation.3 | async-start | bytes 983040 | tf_op jit(solution)/shard_map/all_to_all | solution.py:22
  119.8 3.2 %collective-permute-start.9 = (f16[3,2,32,384]{3,2,0,1:T(8,128)(2,1)S(1)}, f16[3,2,32,384]{3,2,0,1:T(8,128)(2,1)S(1)}, u32[]{:S(2)}, u32[]{:S(2)}) collective-permute-start(f16[3,2,32,384]{3,2,0,1:T(8,128)(2,1)S(1)} %fusion.21), channel_id=1, source_target_pairs={{0,32},{32,0},{64,96},{96,64},{128,160},{160,128},{192,224},{224,1... | collective-permute-start | bytes 442376 | tf_op jit(solution)/shard_map/ppermute | solution.py:101
  123.0 17.0 %collective-permute-done.9 = f16[3,2,32,384]{3,2,0,1:T(8,128)(2,1)S(1)} collective-permute-done((f16[3,2,32,384]{3,2,0,1:T(8,128)(2,1)S(1)}, f16[3,2,32,384]{3,2,0,1:T(8,128)(2,1)S(1)}, u32[]{:S(2)}, u32[]{:S(2)}) %collective-permute-start.9) | collective-permute-done | bytes 147488 | tf_op jit(solution)/shard_map/ppermute | solution.py:101
  140.1 3.3 %collective-permute-start.10 = (f16[3,32,384]{2,1,0:T(8,128)(2,1)S(1)}, f16[3,32,384]{2,1,0:T(8,128)(2,1)S(1)}, u32[]{:S(2)}, u32[]{:S(2)}) collective-permute-start(f16[3,32,384]{2,1,0:T(8,128)(2,1)S(1)} %fusion.24), channel_id=1, source_target_pairs={{0,64},{32,96},{64,0},{96,32},{128,192},{160,224},{192,128},{224,1... | collective-permute-start | bytes 221192 | tf_op jit(solution)/shard_map/ppermute | solution.py:101
  143.5 3.4 %collective-permute-done.10 = f16[3,32,384]{2,1,0:T(8,128)(2,1)S(1)} collective-permute-done((f16[3,32,384]{2,1,0:T(8,128)(2,1)S(1)}, f16[3,32,384]{2,1,0:T(8,128)(2,1)S(1)}, u32[]{:S(2)}, u32[]{:S(2)}) %collective-permute-start.10) | collective-permute-done | bytes 73760 | tf_op jit(solution)/shard_map/ppermute | solution.py:101
  147.0 7.7 %collective-permute-start.12 = (f16[32,384]{1,0:T(8,128)(2,1)S(1)}, f16[32,384]{1,0:T(8,128)(2,1)S(1)}, u32[]{:S(2)}, u32[]{:S(2)}) collective-permute-start(f16[32,384]{1,0:T(8,128)(2,1)S(1)} %get-tuple-element.21), channel_id=1, source_target_pairs={{0,256},{32,288},{64,320},{96,352},{128,0},{160,32},{192,64},{224,... | collective-permute-start | bytes 73736 | tf_op jit(solution)/shard_map/ppermute | solution.py:35
  154.6 2.7 %collective-permute-start.11 = (f16[32,384]{1,0:T(8,128)(2,1)S(1)}, f16[32,384]{1,0:T(8,128)(2,1)S(1)}, u32[]{:S(2)}, u32[]{:S(2)}) collective-permute-start(f16[32,384]{1,0:T(8,128)(2,1)S(1)} %get-tuple-element.20), channel_id=1, source_target_pairs={{0,128},{32,160},{64,192},{96,224},{128,256},{160,288},{192,320},{... | collective-permute-start | bytes 73736 | tf_op jit(solution)/shard_map/ppermute | solution.py:35
  157.4 5.8 %collective-permute-done.11 = f16[32,384]{1,0:T(8,128)(2,1)S(1)} collective-permute-done((f16[32,384]{1,0:T(8,128)(2,1)S(1)}, f16[32,384]{1,0:T(8,128)(2,1)S(1)}, u32[]{:S(2)}, u32[]{:S(2)}) %collective-permute-start.11) | collective-permute-done | bytes 24608 | tf_op jit(solution)/shard_map/ppermute | solution.py:35
  (50 shorter events, 8.3 us)
Async XLA Ops:
  0.6 97.1 %copy-start = (bf16[128,320]{0,1:T(8,128)(2,1)S(1)}, bf16[128,320]{0,1:T(8,128)(2,1)}, u32[]{:S(2)}) copy-start(bf16[128,320]{0,1:T(8,128)(2,1)} %param.8) | copy-start | bytes 245764
  0.6 18.7 %copy-start.1 = (f32[128,96]{0,1:T(8,128)S(1)}, f32[128,96]{0,1:T(8,128)}, u32[]{:S(2)}) copy-start(f32[128,96]{0,1:T(8,128)} %param.6) | copy-start | bytes 147460
  2.4 47.9 %all-to-all-start = ((f16[24,32,384]{2,1,0:T(8,128)(2,1)}), f16[24,32,384]{2,1,0:T(8,128)(2,1)S(1)}, u32[]{:S(2)}, u32[]{:S(2)}) async-start(f16[24,32,384]{2,1,0:T(8,128)(2,1)} %broadcast_in_dim.12), calls=%async_computation | async-start | bytes 1179648 | tf_op jit(solution)/shard_map/all_to_all | solution.py:22
  19.3 14.1 %collective-permute-start.2 = (f16[96,128]{1,0:T(8,128)(2,1)S(1)}, f16[96,128]{1,0:T(8,128)(2,1)S(1)}, u32[]{:S(2)}, u32[]{:S(2)}) collective-permute-start(f16[96,128]{1,0:T(8,128)(2,1)S(1)} %get-tuple-element.25), channel_id=1, source_target_pairs={{0,3},{1,0},{2,1},{3,2},{4,7},{5,4},{6,5},{7,6},{8,11},{9,8},{10,9... | collective-permute-start | bytes 73736 | tf_op jit(solution)/shard_map/ppermute | solution.py:35
  24.3 9.5 %collective-permute-start.1 = (f16[96,128]{1,0:T(8,128)(2,1)S(1)}, f16[96,128]{1,0:T(8,128)(2,1)S(1)}, u32[]{:S(2)}, u32[]{:S(2)}) collective-permute-start(f16[96,128]{1,0:T(8,128)(2,1)S(1)} %get-tuple-element.25), channel_id=1, source_target_pairs={{0,2},{1,3},{2,0},{3,1},{4,6},{5,7},{6,4},{7,5},{8,10},{9,11},{10,... | collective-permute-start | bytes 73736 | tf_op jit(solution)/shard_map/ppermute | solution.py:35
  28.8 7.1 %collective-permute-start = (f16[96,128]{1,0:T(8,128)(2,1)S(1)}, f16[96,128]{1,0:T(8,128)(2,1)S(1)}, u32[]{:S(2)}, u32[]{:S(2)}) collective-permute-start(f16[96,128]{1,0:T(8,128)(2,1)S(1)} %get-tuple-element.25), channel_id=1, source_target_pairs={{0,1},{1,2},{2,3},{3,0},{4,5},{5,6},{6,7},{7,4},{8,9},{9,10},{10,1... | collective-permute-start | bytes 73736 | tf_op jit(solution)/shard_map/ppermute | solution.py:35
  35.9 10.0 %collective-permute-start.4 = (f16[4,96,128]{2,1,0:T(8,128)(2,1)S(1)}, f16[4,96,128]{2,1,0:T(8,128)(2,1)S(1)}, u32[]{:S(2)}, u32[]{:S(2)}) collective-permute-start(f16[4,96,128]{2,1,0:T(8,128)(2,1)S(1)} %pad_maximum_fusion.3), channel_id=1, source_target_pairs={{0,8},{4,12},{8,0},{12,4},{1,9},{5,13},{9,1},{13,5},{2,10},{6,14},... | collective-permute-start | bytes 294920 | tf_op jit(solution)/shard_map/ppermute | solution.py:35
  40.6 6.0 %collective-permute-start.5 = (f16[4,96,128]{2,1,0:T(8,128)(2,1)S(1)}, f16[4,96,128]{2,1,0:T(8,128)(2,1)S(1)}, u32[]{:S(2)}, u32[]{:S(2)}) collective-permute-start(f16[4,96,128]{2,1,0:T(8,128)(2,1)S(1)} %pad_maximum_fusion.3), channel_id=1, source_target_pairs={{0,12},{4,0},{8,4},{12,8},{1,13},{5,1},{9,5},{13,9},{2,14},{6,2},{... | collective-permute-start | bytes 294920 | tf_op jit(solution)/shard_map/ppermute | solution.py:35
  43.4 6.6 %collective-permute-start.3 = (f16[4,96,128]{2,1,0:T(8,128)(2,1)S(1)}, f16[4,96,128]{2,1,0:T(8,128)(2,1)S(1)}, u32[]{:S(2)}, u32[]{:S(2)}) collective-permute-start(f16[4,96,128]{2,1,0:T(8,128)(2,1)S(1)} %pad_maximum_fusion.3), channel_id=1, source_target_pairs={{0,4},{4,8},{8,12},{12,0},{1,5},{5,9},{9,13},{13,1},{2,6},{6,10},{... | collective-permute-start | bytes 294920 | tf_op jit(solution)/shard_map/ppermute | solution.py:35
  50.3 7.5 %collective-permute-start.6 = (f16[24,32,384]{2,1,0:T(8,128)(2,1)S(1)}, f16[24,32,384]{2,1,0:T(8,128)(2,1)S(1)}, u32[]{:S(2)}, u32[]{:S(2)}) collective-permute-start(f16[24,32,384]{2,1,0:T(8,128)(2,1)S(1)} %all-to-all-done), channel_id=1, source_target_pairs={{0,16},{16,0},{1,17},{17,1},{2,18},{18,2},{3,19},{19,3},{4,20},{20... | collective-permute-start | bytes 1769480 | tf_op jit(solution)/shard_map/ppermute | solution.py:30
  56.4 1.4 copy-start.2
  60.7 18.0 %all-to-all-start.1 = ((f16[16,96,128]{2,1,0:T(8,128)(2,1)}), f16[16,96,128]{2,1,0:T(8,128)(2,1)S(1)}, u32[]{:S(2)}, u32[]{:S(2)}) async-start(f16[16,96,128]{2,1,0:T(8,128)(2,1)} %bitcast.33), calls=%async_computation.1 | async-start | bytes 786432 | tf_op jit(solution)/shard_map/all_to_all | solution.py:22
  80.1 17.6 %all-to-all-start.2 = ((bf16[16,96,128]{2,1,0:T(8,128)(2,1)}), bf16[16,96,128]{2,1,0:T(8,128)(2,1)S(1)}, u32[]{:S(2)}, u32[]{:S(2)}) async-start(bf16[16,96,128]{2,1,0:T(8,128)(2,1)} %broadcast_in_dim.25), calls=%async_computation.2 | async-start | bytes 786432 | tf_op jit(solution)/shard_map/all_to_all | solution.py:22
  84.9 17.6 %collective-permute-start.7 = (f16[768,384]{1,0:T(8,128)(2,1)S(1)}, f16[768,384]{1,0:T(8,128)(2,1)S(1)}, u32[]{:S(2)}, u32[]{:S(2)}) collective-permute-start(f16[768,384]{1,0:T(8,128)(2,1)S(1)} %fusion), channel_id=1, source_target_pairs={{0,16},{16,0},{1,17},{17,1},{2,18},{18,2},{3,19},{19,3},{4,20},{20... | collective-permute-start | bytes 1769480 | tf_op jit(solution)/shard_map/ppermute | solution.py:30
  98.0 10.7 %collective-permute-start.13 = (f16[24,32,320]{2,1,0:T(8,128)(2,1)S(1)}, f16[24,32,320]{2,1,0:T(8,128)(2,1)S(1)}, u32[]{:S(2)}, u32[]{:S(2)}) collective-permute-start(f16[24,32,320]{2,1,0:T(8,128)(2,1)S(1)} %fusion.1), channel_id=1, source_target_pairs={{0,16},{16,0},{1,17},{17,1},{2,18},{18,2},{3,19},{19,3},{4,20},{20... | collective-permute-start | bytes 1474568 | tf_op jit(solution)/shard_map/ppermute | solution.py:30
  103.4 16.2 %collective-permute-start.8 = (f16[3,2,2,32,384]{4,3,0,1,2:T(8,128)(2,1)S(1)}, f16[3,2,2,32,384]{4,3,0,1,2:T(8,128)(2,1)S(1)}, u32[]{:S(2)}, u32[]{:S(2)}) collective-permute-start(f16[3,2,2,32,384]{4,3,0,1,2:T(8,128)(2,1)S(1)} %fusion.13), channel_id=1, source_target_pairs={{0,384},{384,0},{1,385},{385,1},{2,386},{386,2},{3,387},{387,3},{4... | collective-permute-start | bytes 884744 | tf_op jit(solution)/shard_map/ppermute | solution.py:101
  110.2 53.6 %all-to-all-start.3 = ((f16[24,80,128]{2,1,0:T(8,128)(2,1)}), f16[24,80,128]{2,1,0:T(8,128)(2,1)S(1)}, u32[]{:S(2)}, u32[]{:S(2)}) async-start(f16[24,80,128]{2,1,0:T(8,128)(2,1)} %maximum_maximum_fusion), calls=%async_computation.3 | async-start | bytes 983040 | tf_op jit(solution)/shard_map/all_to_all | solution.py:22
  119.8 20.3 %collective-permute-start.9 = (f16[3,2,32,384]{3,2,0,1:T(8,128)(2,1)S(1)}, f16[3,2,32,384]{3,2,0,1:T(8,128)(2,1)S(1)}, u32[]{:S(2)}, u32[]{:S(2)}) collective-permute-start(f16[3,2,32,384]{3,2,0,1:T(8,128)(2,1)S(1)} %fusion.21), channel_id=1, source_target_pairs={{0,32},{32,0},{64,96},{96,64},{128,160},{160,128},{192,224},{224,1... | collective-permute-start | bytes 442376 | tf_op jit(solution)/shard_map/ppermute | solution.py:101
  140.1 6.8 %collective-permute-start.10 = (f16[3,32,384]{2,1,0:T(8,128)(2,1)S(1)}, f16[3,32,384]{2,1,0:T(8,128)(2,1)S(1)}, u32[]{:S(2)}, u32[]{:S(2)}) collective-permute-start(f16[3,32,384]{2,1,0:T(8,128)(2,1)S(1)} %fusion.24), channel_id=1, source_target_pairs={{0,64},{32,96},{64,0},{96,32},{128,192},{160,224},{192,128},{224,1... | collective-permute-start | bytes 221192 | tf_op jit(solution)/shard_map/ppermute | solution.py:101
  147.0 10.4 %collective-permute-start.12 = (f16[32,384]{1,0:T(8,128)(2,1)S(1)}, f16[32,384]{1,0:T(8,128)(2,1)S(1)}, u32[]{:S(2)}, u32[]{:S(2)}) collective-permute-start(f16[32,384]{1,0:T(8,128)(2,1)S(1)} %get-tuple-element.21), channel_id=1, source_target_pairs={{0,256},{32,288},{64,320},{96,352},{128,0},{160,32},{192,64},{224,... | collective-permute-start | bytes 73736 | tf_op jit(solution)/shard_map/ppermute | solution.py:35
  154.6 8.6 %collective-permute-start.11 = (f16[32,384]{1,0:T(8,128)(2,1)S(1)}, f16[32,384]{1,0:T(8,128)(2,1)S(1)}, u32[]{:S(2)}, u32[]{:S(2)}) collective-permute-start(f16[32,384]{1,0:T(8,128)(2,1)S(1)} %get-tuple-element.20), channel_id=1, source_target_pairs={{0,128},{32,160},{64,192},{96,224},{128,256},{160,288},{192,320},{... | collective-permute-start | bytes 73736 | tf_op jit(solution)/shard_map/ppermute | solution.py:35

commit v5 on v2

--- a/solution.py
+++ b/solution.py
@@ -14,7 +14,7 @@
 
 EMB_UP = 2.0**18
 IMAGE_UP = 2.0**10
-TEXT_UP = (2.0**11, 2.0**10, 2.0**9, 2.0**7, 2.0**6)
+TEXT_UP = (2.0**11, 2.0**10, 2.0**9, 2.0**8, 2.0**6)
 PROJ_UP = (2.0**-2, 2.0**-3)
 
 
@@ -66,8 +66,7 @@
     other = swap(own).reshape(768, -1).astype(F32)
     own = own.reshape(768, -1).astype(F32)
     near = jnp.stack([image_tile] + [shifted(image_tile, "yh", k) for k in (1, 2, 3)])
-    far = [near] + [shifted(near, "x", k) for k in (1, 3)]
-    far.insert(2, shifted(near, "x", 2))
+    far = [near] + [shifted(near, "x", k) for k in (1, 2, 3)]
     by_x = in_order(far, lax.axis_index("x"))
     image_full = in_order([by_x[:, k] for k in range(4)], lax.axis_index("yh"))
     image_full = jnp.moveaxis(image_full, 0, 1).astype(F32)
@@ -104,14 +103,14 @@
         return mine + got.astype(F32) * (1.0 / TEXT_UP[k])
 
     tiles = halve(tiles, 1, "yl", yl, 0, ((0, 1), (1, 0)))
+    tiles = halve(tiles, 2, "z", z % 2, 2, tuple((i, i ^ 1) for i in range(12)))
     block = z // 4
     came = []
     for step in (1, 2):
         theirs = lax.dynamic_index_in_dim(tiles, (block + step) % 3, 0, keepdims=False)
-        came.append(shifted((theirs * TEXT_UP[2]).astype(HALF), "z", 4 * step))
+        came.append(shifted((theirs * TEXT_UP[3]).astype(HALF), "z", 4 * step))
     tiles = lax.dynamic_index_in_dim(tiles, block, 0, keepdims=False)
-    tiles = tiles + (came[0].astype(F32) + came[1].astype(F32)) * (1.0 / TEXT_UP[2])
-    tiles = halve(tiles, 3, "z", z % 2, 1, tuple((i, i ^ 1) for i in range(12)))
+    tiles = tiles + (came[0].astype(F32) + came[1].astype(F32)) * (1.0 / TEXT_UP[3])
     total = halve(tiles, 4, "z", (z // 2) % 2, 0, tuple((i, i ^ 2) for i in range(12)))
     grad_text = total * scale
 

time: 167 us -> 169 us (1.012)
  the two profiles are of different devices: /device:TPU:8 before, /device:TPU:1 now
where the time goes in v5:
time: 169 us; the launch traced here: 167 us
  starting transfers between devices  91.7 us (54%)
  waiting for transfers between devices  59.7 us (35%)
  matrix products  6.44 us (4%)
  other arithmetic  4.76 us (3%)
  between operations  2.49 us (1%)
  local copies, waits for them, and re-layouts  1.9 us (1%)
    all_to_all x4, starting transfers between devices, exchange(): return lax.all_to_all(tiles, axis, split_axis=0, concat_axis=0, tiled=True)  34.8 us
    ppermute x8, starting transfers between devices, shifted(): lax.ppermute(array, axis, tuple(((i, (i + step) % length) for i in range(...  31.9 us
    ppermute x3, waiting for transfers between devices, halve(): got = lax.ppermute((theirs * TEXT_UP[k]).astype(HALF), axis, pairs)  23.8 us
    all_to_all x4, waiting for transfers between devices, exchange(): return lax.all_to_all(tiles, axis, split_axis=0, concat_axis=0, tiled=True)  22.3 us
    ppermute x3, starting transfers between devices, swap(): return lax.ppermute(array, 'core', ((0, 1), (1, 0)))  14.6 us
    ppermute x8, waiting for transfers between devices, shifted(): lax.ppermute(array, axis, tuple(((i, (i + step) % length) for i in range(...  13.1 us
    ppermute x3, starting transfers between devices, halve(): got = lax.ppermute((theirs * TEXT_UP[k]).astype(HALF), axis, pairs)  10.5 us
    dot_general x6, matrix products, dot(): lax.dot_general(a, b, (((ca,), (cb,)), ((), ())), precision=HIGH, preferr...  4.93 us
  transfers between devices with their start and end apart: 18, of which 10 were waited for; matrix products, arithmetic and copies ran while one was open for 4% of the time, Pallas kernels for 0%

profile of v5, /device:TPU:1, one launch (start us, length us, event | category | flops | bytes accessed | tf_op | source)
XLA Modules:
  0.0 167.0 jit_solution(13052157010773206762)
XLA Ops:
  0.7 0.9 fusion.28
  1.5 0.9 broadcast_in_dim.12
  2.4 16.9 %all-to-all-start = ((f16[24,32,384]{2,1,0:T(8,128)(2,1)}), f16[24,32,384]{2,1,0:T(8,128)(2,1)S(1)}, u32[]{:S(2)}, u32[]{:S(2)}) async-start(f16[24,32,384]{2,1,0:T(8,128)(2,1)} %broadcast_in_dim.12), calls=%async_computation | async-start | bytes 1179648 | tf_op jit(solution)/shard_map/all_to_all | solution.py:22
  19.4 5.0 %collective-permute-start.2 = (f16[96,128]{1,0:T(8,128)(2,1)S(1)}, f16[96,128]{1,0:T(8,128)(2,1)S(1)}, u32[]{:S(2)}, u32[]{:S(2)}) collective-permute-start(f16[96,128]{1,0:T(8,128)(2,1)S(1)} %get-tuple-element.21), channel_id=1, source_target_pairs={{0,3},{1,0},{2,1},{3,2},{4,7},{5,4},{6,5},{7,6},{8,11},{9,8},{10,9... | collective-permute-start | bytes 73736 | tf_op jit(solution)/shard_map/ppermute | solution.py:35
  24.4 4.4 %collective-permute-start.1 = (f16[96,128]{1,0:T(8,128)(2,1)S(1)}, f16[96,128]{1,0:T(8,128)(2,1)S(1)}, u32[]{:S(2)}, u32[]{:S(2)}) collective-permute-start(f16[96,128]{1,0:T(8,128)(2,1)S(1)} %get-tuple-element.21), channel_id=1, source_target_pairs={{0,2},{1,3},{2,0},{3,1},{4,6},{5,7},{6,4},{7,5},{8,10},{9,11},{10,... | collective-permute-start | bytes 73736 | tf_op jit(solution)/shard_map/ppermute | solution.py:35
  28.8 3.3 %collective-permute-start = (f16[96,128]{1,0:T(8,128)(2,1)S(1)}, f16[96,128]{1,0:T(8,128)(2,1)S(1)}, u32[]{:S(2)}, u32[]{:S(2)}) collective-permute-start(f16[96,128]{1,0:T(8,128)(2,1)S(1)} %get-tuple-element.21), channel_id=1, source_target_pairs={{0,1},{1,2},{2,3},{3,0},{4,5},{5,6},{6,7},{7,4},{8,9},{9,10},{10,1... | collective-permute-start | bytes 73736 | tf_op jit(solution)/shard_map/ppermute | solution.py:35
  33.9 2.1 %collective-permute-done = f16[96,128]{1,0:T(8,128)(2,1)S(1)} collective-permute-done((f16[96,128]{1,0:T(8,128)(2,1)S(1)}, f16[96,128]{1,0:T(8,128)(2,1)S(1)}, u32[]{:S(2)}, u32[]{:S(2)}) %collective-permute-start) | collective-permute-done | bytes 24608 | tf_op jit(solution)/shard_map/ppermute | solution.py:35
  36.0 4.7 %collective-permute-start.4 = (f16[4,96,128]{2,1,0:T(8,128)(2,1)S(1)}, f16[4,96,128]{2,1,0:T(8,128)(2,1)S(1)}, u32[]{:S(2)}, u32[]{:S(2)}) collective-permute-start(f16[4,96,128]{2,1,0:T(8,128)(2,1)S(1)} %pad_maximum_fusion.3), channel_id=1, source_target_pairs={{0,8},{4,12},{8,0},{12,4},{1,9},{5,13},{9,1},{13,5},{2,10},{6,14},... | collective-permute-start | bytes 294920 | tf_op jit(solution)/shard_map/ppermute | solution.py:35
  40.6 2.8 %collective-permute-start.5 = (f16[4,96,128]{2,1,0:T(8,128)(2,1)S(1)}, f16[4,96,128]{2,1,0:T(8,128)(2,1)S(1)}, u32[]{:S(2)}, u32[]{:S(2)}) collective-permute-start(f16[4,96,128]{2,1,0:T(8,128)(2,1)S(1)} %pad_maximum_fusion.3), channel_id=1, source_target_pairs={{0,12},{4,0},{8,4},{12,8},{1,13},{5,1},{9,5},{13,9},{2,14},{6,2},{... | collective-permute-start | bytes 294920 | tf_op jit(solution)/shard_map/ppermute | solution.py:35
  43.4 2.5 %collective-permute-start.3 = (f16[4,96,128]{2,1,0:T(8,128)(2,1)S(1)}, f16[4,96,128]{2,1,0:T(8,128)(2,1)S(1)}, u32[]{:S(2)}, u32[]{:S(2)}) collective-permute-start(f16[4,96,128]{2,1,0:T(8,128)(2,1)S(1)} %pad_maximum_fusion.3), channel_id=1, source_target_pairs={{0,4},{4,8},{8,12},{12,0},{1,5},{5,9},{9,13},{13,1},{2,6},{6,10},{... | collective-permute-start | bytes 294920 | tf_op jit(solution)/shard_map/ppermute | solution.py:35
  45.9 0.7 collective-permute-done.5
  46.7 3.3 %collective-permute-done.3 = f16[4,96,128]{2,1,0:T(8,128)(2,1)S(1)} collective-permute-done((f16[4,96,128]{2,1,0:T(8,128)(2,1)S(1)}, f16[4,96,128]{2,1,0:T(8,128)(2,1)S(1)}, u32[]{:S(2)}, u32[]{:S(2)}) %collective-permute-start.3) | collective-permute-done | bytes 98336 | tf_op jit(solution)/shard_map/ppermute | solution.py:35
  50.4 5.9 %collective-permute-start.6 = (f16[24,32,384]{2,1,0:T(8,128)(2,1)S(1)}, f16[24,32,384]{2,1,0:T(8,128)(2,1)S(1)}, u32[]{:S(2)}, u32[]{:S(2)}) collective-permute-start(f16[24,32,384]{2,1,0:T(8,128)(2,1)S(1)} %all-to-all-done), channel_id=1, source_target_pairs={{0,16},{16,0},{1,17},{17,1},{2,18},{18,2},{3,19},{19,3},{4,20},{20... | collective-permute-start | bytes 1769480 | tf_op jit(solution)/shard_map/ppermute | solution.py:30
  59.8 0.9 pad_maximum_fusion.2
  60.7 4.3 %all-to-all-start.1 = ((f16[16,96,128]{2,1,0:T(8,128)(2,1)}), f16[16,96,128]{2,1,0:T(8,128)(2,1)S(1)}, u32[]{:S(2)}, u32[]{:S(2)}) async-start(f16[16,96,128]{2,1,0:T(8,128)(2,1)} %bitcast.33), calls=%async_computation.1 | async-start | bytes 786432 | tf_op jit(solution)/shard_map/all_to_all | solution.py:22
  65.0 13.7 %all-to-all-done.1 = f16[16,96,128]{2,1,0:T(8,128)(2,1)S(1)} async-done(((f16[16,96,128]{2,1,0:T(8,128)(2,1)}), f16[16,96,128]{2,1,0:T(8,128)(2,1)S(1)}, u32[]{:S(2)}, u32[]{:S(2)}) %all-to-all-start.1) | async-done | bytes 393248 | tf_op jit(solution)/shard_map/all_to_all | solution.py:22
  79.3 0.8 broadcast_in_dim.25
  80.1 4.2 %all-to-all-start.2 = ((bf16[16,96,128]{2,1,0:T(8,128)(2,1)}), bf16[16,96,128]{2,1,0:T(8,128)(2,1)S(1)}, u32[]{:S(2)}, u32[]{:S(2)}) async-start(bf16[16,96,128]{2,1,0:T(8,128)(2,1)} %broadcast_in_dim.25), calls=%async_computation.2 | async-start | bytes 786432 | tf_op jit(solution)/shard_map/all_to_all | solution.py:22
  85.0 4.2 %collective-permute-start.7 = (f16[768,384]{1,0:T(8,128)(2,1)S(1)}, f16[768,384]{1,0:T(8,128)(2,1)}, u32[]{:S(2)}, u32[]{:S(2)}) collective-permute-start(f16[768,384]{1,0:T(8,128)(2,1)S(1)} %fusion), channel_id=1, source_target_pairs={{0,16},{16,0},{1,17},{17,1},{2,18},{18,2},{3,19},{19,3},{4,20},{20... | collective-permute-start | bytes 1769480 | tf_op jit(solution)/shard_map/ppermute | solution.py:30
  89.2 8.6 %all-to-all-done.2 = bf16[16,96,128]{2,1,0:T(8,128)(2,1)S(1)} async-done(((bf16[16,96,128]{2,1,0:T(8,128)(2,1)}), bf16[16,96,128]{2,1,0:T(8,128)(2,1)S(1)}, u32[]{:S(2)}, u32[]{:S(2)}) %all-to-all-start.2) | async-done | bytes 393248 | tf_op jit(solution)/shard_map/all_to_all | solution.py:22
  98.0 4.5 %collective-permute-start.13 = (f16[24,32,320]{2,1,0:T(8,128)(2,1)S(1)}, f16[24,32,320]{2,1,0:T(8,128)(2,1)S(1)}, u32[]{:S(2)}, u32[]{:S(2)}) collective-permute-start(f16[24,32,320]{2,1,0:T(8,128)(2,1)S(1)} %fusion.1), channel_id=1, source_target_pairs={{0,16},{16,0},{1,17},{17,1},{2,18},{18,2},{3,19},{19,3},{4,20},{20... | collective-permute-start | bytes 1474568 | tf_op jit(solution)/shard_map/ppermute | solution.py:30
  102.6 1.7 %multiply_add_fusion = f32[768,384]{1,0:T(8,128)S(1)} fusion(f16[768,384]{1,0:T(8,128)(2,1)} %collective-permute-done.7, f16[768,128]{1,0:T(8,128)(2,1)S(1)} %bitcast.117, f32[128,384]{1,0:T(8,128)S(1)} %fusion.11), kind=kOutput, calls=%fused_computation.9 | convolution fusion | flops 227672064 | bytes 2162688 | tf_op jit(solution)/shard_map/dot_general | solution.py:55
  104.5 5.3 %collective-permute-start.8 = (f16[3,2,2,32,384]{4,3,1,0,2:T(8,128)(2,1)S(1)}, f16[3,2,2,32,384]{4,3,1,0,2:T(8,128)(2,1)S(1)}, u32[]{:S(2)}, u32[]{:S(2)}) collective-permute-start(f16[3,2,2,32,384]{4,3,1,0,2:T(8,128)(2,1)S(1)} %fusion.13), channel_id=1, source_target_pairs={{0,384},{384,0},{1,385},{385,1},{2,386},{386,2},{3,387},{387,3},{4... | collective-permute-start | bytes 884744 | tf_op jit(solution)/shard_map/ppermute | solution.py:101
  109.8 1.2 multiply_convert_fusion
  111.0 9.4 %all-to-all-start.3 = ((f16[24,32,320]{2,1,0:T(8,128)(2,1)}), f16[24,32,320]{2,1,0:T(8,128)(2,1)S(1)}, u32[]{:S(2)}, u32[]{:S(2)}) async-start(f16[24,32,320]{2,1,0:T(8,128)(2,1)} %multiply_convert_fusion), calls=%async_computation.3 | async-start | bytes 1179648 | tf_op jit(solution)/shard_map/all_to_all | solution.py:22
  120.6 3.2 %collective-permute-start.9 = (f16[3,2,32,384]{3,2,1,0:T(8,128)(2,1)S(1)}, f16[3,2,32,384]{3,2,1,0:T(8,128)(2,1)S(1)}, u32[]{:S(2)}, u32[]{:S(2)}) collective-permute-start(f16[3,2,32,384]{3,2,1,0:T(8,128)(2,1)S(1)} %fusion.21), channel_id=1, source_target_pairs={{0,32},{32,0},{64,96},{96,64},{128,160},{160,128},{192,224},{224,1... | collective-permute-start | bytes 442376 | tf_op jit(solution)/shard_map/ppermute | solution.py:101
  123.8 20.1 %collective-permute-done.9 = f16[3,2,32,384]{3,2,1,0:T(8,128)(2,1)S(1)} collective-permute-done((f16[3,2,32,384]{3,2,1,0:T(8,128)(2,1)S(1)}, f16[3,2,32,384]{3,2,1,0:T(8,128)(2,1)S(1)}, u32[]{:S(2)}, u32[]{:S(2)}) %collective-permute-start.9) | collective-permute-done | bytes 147488 | tf_op jit(solution)/shard_map/ppermute | solution.py:101
  144.0 7.0 %collective-permute-start.11 = (f16[2,32,384]{2,1,0:T(8,128)(2,1)S(1)}, f16[2,32,384]{2,1,0:T(8,128)(2,1)S(1)}, u32[]{:S(2)}, u32[]{:S(2)}) collective-permute-start(f16[2,32,384]{2,1,0:T(8,128)(2,1)S(1)} %get-tuple-element.17), channel_id=1, source_target_pairs={{0,256},{32,288},{64,320},{96,352},{128,0},{160,32},{192,64},{224,... | collective-permute-start | bytes 147464 | tf_op jit(solution)/shard_map/ppermute | solution.py:35
  151.0 2.2 %collective-permute-start.10 = (f16[2,32,384]{2,1,0:T(8,128)(2,1)S(1)}, f16[2,32,384]{2,1,0:T(8,128)(2,1)S(1)}, u32[]{:S(2)}, u32[]{:S(2)}) collective-permute-start(f16[2,32,384]{2,1,0:T(8,128)(2,1)S(1)} %get-tuple-element.16), channel_id=1, source_target_pairs={{0,128},{32,160},{64,192},{96,224},{128,256},{160,288},{192,320},{... | collective-permute-start | bytes 147464 | tf_op jit(solution)/shard_map/ppermute | solution.py:35
  153.3 6.6 %collective-permute-done.10 = f16[2,32,384]{2,1,0:T(8,128)(2,1)S(1)} collective-permute-done((f16[2,32,384]{2,1,0:T(8,128)(2,1)S(1)}, f16[2,32,384]{2,1,0:T(8,128)(2,1)S(1)}, u32[]{:S(2)}, u32[]{:S(2)}) %collective-permute-start.10) | collective-permute-done | bytes 49184 | tf_op jit(solution)/shard_map/ppermute | solution.py:35
  159.9 2.1 %collective-permute-start.12 = (f16[32,384]{1,0:T(8,128)(2,1)S(1)}, f16[32,384]{1,0:T(8,128)(2,1)S(1)}, u32[]{:S(2)}, u32[]{:S(2)}) collective-permute-start(f16[32,384]{1,0:T(8,128)(2,1)S(1)} %fusion.29), channel_id=1, source_target_pairs={{0,64},{32,96},{64,0},{96,32},{128,192},{160,224},{192,128},{224,1... | collective-permute-start | bytes 73736 | tf_op jit(solution)/shard_map/ppermute | solution.py:101
  162.0 3.6 %collective-permute-done.12 = f16[32,384]{1,0:T(8,128)(2,1)S(1)} collective-permute-done((f16[32,384]{1,0:T(8,128)(2,1)S(1)}, f16[32,384]{1,0:T(8,128)(2,1)S(1)}, u32[]{:S(2)}, u32[]{:S(2)}) %collective-permute-start.12) | collective-permute-done | bytes 24608 | tf_op jit(solution)/shard_map/ppermute | solution.py:101
  (44 shorter events, 7.7 us)
Async XLA Ops:
  0.6 97.1 %copy-start = (bf16[128,320]{0,1:T(8,128)(2,1)S(1)}, bf16[128,320]{0,1:T(8,128)(2,1)}, u32[]{:S(2)}) copy-start(bf16[128,320]{0,1:T(8,128)(2,1)} %param.8) | copy-start | bytes 245764
  0.6 18.7 %copy-start.1 = (f32[128,96]{0,1:T(8,128)S(1)}, f32[128,96]{0,1:T(8,128)}, u32[]{:S(2)}) copy-start(f32[128,96]{0,1:T(8,128)} %param.6) | copy-start | bytes 147460
  2.4 47.9 %all-to-all-start = ((f16[24,32,384]{2,1,0:T(8,128)(2,1)}), f16[24,32,384]{2,1,0:T(8,128)(2,1)S(1)}, u32[]{:S(2)}, u32[]{:S(2)}) async-start(f16[24,32,384]{2,1,0:T(8,128)(2,1)} %broadcast_in_dim.12), calls=%async_computation | async-start | bytes 1179648 | tf_op jit(solution)/shard_map/all_to_all | solution.py:22
  19.4 14.1 %collective-permute-start.2 = (f16[96,128]{1,0:T(8,128)(2,1)S(1)}, f16[96,128]{1,0:T(8,128)(2,1)S(1)}, u32[]{:S(2)}, u32[]{:S(2)}) collective-permute-start(f16[96,128]{1,0:T(8,128)(2,1)S(1)} %get-tuple-element.21), channel_id=1, source_target_pairs={{0,3},{1,0},{2,1},{3,2},{4,7},{5,4},{6,5},{7,6},{8,11},{9,8},{10,9... | collective-permute-start | bytes 73736 | tf_op jit(solution)/shard_map/ppermute | solution.py:35
  24.4 9.5 %collective-permute-start.1 = (f16[96,128]{1,0:T(8,128)(2,1)S(1)}, f16[96,128]{1,0:T(8,128)(2,1)S(1)}, u32[]{:S(2)}, u32[]{:S(2)}) collective-permute-start(f16[96,128]{1,0:T(8,128)(2,1)S(1)} %get-tuple-element.21), channel_id=1, source_target_pairs={{0,2},{1,3},{2,0},{3,1},{4,6},{5,7},{6,4},{7,5},{8,10},{9,11},{10,... | collective-permute-start | bytes 73736 | tf_op jit(solution)/shard_map/ppermute | solution.py:35
  28.8 7.1 %collective-permute-start = (f16[96,128]{1,0:T(8,128)(2,1)S(1)}, f16[96,128]{1,0:T(8,128)(2,1)S(1)}, u32[]{:S(2)}, u32[]{:S(2)}) collective-permute-start(f16[96,128]{1,0:T(8,128)(2,1)S(1)} %get-tuple-element.21), channel_id=1, source_target_pairs={{0,1},{1,2},{2,3},{3,0},{4,5},{5,6},{6,7},{7,4},{8,9},{9,10},{10,1... | collective-permute-start | bytes 73736 | tf_op jit(solution)/shard_map/ppermute | solution.py:35
  36.0 10.0 %collective-permute-start.4 = (f16[4,96,128]{2,1,0:T(8,128)(2,1)S(1)}, f16[4,96,128]{2,1,0:T(8,128)(2,1)S(1)}, u32[]{:S(2)}, u32[]{:S(2)}) collective-permute-start(f16[4,96,128]{2,1,0:T(8,128)(2,1)S(1)} %pad_maximum_fusion.3), channel_id=1, source_target_pairs={{0,8},{4,12},{8,0},{12,4},{1,9},{5,13},{9,1},{13,5},{2,10},{6,14},... | collective-permute-start | bytes 294920 | tf_op jit(solution)/shard_map/ppermute | solution.py:35
  40.6 6.0 %collective-permute-start.5 = (f16[4,96,128]{2,1,0:T(8,128)(2,1)S(1)}, f16[4,96,128]{2,1,0:T(8,128)(2,1)S(1)}, u32[]{:S(2)}, u32[]{:S(2)}) collective-permute-start(f16[4,96,128]{2,1,0:T(8,128)(2,1)S(1)} %pad_maximum_fusion.3), channel_id=1, source_target_pairs={{0,12},{4,0},{8,4},{12,8},{1,13},{5,1},{9,5},{13,9},{2,14},{6,2},{... | collective-permute-start | bytes 294920 | tf_op jit(solution)/shard_map/ppermute | solution.py:35
  43.4 6.6 %collective-permute-start.3 = (f16[4,96,128]{2,1,0:T(8,128)(2,1)S(1)}, f16[4,96,128]{2,1,0:T(8,128)(2,1)S(1)}, u32[]{:S(2)}, u32[]{:S(2)}) collective-permute-start(f16[4,96,128]{2,1,0:T(8,128)(2,1)S(1)} %pad_maximum_fusion.3), channel_id=1, source_target_pairs={{0,4},{4,8},{8,12},{12,0},{1,5},{5,9},{9,13},{13,1},{2,6},{6,10},{... | collective-permute-start | bytes 294920 | tf_op jit(solution)/shard_map/ppermute | solution.py:35
  50.4 7.5 %collective-permute-start.6 = (f16[24,32,384]{2,1,0:T(8,128)(2,1)S(1)}, f16[24,32,384]{2,1,0:T(8,128)(2,1)S(1)}, u32[]{:S(2)}, u32[]{:S(2)}) collective-permute-start(f16[24,32,384]{2,1,0:T(8,128)(2,1)S(1)} %all-to-all-done), channel_id=1, source_target_pairs={{0,16},{16,0},{1,17},{17,1},{2,18},{18,2},{3,19},{19,3},{4,20},{20... | collective-permute-start | bytes 1769480 | tf_op jit(solution)/shard_map/ppermute | solution.py:30
  56.4 1.4 copy-start.2
  60.7 18.0 %all-to-all-start.1 = ((f16[16,96,128]{2,1,0:T(8,128)(2,1)}), f16[16,96,128]{2,1,0:T(8,128)(2,1)S(1)}, u32[]{:S(2)}, u32[]{:S(2)}) async-start(f16[16,96,128]{2,1,0:T(8,128)(2,1)} %bitcast.33), calls=%async_computation.1 | async-start | bytes 786432 | tf_op jit(solution)/shard_map/all_to_all | solution.py:22
  80.1 17.6 %all-to-all-start.2 = ((bf16[16,96,128]{2,1,0:T(8,128)(2,1)}), bf16[16,96,128]{2,1,0:T(8,128)(2,1)S(1)}, u32[]{:S(2)}, u32[]{:S(2)}) async-start(bf16[16,96,128]{2,1,0:T(8,128)(2,1)} %broadcast_in_dim.25), calls=%async_computation.2 | async-start | bytes 786432 | tf_op jit(solution)/shard_map/all_to_all | solution.py:22
  85.0 17.6 %collective-permute-start.7 = (f16[768,384]{1,0:T(8,128)(2,1)S(1)}, f16[768,384]{1,0:T(8,128)(2,1)}, u32[]{:S(2)}, u32[]{:S(2)}) collective-permute-start(f16[768,384]{1,0:T(8,128)(2,1)S(1)} %fusion), channel_id=1, source_target_pairs={{0,16},{16,0},{1,17},{17,1},{2,18},{18,2},{3,19},{19,3},{4,20},{20... | collective-permute-start | bytes 1769480 | tf_op jit(solution)/shard_map/ppermute | solution.py:30
  98.0 11.8 %collective-permute-start.13 = (f16[24,32,320]{2,1,0:T(8,128)(2,1)S(1)}, f16[24,32,320]{2,1,0:T(8,128)(2,1)S(1)}, u32[]{:S(2)}, u32[]{:S(2)}) collective-permute-start(f16[24,32,320]{2,1,0:T(8,128)(2,1)S(1)} %fusion.1), channel_id=1, source_target_pairs={{0,16},{16,0},{1,17},{17,1},{2,18},{18,2},{3,19},{19,3},{4,20},{20... | collective-permute-start | bytes 1474568 | tf_op jit(solution)/shard_map/ppermute | solution.py:30
  104.5 15.9 %collective-permute-start.8 = (f16[3,2,2,32,384]{4,3,1,0,2:T(8,128)(2,1)S(1)}, f16[3,2,2,32,384]{4,3,1,0,2:T(8,128)(2,1)S(1)}, u32[]{:S(2)}, u32[]{:S(2)}) collective-permute-start(f16[3,2,2,32,384]{4,3,1,0,2:T(8,128)(2,1)S(1)} %fusion.13), channel_id=1, source_target_pairs={{0,384},{384,0},{1,385},{385,1},{2,386},{386,2},{3,387},{387,3},{4... | collective-permute-start | bytes 884744 | tf_op jit(solution)/shard_map/ppermute | solution.py:101
  111.0 55.3 %all-to-all-start.3 = ((f16[24,32,320]{2,1,0:T(8,128)(2,1)}), f16[24,32,320]{2,1,0:T(8,128)(2,1)S(1)}, u32[]{:S(2)}, u32[]{:S(2)}) async-start(f16[24,32,320]{2,1,0:T(8,128)(2,1)} %multiply_convert_fusion), calls=%async_computation.3 | async-start | bytes 1179648 | tf_op jit(solution)/shard_map/all_to_all | solution.py:22
  120.6 23.4 %collective-permute-start.9 = (f16[3,2,32,384]{3,2,1,0:T(8,128)(2,1)S(1)}, f16[3,2,32,384]{3,2,1,0:T(8,128)(2,1)S(1)}, u32[]{:S(2)}, u32[]{:S(2)}) collective-permute-start(f16[3,2,32,384]{3,2,1,0:T(8,128)(2,1)S(1)} %fusion.21), channel_id=1, source_target_pairs={{0,32},{32,0},{64,96},{96,64},{128,160},{160,128},{192,224},{224,1... | collective-permute-start | bytes 442376 | tf_op jit(solution)/shard_map/ppermute | solution.py:101
  144.0 9.2 %collective-permute-start.11 = (f16[2,32,384]{2,1,0:T(8,128)(2,1)S(1)}, f16[2,32,384]{2,1,0:T(8,128)(2,1)S(1)}, u32[]{:S(2)}, u32[]{:S(2)}) collective-permute-start(f16[2,32,384]{2,1,0:T(8,128)(2,1)S(1)} %get-tuple-element.17), channel_id=1, source_target_pairs={{0,256},{32,288},{64,320},{96,352},{128,0},{160,32},{192,64},{224,... | collective-permute-start | bytes 147464 | tf_op jit(solution)/shard_map/ppermute | solution.py:35
  151.0 8.8 %collective-permute-start.10 = (f16[2,32,384]{2,1,0:T(8,128)(2,1)S(1)}, f16[2,32,384]{2,1,0:T(8,128)(2,1)S(1)}, u32[]{:S(2)}, u32[]{:S(2)}) collective-permute-start(f16[2,32,384]{2,1,0:T(8,128)(2,1)S(1)} %get-tuple-element.16), channel_id=1, source_target_pairs={{0,128},{32,160},{64,192},{96,224},{128,256},{160,288},{192,320},{... | collective-permute-start | bytes 147464 | tf_op jit(solution)/shard_map/ppermute | solution.py:35
  159.9 5.7 %collective-permute-start.12 = (f16[32,384]{1,0:T(8,128)(2,1)S(1)}, f16[32,384]{1,0:T(8,128)(2,1)S(1)}, u32[]{:S(2)}, u32[]{:S(2)}) collective-permute-start(f16[32,384]{1,0:T(8,128)(2,1)S(1)} %fusion.29), channel_id=1, source_target_pairs={{0,64},{32,96},{64,0},{96,32},{128,192},{160,224},{192,128},{224,1... | collective-permute-start | bytes 73736 | tf_op jit(solution)/shard_map/ppermute | solution.py:101

commit v6 on v4

--- a/solution.py
+++ b/solution.py
@@ -121,12 +121,8 @@
     got = swap((weights(1 - core) * PROJ_UP[0]).astype(HALF))
     mine = weights(core)
     sent = ((mine + got.astype(F32) * (1.0 / PROJ_UP[0])) * PROJ_UP[1]).astype(HALF)
-    end = jnp.concatenate((sent[:, :16, 256:], sent[:, 16:, 256:]), axis=2)
-    sent = jnp.concatenate((sent[:, :, :128], sent[:, :, 128:256], end), axis=1)
     got = exchange(sent, CHIPS)
-    total = got.astype(F32).sum(axis=0) * (1.0 / PROJ_UP[1])
-    end = jnp.concatenate((total[64:, :64], total[64:, 64:]), axis=0)
-    grad_proj = jnp.concatenate((total[:32], total[32:64], end), axis=1)
+    grad_proj = got.astype(F32).sum(axis=0) * (1.0 / PROJ_UP[1])
     return (grad_image.T, grad_text.T, grad_proj.T)
 
 

time: 167 us -> 171 us (1.024)
  waiting for transfers between devices: 55.6 us -> 58.5 us
  matrix products: 4.54 us -> 6.44 us
    ppermute x3, waiting for transfers between devices: 20.4 us -> 23.5 us  [halve(): got = lax.ppermute((theirs * TEXT_UP[k]).astype(HALF), axis, pairs)]
  transfers between devices with their start and end apart: 18 -> 18, of which waited for: 10 -> 10; matrix products, arithmetic and copies ran while one was open for 3% -> 4% of each run, Pallas kernels for 0% -> 0%
where the time goes in v6:
time: 171 us; the launch traced here: 169 us
  starting transfers between devices  94.4 us (55%)
  waiting for transfers between devices  58.5 us (34%)
  matrix products  6.44 us (4%)
  other arithmetic  4.76 us (3%)
  between operations  2.5 us (1%)
  local copies, waits for them, and re-layouts  1.9 us (1%)
    all_to_all x4, starting transfers between devices, exchange(): return lax.all_to_all(tiles, axis, split_axis=0, concat_axis=0, tiled=True)  34.8 us
    ppermute x8, starting transfers between devices, shifted(): lax.ppermute(array, axis, tuple(((i, (i + step) % length) for i in range(...  33.2 us
    ppermute x3, waiting for transfers between devices, halve(): got = lax.ppermute((theirs * TEXT_UP[k]).astype(HALF), axis, pairs)  23.5 us
    all_to_all x4, waiting for transfers between devices, exchange(): return lax.all_to_all(tiles, axis, split_axis=0, concat_axis=0, tiled=True)  22.3 us
    ppermute x3, starting transfers between devices, swap(): return lax.ppermute(array, 'core', ((0, 1), (1, 0)))  14.6 us
    ppermute x8, waiting for transfers between devices, shifted(): lax.ppermute(array, axis, tuple(((i, (i + step) % length) for i in range(...  12.2 us
    ppermute x3, starting transfers between devices, halve(): got = lax.ppermute((theirs * TEXT_UP[k]).astype(HALF), axis, pairs)  11.8 us
    dot_general x6, matrix products, dot(): lax.dot_general(a, b, (((ca,), (cb,)), ((), ())), precision=HIGH, preferr...  4.93 us
  transfers between devices with their start and end apart: 18, of which 10 were waited for; matrix products, arithmetic and copies ran while one was open for 4% of the time, Pallas kernels for 0%

profile of v6, /device:TPU:1, one launch (start us, length us, event | category | flops | bytes accessed | tf_op | source)
XLA Modules:
  0.0 168.5 jit_solution(15819313845749133287)
XLA Ops:
  0.7 0.9 fusion.27
  1.5 0.9 broadcast_in_dim.12
  2.4 16.9 %all-to-all-start = ((f16[24,32,384]{2,1,0:T(8,128)(2,1)}), f16[24,32,384]{2,1,0:T(8,128)(2,1)S(1)}, u32[]{:S(2)}, u32[]{:S(2)}) async-start(f16[24,32,384]{2,1,0:T(8,128)(2,1)} %broadcast_in_dim.12), calls=%async_computation | async-start | bytes 1179648 | tf_op jit(solution)/shard_map/all_to_all | solution.py:22
  19.4 5.0 %collective-permute-start.2 = (f16[96,128]{1,0:T(8,128)(2,1)S(1)}, f16[96,128]{1,0:T(8,128)(2,1)S(1)}, u32[]{:S(2)}, u32[]{:S(2)}) collective-permute-start(f16[96,128]{1,0:T(8,128)(2,1)S(1)} %get-tuple-element.21), channel_id=1, source_target_pairs={{0,3},{1,0},{2,1},{3,2},{4,7},{5,4},{6,5},{7,6},{8,11},{9,8},{10,9... | collective-permute-start | bytes 73736 | tf_op jit(solution)/shard_map/ppermute | solution.py:35
  24.4 4.4 %collective-permute-start.1 = (f16[96,128]{1,0:T(8,128)(2,1)S(1)}, f16[96,128]{1,0:T(8,128)(2,1)S(1)}, u32[]{:S(2)}, u32[]{:S(2)}) collective-permute-start(f16[96,128]{1,0:T(8,128)(2,1)S(1)} %get-tuple-element.21), channel_id=1, source_target_pairs={{0,2},{1,3},{2,0},{3,1},{4,6},{5,7},{6,4},{7,5},{8,10},{9,11},{10,... | collective-permute-start | bytes 73736 | tf_op jit(solution)/shard_map/ppermute | solution.py:35
  28.8 3.3 %collective-permute-start = (f16[96,128]{1,0:T(8,128)(2,1)S(1)}, f16[96,128]{1,0:T(8,128)(2,1)S(1)}, u32[]{:S(2)}, u32[]{:S(2)}) collective-permute-start(f16[96,128]{1,0:T(8,128)(2,1)S(1)} %get-tuple-element.21), channel_id=1, source_target_pairs={{0,1},{1,2},{2,3},{3,0},{4,5},{5,6},{6,7},{7,4},{8,9},{9,10},{10,1... | collective-permute-start | bytes 73736 | tf_op jit(solution)/shard_map/ppermute | solution.py:35
  33.9 2.1 %collective-permute-done = f16[96,128]{1,0:T(8,128)(2,1)S(1)} collective-permute-done((f16[96,128]{1,0:T(8,128)(2,1)S(1)}, f16[96,128]{1,0:T(8,128)(2,1)S(1)}, u32[]{:S(2)}, u32[]{:S(2)}) %collective-permute-start) | collective-permute-done | bytes 24608 | tf_op jit(solution)/shard_map/ppermute | solution.py:35
  36.0 4.7 %collective-permute-start.4 = (f16[4,96,128]{2,1,0:T(8,128)(2,1)S(1)}, f16[4,96,128]{2,1,0:T(8,128)(2,1)S(1)}, u32[]{:S(2)}, u32[]{:S(2)}) collective-permute-start(f16[4,96,128]{2,1,0:T(8,128)(2,1)S(1)} %pad_maximum_fusion.3), channel_id=1, source_target_pairs={{0,8},{4,12},{8,0},{12,4},{1,9},{5,13},{9,1},{13,5},{2,10},{6,14},... | collective-permute-start | bytes 294920 | tf_op jit(solution)/shard_map/ppermute | solution.py:35
  40.6 2.8 %collective-permute-start.5 = (f16[4,96,128]{2,1,0:T(8,128)(2,1)S(1)}, f16[4,96,128]{2,1,0:T(8,128)(2,1)S(1)}, u32[]{:S(2)}, u32[]{:S(2)}) collective-permute-start(f16[4,96,128]{2,1,0:T(8,128)(2,1)S(1)} %pad_maximum_fusion.3), channel_id=1, source_target_pairs={{0,12},{4,0},{8,4},{12,8},{1,13},{5,1},{9,5},{13,9},{2,14},{6,2},{... | collective-permute-start | bytes 294920 | tf_op jit(solution)/shard_map/ppermute | solution.py:35
  43.4 2.5 %collective-permute-start.3 = (f16[4,96,128]{2,1,0:T(8,128)(2,1)S(1)}, f16[4,96,128]{2,1,0:T(8,128)(2,1)S(1)}, u32[]{:S(2)}, u32[]{:S(2)}) collective-permute-start(f16[4,96,128]{2,1,0:T(8,128)(2,1)S(1)} %pad_maximum_fusion.3), channel_id=1, source_target_pairs={{0,4},{4,8},{8,12},{12,0},{1,5},{5,9},{9,13},{13,1},{2,6},{6,10},{... | collective-permute-start | bytes 294920 | tf_op jit(solution)/shard_map/ppermute | solution.py:35
  45.9 0.7 collective-permute-done.5
  46.7 3.3 %collective-permute-done.3 = f16[4,96,128]{2,1,0:T(8,128)(2,1)S(1)} collective-permute-done((f16[4,96,128]{2,1,0:T(8,128)(2,1)S(1)}, f16[4,96,128]{2,1,0:T(8,128)(2,1)S(1)}, u32[]{:S(2)}, u32[]{:S(2)}) %collective-permute-start.3) | collective-permute-done | bytes 98336 | tf_op jit(solution)/shard_map/ppermute | solution.py:35
  50.4 5.9 %collective-permute-start.6 = (f16[24,32,384]{2,1,0:T(8,128)(2,1)S(1)}, f16[24,32,384]{2,1,0:T(8,128)(2,1)S(1)}, u32[]{:S(2)}, u32[]{:S(2)}) collective-permute-start(f16[24,32,384]{2,1,0:T(8,128)(2,1)S(1)} %all-to-all-done), channel_id=1, source_target_pairs={{0,16},{16,0},{1,17},{17,1},{2,18},{18,2},{3,19},{19,3},{4,20},{20... | collective-permute-start | bytes 1769480 | tf_op jit(solution)/shard_map/ppermute | solution.py:30
  59.8 0.9 pad_maximum_fusion.2
  60.7 4.3 %all-to-all-start.1 = ((f16[16,96,128]{2,1,0:T(8,128)(2,1)}), f16[16,96,128]{2,1,0:T(8,128)(2,1)S(1)}, u32[]{:S(2)}, u32[]{:S(2)}) async-start(f16[16,96,128]{2,1,0:T(8,128)(2,1)} %bitcast.33), calls=%async_computation.1 | async-start | bytes 786432 | tf_op jit(solution)/shard_map/all_to_all | solution.py:22
  65.0 13.7 %all-to-all-done.1 = f16[16,96,128]{2,1,0:T(8,128)(2,1)S(1)} async-done(((f16[16,96,128]{2,1,0:T(8,128)(2,1)}), f16[16,96,128]{2,1,0:T(8,128)(2,1)S(1)}, u32[]{:S(2)}, u32[]{:S(2)}) %all-to-all-start.1) | async-done | bytes 393248 | tf_op jit(solution)/shard_map/all_to_all | solution.py:22
  79.3 0.8 broadcast_in_dim.25
  80.1 4.2 %all-to-all-start.2 = ((bf16[16,96,128]{2,1,0:T(8,128)(2,1)}), bf16[16,96,128]{2,1,0:T(8,128)(2,1)S(1)}, u32[]{:S(2)}, u32[]{:S(2)}) async-start(bf16[16,96,128]{2,1,0:T(8,128)(2,1)} %broadcast_in_dim.25), calls=%async_computation.2 | async-start | bytes 786432 | tf_op jit(solution)/shard_map/all_to_all | solution.py:22
  85.0 4.2 %collective-permute-start.7 = (f16[768,384]{1,0:T(8,128)(2,1)S(1)}, f16[768,384]{1,0:T(8,128)(2,1)}, u32[]{:S(2)}, u32[]{:S(2)}) collective-permute-start(f16[768,384]{1,0:T(8,128)(2,1)S(1)} %fusion), channel_id=1, source_target_pairs={{0,16},{16,0},{1,17},{17,1},{2,18},{18,2},{3,19},{19,3},{4,20},{20... | collective-permute-start | bytes 1769480 | tf_op jit(solution)/shard_map/ppermute | solution.py:30
  89.2 8.6 %all-to-all-done.2 = bf16[16,96,128]{2,1,0:T(8,128)(2,1)S(1)} async-done(((bf16[16,96,128]{2,1,0:T(8,128)(2,1)}), bf16[16,96,128]{2,1,0:T(8,128)(2,1)S(1)}, u32[]{:S(2)}, u32[]{:S(2)}) %all-to-all-start.2) | async-done | bytes 393248 | tf_op jit(solution)/shard_map/all_to_all | solution.py:22
  98.0 4.5 %collective-permute-start.13 = (f16[24,32,320]{2,1,0:T(8,128)(2,1)S(1)}, f16[24,32,320]{2,1,0:T(8,128)(2,1)S(1)}, u32[]{:S(2)}, u32[]{:S(2)}) collective-permute-start(f16[24,32,320]{2,1,0:T(8,128)(2,1)S(1)} %fusion.1), channel_id=1, source_target_pairs={{0,16},{16,0},{1,17},{17,1},{2,18},{18,2},{3,19},{19,3},{4,20},{20... | collective-permute-start | bytes 1474568 | tf_op jit(solution)/shard_map/ppermute | solution.py:30
  102.6 1.7 %multiply_add_fusion = f32[768,384]{1,0:T(8,128)S(1)} fusion(f16[768,384]{1,0:T(8,128)(2,1)} %collective-permute-done.7, f16[768,128]{1,0:T(8,128)(2,1)S(1)} %bitcast.117, f32[128,384]{1,0:T(8,128)S(1)} %fusion.11), kind=kOutput, calls=%fused_computation.9 | convolution fusion | flops 227672064 | bytes 2162688 | tf_op jit(solution)/shard_map/dot_general | solution.py:55
  104.5 5.3 %collective-permute-start.8 = (f16[3,2,2,32,384]{4,3,0,1,2:T(8,128)(2,1)S(1)}, f16[3,2,2,32,384]{4,3,0,1,2:T(8,128)(2,1)S(1)}, u32[]{:S(2)}, u32[]{:S(2)}) collective-permute-start(f16[3,2,2,32,384]{4,3,0,1,2:T(8,128)(2,1)S(1)} %fusion.13), channel_id=1, source_target_pairs={{0,384},{384,0},{1,385},{385,1},{2,386},{386,2},{3,387},{387,3},{4... | collective-permute-start | bytes 884744 | tf_op jit(solution)/shard_map/ppermute | solution.py:101
  109.8 1.2 multiply_convert_fusion
  111.0 9.4 %all-to-all-start.3 = ((f16[24,32,320]{2,1,0:T(8,128)(2,1)}), f16[24,32,320]{2,1,0:T(8,128)(2,1)S(1)}, u32[]{:S(2)}, u32[]{:S(2)}) async-start(f16[24,32,320]{2,1,0:T(8,128)(2,1)} %multiply_convert_fusion), calls=%async_computation.3 | async-start | bytes 1179648 | tf_op jit(solution)/shard_map/all_to_all | solution.py:22
  120.6 3.2 %collective-permute-start.9 = (f16[3,2,32,384]{3,2,0,1:T(8,128)(2,1)S(1)}, f16[3,2,32,384]{3,2,0,1:T(8,128)(2,1)S(1)}, u32[]{:S(2)}, u32[]{:S(2)}) collective-permute-start(f16[3,2,32,384]{3,2,0,1:T(8,128)(2,1)S(1)} %fusion.21), channel_id=1, source_target_pairs={{0,32},{32,0},{64,96},{96,64},{128,160},{160,128},{192,224},{224,1... | collective-permute-start | bytes 442376 | tf_op jit(solution)/shard_map/ppermute | solution.py:101
  123.8 20.2 %collective-permute-done.9 = f16[3,2,32,384]{3,2,0,1:T(8,128)(2,1)S(1)} collective-permute-done((f16[3,2,32,384]{3,2,0,1:T(8,128)(2,1)S(1)}, f16[3,2,32,384]{3,2,0,1:T(8,128)(2,1)S(1)}, u32[]{:S(2)}, u32[]{:S(2)}) %collective-permute-start.9) | collective-permute-done | bytes 147488 | tf_op jit(solution)/shard_map/ppermute | solution.py:101
  144.0 3.3 %collective-permute-start.10 = (f16[3,32,384]{2,1,0:T(8,128)(2,1)S(1)}, f16[3,32,384]{2,1,0:T(8,128)(2,1)S(1)}, u32[]{:S(2)}, u32[]{:S(2)}) collective-permute-start(f16[3,32,384]{2,1,0:T(8,128)(2,1)S(1)} %fusion.24), channel_id=1, source_target_pairs={{0,64},{32,96},{64,0},{96,32},{128,192},{160,224},{192,128},{224,1... | collective-permute-start | bytes 221192 | tf_op jit(solution)/shard_map/ppermute | solution.py:101
  147.5 3.4 %collective-permute-done.10 = f16[3,32,384]{2,1,0:T(8,128)(2,1)S(1)} collective-permute-done((f16[3,32,384]{2,1,0:T(8,128)(2,1)S(1)}, f16[3,32,384]{2,1,0:T(8,128)(2,1)S(1)}, u32[]{:S(2)}, u32[]{:S(2)}) %collective-permute-start.10) | collective-permute-done | bytes 73760 | tf_op jit(solution)/shard_map/ppermute | solution.py:101
  150.9 7.8 %collective-permute-start.12 = (f16[32,384]{1,0:T(8,128)(2,1)S(1)}, f16[32,384]{1,0:T(8,128)(2,1)S(1)}, u32[]{:S(2)}, u32[]{:S(2)}) collective-permute-start(f16[32,384]{1,0:T(8,128)(2,1)S(1)} %get-tuple-element.17), channel_id=1, source_target_pairs={{0,256},{32,288},{64,320},{96,352},{128,0},{160,32},{192,64},{224,... | collective-permute-start | bytes 73736 | tf_op jit(solution)/shard_map/ppermute | solution.py:35
  158.7 2.8 %collective-permute-start.11 = (f16[32,384]{1,0:T(8,128)(2,1)S(1)}, f16[32,384]{1,0:T(8,128)(2,1)S(1)}, u32[]{:S(2)}, u32[]{:S(2)}) collective-permute-start(f16[32,384]{1,0:T(8,128)(2,1)S(1)} %get-tuple-element.16), channel_id=1, source_target_pairs={{0,128},{32,160},{64,192},{96,224},{128,256},{160,288},{192,320},{... | collective-permute-start | bytes 73736 | tf_op jit(solution)/shard_map/ppermute | solution.py:35
  161.5 5.7 %collective-permute-done.11 = f16[32,384]{1,0:T(8,128)(2,1)S(1)} collective-permute-done((f16[32,384]{1,0:T(8,128)(2,1)S(1)}, f16[32,384]{1,0:T(8,128)(2,1)S(1)}, u32[]{:S(2)}, u32[]{:S(2)}) %collective-permute-start.11) | collective-permute-done | bytes 24608 | tf_op jit(solution)/shard_map/ppermute | solution.py:35
  (44 shorter events, 7.7 us)
Async XLA Ops:
  0.6 97.1 %copy-start = (bf16[128,320]{0,1:T(8,128)(2,1)S(1)}, bf16[128,320]{0,1:T(8,128)(2,1)}, u32[]{:S(2)}) copy-start(bf16[128,320]{0,1:T(8,128)(2,1)} %param.8) | copy-start | bytes 245764
  0.6 18.7 %copy-start.1 = (f32[128,96]{0,1:T(8,128)S(1)}, f32[128,96]{0,1:T(8,128)}, u32[]{:S(2)}) copy-start(f32[128,96]{0,1:T(8,128)} %param.6) | copy-start | bytes 147460
  2.4 47.9 %all-to-all-start = ((f16[24,32,384]{2,1,0:T(8,128)(2,1)}), f16[24,32,384]{2,1,0:T(8,128)(2,1)S(1)}, u32[]{:S(2)}, u32[]{:S(2)}) async-start(f16[24,32,384]{2,1,0:T(8,128)(2,1)} %broadcast_in_dim.12), calls=%async_computation | async-start | bytes 1179648 | tf_op jit(solution)/shard_map/all_to_all | solution.py:22
  19.4 14.1 %collective-permute-start.2 = (f16[96,128]{1,0:T(8,128)(2,1)S(1)}, f16[96,128]{1,0:T(8,128)(2,1)S(1)}, u32[]{:S(2)}, u32[]{:S(2)}) collective-permute-start(f16[96,128]{1,0:T(8,128)(2,1)S(1)} %get-tuple-element.21), channel_id=1, source_target_pairs={{0,3},{1,0},{2,1},{3,2},{4,7},{5,4},{6,5},{7,6},{8,11},{9,8},{10,9... | collective-permute-start | bytes 73736 | tf_op jit(solution)/shard_map/ppermute | solution.py:35
  24.4 9.5 %collective-permute-start.1 = (f16[96,128]{1,0:T(8,128)(2,1)S(1)}, f16[96,128]{1,0:T(8,128)(2,1)S(1)}, u32[]{:S(2)}, u32[]{:S(2)}) collective-permute-start(f16[96,128]{1,0:T(8,128)(2,1)S(1)} %get-tuple-element.21), channel_id=1, source_target_pairs={{0,2},{1,3},{2,0},{3,1},{4,6},{5,7},{6,4},{7,5},{8,10},{9,11},{10,... | collective-permute-start | bytes 73736 | tf_op jit(solution)/shard_map/ppermute | solution.py:35
  28.8 7.1 %collective-permute-start = (f16[96,128]{1,0:T(8,128)(2,1)S(1)}, f16[96,128]{1,0:T(8,128)(2,1)S(1)}, u32[]{:S(2)}, u32[]{:S(2)}) collective-permute-start(f16[96,128]{1,0:T(8,128)(2,1)S(1)} %get-tuple-element.21), channel_id=1, source_target_pairs={{0,1},{1,2},{2,3},{3,0},{4,5},{5,6},{6,7},{7,4},{8,9},{9,10},{10,1... | collective-permute-start | bytes 73736 | tf_op jit(solution)/shard_map/ppermute | solution.py:35
  36.0 10.0 %collective-permute-start.4 = (f16[4,96,128]{2,1,0:T(8,128)(2,1)S(1)}, f16[4,96,128]{2,1,0:T(8,128)(2,1)S(1)}, u32[]{:S(2)}, u32[]{:S(2)}) collective-permute-start(f16[4,96,128]{2,1,0:T(8,128)(2,1)S(1)} %pad_maximum_fusion.3), channel_id=1, source_target_pairs={{0,8},{4,12},{8,0},{12,4},{1,9},{5,13},{9,1},{13,5},{2,10},{6,14},... | collective-permute-start | bytes 294920 | tf_op jit(solution)/shard_map/ppermute | solution.py:35
  40.6 6.0 %collective-permute-start.5 = (f16[4,96,128]{2,1,0:T(8,128)(2,1)S(1)}, f16[4,96,128]{2,1,0:T(8,128)(2,1)S(1)}, u32[]{:S(2)}, u32[]{:S(2)}) collective-permute-start(f16[4,96,128]{2,1,0:T(8,128)(2,1)S(1)} %pad_maximum_fusion.3), channel_id=1, source_target_pairs={{0,12},{4,0},{8,4},{12,8},{1,13},{5,1},{9,5},{13,9},{2,14},{6,2},{... | collective-permute-start | bytes 294920 | tf_op jit(solution)/shard_map/ppermute | solution.py:35
  43.4 6.6 %collective-permute-start.3 = (f16[4,96,128]{2,1,0:T(8,128)(2,1)S(1)}, f16[4,96,128]{2,1,0:T(8,128)(2,1)S(1)}, u32[]{:S(2)}, u32[]{:S(2)}) collective-permute-start(f16[4,96,128]{2,1,0:T(8,128)(2,1)S(1)} %pad_maximum_fusion.3), channel_id=1, source_target_pairs={{0,4},{4,8},{8,12},{12,0},{1,5},{5,9},{9,13},{13,1},{2,6},{6,10},{... | collective-permute-start | bytes 294920 | tf_op jit(solution)/shard_map/ppermute | solution.py:35
  50.4 7.5 %collective-permute-start.6 = (f16[24,32,384]{2,1,0:T(8,128)(2,1)S(1)}, f16[24,32,384]{2,1,0:T(8,128)(2,1)S(1)}, u32[]{:S(2)}, u32[]{:S(2)}) collective-permute-start(f16[24,32,384]{2,1,0:T(8,128)(2,1)S(1)} %all-to-all-done), channel_id=1, source_target_pairs={{0,16},{16,0},{1,17},{17,1},{2,18},{18,2},{3,19},{19,3},{4,20},{20... | collective-permute-start | bytes 1769480 | tf_op jit(solution)/shard_map/ppermute | solution.py:30
  56.4 1.4 copy-start.2
  60.7 18.0 %all-to-all-start.1 = ((f16[16,96,128]{2,1,0:T(8,128)(2,1)}), f16[16,96,128]{2,1,0:T(8,128)(2,1)S(1)}, u32[]{:S(2)}, u32[]{:S(2)}) async-start(f16[16,96,128]{2,1,0:T(8,128)(2,1)} %bitcast.33), calls=%async_computation.1 | async-start | bytes 786432 | tf_op jit(solution)/shard_map/all_to_all | solution.py:22
  80.1 17.6 %all-to-all-start.2 = ((bf16[16,96,128]{2,1,0:T(8,128)(2,1)}), bf16[16,96,128]{2,1,0:T(8,128)(2,1)S(1)}, u32[]{:S(2)}, u32[]{:S(2)}) async-start(bf16[16,96,128]{2,1,0:T(8,128)(2,1)} %broadcast_in_dim.25), calls=%async_computation.2 | async-start | bytes 786432 | tf_op jit(solution)/shard_map/all_to_all | solution.py:22
  85.0 17.6 %collective-permute-start.7 = (f16[768,384]{1,0:T(8,128)(2,1)S(1)}, f16[768,384]{1,0:T(8,128)(2,1)}, u32[]{:S(2)}, u32[]{:S(2)}) collective-permute-start(f16[768,384]{1,0:T(8,128)(2,1)S(1)} %fusion), channel_id=1, source_target_pairs={{0,16},{16,0},{1,17},{17,1},{2,18},{18,2},{3,19},{19,3},{4,20},{20... | collective-permute-start | bytes 1769480 | tf_op jit(solution)/shard_map/ppermute | solution.py:30
  98.0 11.8 %collective-permute-start.13 = (f16[24,32,320]{2,1,0:T(8,128)(2,1)S(1)}, f16[24,32,320]{2,1,0:T(8,128)(2,1)S(1)}, u32[]{:S(2)}, u32[]{:S(2)}) collective-permute-start(f16[24,32,320]{2,1,0:T(8,128)(2,1)S(1)} %fusion.1), channel_id=1, source_target_pairs={{0,16},{16,0},{1,17},{17,1},{2,18},{18,2},{3,19},{19,3},{4,20},{20... | collective-permute-start | bytes 1474568 | tf_op jit(solution)/shard_map/ppermute | solution.py:30
  104.5 15.9 %collective-permute-start.8 = (f16[3,2,2,32,384]{4,3,0,1,2:T(8,128)(2,1)S(1)}, f16[3,2,2,32,384]{4,3,0,1,2:T(8,128)(2,1)S(1)}, u32[]{:S(2)}, u32[]{:S(2)}) collective-permute-start(f16[3,2,2,32,384]{4,3,0,1,2:T(8,128)(2,1)S(1)} %fusion.13), channel_id=1, source_target_pairs={{0,384},{384,0},{1,385},{385,1},{2,386},{386,2},{3,387},{387,3},{4... | collective-permute-start | bytes 884744 | tf_op jit(solution)/shard_map/ppermute | solution.py:101
  111.0 56.8 %all-to-all-start.3 = ((f16[24,32,320]{2,1,0:T(8,128)(2,1)}), f16[24,32,320]{2,1,0:T(8,128)(2,1)S(1)}, u32[]{:S(2)}, u32[]{:S(2)}) async-start(f16[24,32,320]{2,1,0:T(8,128)(2,1)} %multiply_convert_fusion), calls=%async_computation.3 | async-start | bytes 1179648 | tf_op jit(solution)/shard_map/all_to_all | solution.py:22
  120.6 23.4 %collective-permute-start.9 = (f16[3,2,32,384]{3,2,0,1:T(8,128)(2,1)S(1)}, f16[3,2,32,384]{3,2,0,1:T(8,128)(2,1)S(1)}, u32[]{:S(2)}, u32[]{:S(2)}) collective-permute-start(f16[3,2,32,384]{3,2,0,1:T(8,128)(2,1)S(1)} %fusion.21), channel_id=1, source_target_pairs={{0,32},{32,0},{64,96},{96,64},{128,160},{160,128},{192,224},{224,1... | collective-permute-start | bytes 442376 | tf_op jit(solution)/shard_map/ppermute | solution.py:101
  144.0 6.8 %collective-permute-start.10 = (f16[3,32,384]{2,1,0:T(8,128)(2,1)S(1)}, f16[3,32,384]{2,1,0:T(8,128)(2,1)S(1)}, u32[]{:S(2)}, u32[]{:S(2)}) collective-permute-start(f16[3,32,384]{2,1,0:T(8,128)(2,1)S(1)} %fusion.24), channel_id=1, source_target_pairs={{0,64},{32,96},{64,0},{96,32},{128,192},{160,224},{192,128},{224,1... | collective-permute-start | bytes 221192 | tf_op jit(solution)/shard_map/ppermute | solution.py:101
  150.9 10.6 %collective-permute-start.12 = (f16[32,384]{1,0:T(8,128)(2,1)S(1)}, f16[32,384]{1,0:T(8,128)(2,1)S(1)}, u32[]{:S(2)}, u32[]{:S(2)}) collective-permute-start(f16[32,384]{1,0:T(8,128)(2,1)S(1)} %get-tuple-element.17), channel_id=1, source_target_pairs={{0,256},{32,288},{64,320},{96,352},{128,0},{160,32},{192,64},{224,... | collective-permute-start | bytes 73736 | tf_op jit(solution)/shard_map/ppermute | solution.py:35
  158.7 8.5 %collective-permute-start.11 = (f16[32,384]{1,0:T(8,128)(2,1)S(1)}, f16[32,384]{1,0:T(8,128)(2,1)S(1)}, u32[]{:S(2)}, u32[]{:S(2)}) collective-permute-start(f16[32,384]{1,0:T(8,128)(2,1)S(1)} %get-tuple-element.16), channel_id=1, source_target_pairs={{0,128},{32,160},{64,192},{96,224},{128,256},{160,288},{192,320},{... | collective-permute-start | bytes 73736 | tf_op jit(solution)/shard_map/ppermute | solution.py:35
